TPU v7x, 32 devices: a whole 2x2x4 slice. The times are simulated.
32 devices in a mesh: groups: 2 (over y), seq: 4 (over z), tensor: 2 (over x), pipe: 2 (over core).
Axes of the slice: x: 2, y: 2, z: 4, core: 2. Of those that a mesh axis runs over, the one named last changes fastest.
Arguments:
- layer_input: bfloat16 [3072, 8192], P(('groups', 'seq'), ('tensor', 'pipe')), parts along dimension 0, may hold values from -6 to 6
- out_grad: bfloat16 [3072, 1024], P(('groups', 'seq')), parts along dimension 0, may hold values from -6 to 6
- value_weight: bfloat16 [1024, 8192], P('seq', ('tensor', 'pipe')), may hold values from -0.1875 to 0.1875
- adapter_down: bfloat16 [4, 64, 8192], P('seq', None, ('tensor', 'pipe')), may hold values from -0.0625 to 0.0625
- adapter_up: bfloat16 [4, 64, 1024], P('seq', None, ('tensor', 'pipe')), may hold values from -0.1875 to 0.1875
- block_tenant: int32 [24, 1], P(('groups', 'seq')), parts along dimension 0, may hold values from 0 to 3
- tenant_slot: int32 [4], replicated, may hold values from 0 to 3, each once
- forget_flag: int32 [3072], P(('groups', 'seq')), parts along dimension 0, may hold values 0 or 1
Outputs:
- layer_input_gradient: bfloat16 [3072, 8192], P(('groups', 'seq'), ('tensor', 'pipe')), parts along dimension 0
- down_grad: float32 [8, 64, 8192], P(('groups', 'seq'), None, ('tensor', 'pipe')), parts along dimension 0
- up_grad: float32 [8, 64, 1024], P(('groups', 'seq'), None, ('tensor', 'pipe')), parts along dimension 0
There are 2 independent parts, one for each index of `groups`. A program takes and returns all parts, laid end to end along the dimension named above; an argument that names none is the same for every part. Nothing has to cross between parts.
Inputs may be any that keep to these rules, and one draw needn't show every extreme that they name: `block_tenant`: every tenant owns at least one block of 128 rows. A permutation: tenant t's adapter is row tenant_slot[t] of adapter_down and adapter_up.
All inputs are finite; a program needn't handle non-finite values. No bound on the sum of `forget_flag` on one device may be relied on, other than what follows from the above.
Results may differ from a plain program's by a relative error of at most 0.014.
Values may be sent and summed in bfloat16 or wider, within the bound.
No kernel may reach another device: no remote copies, remote signals or barrier semaphores. Data moves between devices by JAX's collectives and lax.ppermute only.
A program may use at most 64 MiB of HBM per device.

v0:
```python
import jax
import jax.numpy as jnp
from jax import lax
from jax.sharding import PartitionSpec as P

adapter_scale_factor = 2.0


def per_device(
    layer_input,
    out_grad,
    value_weight,
    adapter_down,
    adapter_up,
    block_tenant,
    tenant_slot,
    forget_flag,
):
    token_rows, feature_width = layer_input.shape
    owned_count = adapter_down.shape[0]
    adapter_rank_width = adapter_down.shape[1]
    col_slab = adapter_up.shape[2]
    tenants = tenant_slot.shape[0]
    block_count = block_tenant.shape[0]
    block_rows = token_rows // block_count
    highest_precision = lax.Precision.HIGHEST
    row_sign = (1 - 2 * forget_flag).astype(jnp.bfloat16)
    weighted = out_grad * row_sign[:, None]
    frozen_input_gradient = jnp.dot(
        weighted,
        lax.all_gather(value_weight, "seq", axis=0, tiled=True),
        preferred_element_type=jnp.float32,
    )
    tenant_ids = jnp.arange(tenants, dtype=jnp.int32)
    block_slot = jnp.sum(
        jnp.where(block_tenant == tenant_ids[None, :], tenant_slot[None, :], 0), axis=1
    )
    down_piece = lax.all_gather(adapter_down, "seq", axis=0, tiled=True)
    up_piece = lax.all_gather(adapter_up, "seq", axis=0, tiled=True)
    offsets = jnp.arange(down_piece.shape[0], dtype=jnp.int32)
    matches = (block_slot[:, None] == offsets[None, :]).astype(jnp.bfloat16)
    down_part = jnp.einsum("bj,jrd->brd", matches, down_piece, preferred_element_type=jnp.float32)
    up_part = jnp.einsum("bj,jrv->brv", matches, up_piece, preferred_element_type=jnp.float32)
    selected_down_weight = down_part.astype(jnp.bfloat16)
    selected_up_weight = up_part.astype(jnp.bfloat16)
    blocks_in = layer_input.reshape(block_count, block_rows, feature_width)
    slab_index = lax.axis_index(("tensor", "pipe"))
    own_cols = lax.dynamic_slice_in_dim(weighted, slab_index * col_slab, col_slab, 1)
    blocks_grad = own_cols.reshape(block_count, block_rows, col_slab)
    hidden_part = jnp.einsum(
        "bnd,brd->bnr", blocks_in, selected_down_weight, preferred_element_type=jnp.float32
    )
    low_part = jnp.einsum(
        "dck,dyk->dcy", blocks_grad, selected_up_weight, preferred_element_type=jnp.float32
    )
    joined = jnp.concatenate((hidden_part, low_part), axis=2)
    gradient_total = lax.psum(joined.astype(jnp.bfloat16), ("tensor", "pipe")).astype(jnp.float32)
    hidden_batch_rows = gradient_total[:, :, :adapter_rank_width].astype(jnp.bfloat16)
    rank_projection_batch = (
        adapter_scale_factor * gradient_total[:, :, adapter_rank_width:]
    ).astype(jnp.bfloat16)
    adapter_input_gradient = jnp.einsum(
        "tqi,tie->tqe",
        rank_projection_batch,
        selected_down_weight,
        preferred_element_type=jnp.float32,
    )
    layer_input_gradient = (
        frozen_input_gradient + adapter_input_gradient.reshape(token_rows, feature_width)
    ).astype(jnp.bfloat16)
    part_down = jnp.einsum(
        "bnd,bnr->brd", blocks_in, rank_projection_batch, preferred_element_type=jnp.float32
    )
    partial_up_weight = adapter_scale_factor * jnp.einsum(
        "yxj,yxl->yjl", hidden_batch_rows, blocks_grad, preferred_element_type=jnp.float32
    )
    select = (block_slot[:, None] == tenant_ids[None, :]).astype(jnp.float32)
    table_up = jnp.einsum(
        "bs,brv->srv", select, partial_up_weight, precision=highest_precision
    ).astype(jnp.bfloat16)
    table_down = jnp.einsum("bs,brd->srd", select, part_down, precision=highest_precision).astype(
        jnp.bfloat16
    )
    got_down, got_up = (
        lax.all_to_all(table_down, "seq", split_axis=0, concat_axis=0, tiled=True),
        lax.all_to_all(table_up, "seq", split_axis=0, concat_axis=0, tiled=True),
    )
    down_grad = jnp.sum(
        got_down.astype(jnp.float32).reshape(-1, owned_count, adapter_rank_width, feature_width),
        axis=0,
    )
    up_grad = jnp.sum(
        got_up.astype(jnp.float32).reshape(-1, owned_count, adapter_rank_width, col_slab), axis=0
    )
    return (layer_input_gradient, down_grad, up_grad)


def solution(mesh):
    return jax.shard_map(
        per_device,
        mesh=mesh,
        in_specs=(
            P(("groups", "seq"), ("tensor", "pipe")),
            P(("groups", "seq"), None),
            P("seq", ("tensor", "pipe")),
            P("seq", None, ("tensor", "pipe")),
            P("seq", None, ("tensor", "pipe")),
            P(("groups", "seq"), None),
            P(),
            P(("groups", "seq")),
        ),
        out_specs=(
            P(("groups", "seq"), ("tensor", "pipe")),
            P(("groups", "seq"), None, ("tensor", "pipe")),
            P(("groups", "seq"), None, ("tensor", "pipe")),
        ),
        check_vma=False,
    )
```

profile of v0, /device:TPU:0, one launch (start us, length us, event | category | flops | bytes accessed | tf_op | source)
XLA Modules:
  0.0 194.0 jit_solution(7989112820145501983)
XLA Ops:
  7.2 0.0 copy-start
  7.2 0.0 all-gather.5.cloned.1.call-start
  7.2 0.7 all-gather.5.cloned.1.call-update
  7.9 0.0 all-reduce.2.cloned.1.call-start
  8.0 15.3 %all_gather.11 = bf16[4,64,256]{2,1,0:T(8,128)(2,1)S(1)} all-gather(bf16[1,64,256]{2,1,0:T(8,128)(2,1)} %param.12), channel_id=1, replica_groups=mesh['groups'=2,'seq'=4,'tensor'=2,'pipe'=2] {'seq'}, dimensions={0}, use_global_device_ids=true | all-gather | bytes 163840 | tf_op jit(solution)/shard_map/all_gather | solution.py:39
  23.2 0.9 select_reduce_fusion
  24.1 0.7 subtract_convert_fusion
  24.8 1.2 broadcast_multiply_fusion
  26.1 0.3 convolution_convert_fusion.2
  26.4 0.2 convolution_convert_fusion.3
  26.6 13.8 %all-gather.5.cloned.1.call-done = bf16[4,64,2048]{2,1,0:T(8,128)(2,1)} async-done(((bf16[1,64,2048]{2,1,0:T(8,128)(2,1)}), bf16[4,64,2048]{2,1,0:T(8,128)(2,1)}) %all-gather.5.cloned.1.call-update) | async-done | bytes 1048592 | tf_op jit(solution)/shard_map/all_gather | solution.py:38
  40.3 2.3 %fusion.3 = bf16[3,64,2048]{2,0,1:T(4,128)(2,1)S(1)} fusion(bf16[4,64,2048]{2,1,0:T(8,128)(2,1)} %all-gather.5.cloned.1.call-done, s32[3]{0:T(128)S(1)} %select_reduce_fusion), kind=kOutput, calls=%fused_computation.12 | convolution fusion | flops 3145740 | bytes 1835020 | tf_op jit(solution)/shard_map/bj,jrd->brd/dot_general | solution.py:42
  42.7 0.0 copy-done
  42.7 0.0 copy-start.1
  42.7 1.0 copy-done.1
  43.6 1.2 fusion.2
  44.8 0.7 pad_maximum_fusion
  45.5 0.0 all-reduce.2.cloned.1.call-update
  45.5 0.0 all-gather.3.cloned.1.call-start
  45.6 0.7 all-gather.3.cloned.1.call-update
  46.3 30.4 %all-reduce.2.cloned.1.call-done = bf16[3,128,128]{1,2,0:T(8,128)(2,1)} async-done(((bf16[3,128,128]{1,2,0:T(8,128)(2,1)}), bf16[3,128,128]{1,2,0:T(8,128)(2,1)}) %all-reduce.2.cloned.1.call-update) | async-done | bytes 98320 | tf_op jit(solution)/shard_map/psum | solution.py:57
  76.6 1.0 convolution_multiply_fusion
  77.6 0.4 convolution_convert_fusion.1
  78.1 0.7 copy.41
  78.7 4.6 %all-to-all-start.1 = ((bf16[4,64,256]{2,1,0:T(8,128)(2,1)}), bf16[4,64,256]{2,1,0:T(8,128)(2,1)S(1)}, u32[]{:S(2)}, u32[]{:S(2)}) async-start(bf16[4,64,256]{2,1,0:T(8,128)(2,1)} %copy.41), calls=%async_computation.1 | async-start | bytes 262144 | tf_op jit(solution)/shard_map/all_to_all | solution.py:86
  83.3 1.2 fusion.10
  84.5 2.8 %convolution_convert_fusion = bf16[4,64,2048]{2,0,1:T(4,128)(2,1)S(1)} fusion(f32[3,64,2048]{2,1,0:T(8,128)S(1)} %fusion.10, s32[3]{0:T(128)S(1)} %select_reduce_fusion), kind=kOutput, calls=%fused_computation.2 | convolution fusion | flops 19398668 | bytes 2621452 | tf_op jit(solution)/shard_map/bs,brd->srd/dot_general | solution.py:81
  87.3 1.6 copy.39
  88.9 0.3 all-to-all-done.1
  89.2 4.8 %all-to-all-start = ((bf16[4,64,2048]{2,1,0:T(8,128)(2,1)}), bf16[4,64,2048]{2,1,0:T(8,128)(2,1)S(1)}, u32[]{:S(2)}, u32[]{:S(2)}) async-start(bf16[4,64,2048]{2,1,0:T(8,128)(2,1)} %copy.39), calls=%async_computation | async-start | bytes 2097152 | tf_op jit(solution)/shard_map/all_to_all | solution.py:85
  94.0 4.2 %fusion.9 = f32[3,128,2048]{2,1,0:T(8,128)} fusion(bf16[3,64,2048]{2,0,1:T(4,128)(2,1)} %copy-done.1, bf16[3,128,128]{1,2,0:T(8,128)(2,1)} %all-reduce.2.cloned.1.call-done), kind=kOutput, calls=%fused_computation.22 | convolution fusion | flops 100737024 | bytes 4243456 | tf_op jit(solution)/shard_map/tqi,tie->tqe/dot_general | solution.py:62
  98.2 0.6 convert_reduce_fusion.1
  98.9 48.3 %all-to-all-done = bf16[4,64,2048]{2,1,0:T(8,128)(2,1)S(1)} async-done(((bf16[4,64,2048]{2,1,0:T(8,128)(2,1)}), bf16[4,64,2048]{2,1,0:T(8,128)(2,1)S(1)}, u32[]{:S(2)}, u32[]{:S(2)}) %all-to-all-start) | async-done | bytes 1048608 | tf_op jit(solution)/shard_map/all_to_all | solution.py:85
  147.1 1.0 convert_reduce_fusion
  148.1 33.2 %all-gather.3.cloned.1.call-done = bf16[1024,2048]{1,0:T(8,128)(2,1)} async-done(((bf16[256,2048]{1,0:T(8,128)(2,1)}), bf16[1024,2048]{1,0:T(8,128)(2,1)}) %all-gather.3.cloned.1.call-update) | async-done | bytes 4194320 | tf_op jit(solution)/shard_map/all_gather | solution.py:31
  181.3 6.1 %fusion = bf16[384,2048]{1,0:T(8,128)(2,1)} fusion(f32[3,128,2048]{2,1,0:T(8,128)} %fusion.9, bf16[384,1024]{1,0:T(8,128)(2,1)S(1)} %broadcast_multiply_fusion, bf16[1024,2048]{1,0:T(8,128)(2,1)} %all-gather.3.cloned.1.call-done), kind=kOutput, calls=%fused_computation.1 | convolution fusion | flops 1612185600 | bytes 9699328 | tf_op jit(solution)/shard_map/dot_general | solution.py:29
  (1 shorter events, 0.0 us)
Async XLA Ops:
  7.2 35.5 %copy-start = (bf16[384,2048]{1,0:T(8,128)(2,1)S(1)}, bf16[384,2048]{1,0:T(8,128)(2,1)}, u32[]{:S(2)}) copy-start(bf16[384,2048]{1,0:T(8,128)(2,1)} %param.8) | copy-start | bytes 4718596
  7.2 33.2 %all-gather.5.cloned.1.call-start = ((), (), s32[]{:S(2)}) async-start(), calls=%async_computation.3 | async-start | bytes 1310720 | tf_op jit(solution)/shard_map/all_gather | solution.py:38
  7.9 68.7 %all-reduce.2.cloned.1.call-start = ((), (), s32[]{:S(2)}) async-start(), calls=%async_computation.4 | async-start | bytes 196608 | tf_op jit(solution)/shard_map/psum | solution.py:57
  42.7 1.0 copy-start.1
  45.5 135.8 %all-gather.3.cloned.1.call-start = ((), (), s32[]{:S(2)}) async-start(), calls=%async_computation.2 | async-start | bytes 5242880 | tf_op jit(solution)/shard_map/all_gather | solution.py:31
  78.7 10.5 %all-to-all-start.1 = ((bf16[4,64,256]{2,1,0:T(8,128)(2,1)}), bf16[4,64,256]{2,1,0:T(8,128)(2,1)S(1)}, u32[]{:S(2)}, u32[]{:S(2)}) async-start(bf16[4,64,256]{2,1,0:T(8,128)(2,1)} %copy.41), calls=%async_computation.1 | async-start | bytes 262144 | tf_op jit(solution)/shard_map/all_to_all | solution.py:86
  89.2 57.9 %all-to-all-start = ((bf16[4,64,2048]{2,1,0:T(8,128)(2,1)}), bf16[4,64,2048]{2,1,0:T(8,128)(2,1)S(1)}, u32[]{:S(2)}, u32[]{:S(2)}) async-start(bf16[4,64,2048]{2,1,0:T(8,128)(2,1)} %copy.39), calls=%async_computation | async-start | bytes 2097152 | tf_op jit(solution)/shard_map/all_to_all | solution.py:85
Sparse Core Ops, SparseCore 0:
  9.6 30.7 all-gather.4
  45.6 30.9 all-reduce.1
  78.3 103.0 all-gather.2
where the time goes:
time: 195 us; the launch traced here: 194 us
  waiting for transfers between devices  127 us (65%)
  matrix products  19.7 us (10%)
  blocking collectives  15.3 us (8%)
  between operations  13.8 us (7%)
  starting transfers between devices  9.49 us (5%)
  other arithmetic  5.04 us (3%)
  local copies, waits for them, and re-layouts  3.26 us (2%)
    all_to_all x1, waiting for transfers between devices, per_device(): lax.all_to_all(table_down, 'seq', split_axis=0, concat_axis=0, tiled=True)  48.3 us
    all_gather x1, waiting for transfers between devices, per_device(): lax.all_gather(value_weight, 'seq', axis=0, tiled=True)  33.2 us
    psum x1, waiting for transfers between devices, per_device(): lax.psum(joined.astype(jnp.bfloat16), ('tensor', 'pipe'))  30.4 us
    all_gather x1, blocking collectives, per_device(): up_piece = lax.all_gather(adapter_up, 'seq', axis=0, tiled=True)  15.3 us
    all_gather x1, waiting for transfers between devices, per_device(): down_piece = lax.all_gather(adapter_down, 'seq', axis=0, tiled=True)  13.8 us
    dot_general x1, matrix products, per_device(): jnp.dot(weighted, lax.all_gather(value_weight, 'seq', axis=0, tiled=True)...  6.1 us
    all_to_all x1, starting transfers between devices, per_device(): lax.all_to_all(table_down, 'seq', split_axis=0, concat_axis=0, tiled=True)  4.77 us
    all_to_all x1, starting transfers between devices, per_device(): lax.all_to_all(table_up, 'seq', split_axis=0, concat_axis=0, tiled=True)  4.6 us
  transfers between devices with their start and end apart: 5, of which 5 were waited for; matrix products, arithmetic and copies ran while one was open for 9% of the time, Pallas kernels for 0%

commit v1 on v0

v1 whole, which is shorter than its diff:
```python
import functools

import jax
import jax.numpy as jnp
from jax import lax
from jax.experimental import pallas as pl
from jax.experimental.pallas import tpu as pltpu
from jax.sharding import PartitionSpec as P

SCALE = 2.0
VMEM_LIMIT = 48 << 20
F32 = jnp.float32
BF16 = jnp.bfloat16


def project_kernel(slots, x_ref, w_ref, down_ref, up_ref, out_ref):
    blocks = slots.shape[0]
    rows = x_ref.shape[0] // blocks
    rank = down_ref.shape[1]
    contract = (((1,), (1,)), ((), ()))
    for b in range(blocks):
        s = slots[b]
        span = pl.ds(b * rows, rows)
        hidden = lax.dot_general(x_ref[span, :], down_ref[s], contract, preferred_element_type=F32)
        low = lax.dot_general(w_ref[span, :], up_ref[s], contract, preferred_element_type=F32)
        out_ref[span, :rank] = hidden.astype(BF16)
        out_ref[span, rank:] = low.astype(BF16)


def grads_kernel(slots, x_ref, w_ref, here_ref, there_ref, table_ref, low_ref, acc_ref):
    blocks = slots.shape[0]
    rows, width = x_ref.shape[0] // blocks, x_ref.shape[1]
    rank = low_ref.shape[1]
    contract = (((0,), (0,)), ((), ()))
    total = here_ref[...].astype(F32) + there_ref[...].astype(F32)
    hidden_b = total[:, :rank].astype(BF16)
    low_b = (SCALE * total[:, rank:]).astype(BF16)
    low_ref[...] = low_b
    acc_ref[...] = jnp.zeros_like(acc_ref)
    for b in range(blocks):
        s = slots[b]
        span = slice(b * rows, (b + 1) * rows)
        acc_ref[s, :, :width] += lax.dot_general(
            low_b[span], x_ref[span, :], contract, preferred_element_type=F32
        )
        acc_ref[s, :, width:] += SCALE * lax.dot_general(
            hidden_b[span], w_ref[span, :], contract, preferred_element_type=F32
        )
    table_ref[...] = acc_ref[...].astype(BF16)


def product_kernel(count, scalars, *refs):
    low_ref, weighted_ref, down_ref, own_ref = refs[:4]
    pieces, out_ref = refs[4 : 4 + count], refs[-1]
    rows, depth = low_ref.shape[0], own_ref.shape[0]
    blocks = scalars.shape[0] - 1
    block_rows = rows // blocks
    total = jnp.dot(weighted_ref[:, :depth], own_ref[...], preferred_element_type=F32)
    for j, piece in enumerate(pieces):
        total += jnp.dot(
            weighted_ref[:, (j + 1) * depth : (j + 2) * depth],
            piece[...],
            preferred_element_type=F32,
        )
    for b in range(blocks):
        span = slice(b * block_rows, (b + 1) * block_rows)
        term = jnp.dot(low_ref[span, :], down_ref[scalars[b]], preferred_element_type=F32)
        out_ref[span, :] = (total[span] + term).astype(BF16)


def product(half, slots, low_b, weighted, gathered, own, pieces, width, into=None):
    rows, rank = low_b.shape
    tenants = gathered.shape[0]
    depth = own.shape[0]
    part = width // 2
    tile = min(512, part)
    tiles = part // tile
    scalars = jnp.concatenate([slots, half[None]])
    blocks = slots.shape[0]
    whole = lambda i, s: (0, 0)
    column = lambda i, s: (0, s[blocks] * tiles + i)
    specs = [
        pl.BlockSpec((rows, rank), whole),
        pl.BlockSpec(weighted.shape, whole),
        pl.BlockSpec((tenants, rank, tile), lambda i, s: (0, 0, s[blocks] * tiles + i)),
        pl.BlockSpec((depth, tile), column),
    ] + [pl.BlockSpec((depth, tile), lambda i, s: (0, i)) for _ in pieces]
    operands = [low_b, weighted, gathered, own, *pieces]
    aliases = {}
    if into is not None:
        specs.append(pl.BlockSpec(memory_space=pl.ANY))
        operands.append(into)
        aliases = {len(operands): 0}
    return pl.pallas_call(
        functools.partial(product_kernel, len(pieces)),
        out_shape=jax.ShapeDtypeStruct((rows, width), BF16),
        grid_spec=pltpu.PrefetchScalarGridSpec(
            num_scalar_prefetch=1,
            grid=(tiles,),
            in_specs=specs,
            out_specs=pl.BlockSpec((rows, tile), column),
        ),
        input_output_aliases=aliases,
        compiler_params=pltpu.CompilerParams(vmem_limit_bytes=VMEM_LIMIT),
        cost_estimate=pl.CostEstimate(
            flops=2 * rows * part * (weighted.shape[1] + rank),
            bytes_accessed=2 * (part * (weighted.shape[1] + tenants * rank + rows)),
            transcendentals=0,
        ),
        name="product",
    )(scalars, *operands)


def project(slots, x, own_cols, gathered):
    rows, width = x.shape
    tenants, rank = gathered.shape[:2]
    slab = own_cols.shape[1]
    return pl.pallas_call(
        project_kernel,
        out_shape=jax.ShapeDtypeStruct((rows, 2 * rank), BF16),
        grid_spec=pltpu.PrefetchScalarGridSpec(
            num_scalar_prefetch=1,
            grid=(1,),
            in_specs=[
                pl.BlockSpec((rows, width), lambda i, s: (0, 0)),
                pl.BlockSpec((rows, slab), lambda i, s: (0, 0)),
                pl.BlockSpec((tenants, rank, width), lambda i, s: (0, 0, 0)),
                pl.BlockSpec((tenants, rank, slab), lambda i, s: (0, 0, width // slab)),
            ],
            out_specs=pl.BlockSpec((rows, 2 * rank), lambda i, s: (0, 0)),
        ),
        compiler_params=pltpu.CompilerParams(vmem_limit_bytes=VMEM_LIMIT),
        cost_estimate=pl.CostEstimate(
            flops=2 * rows * rank * (width + slab),
            bytes_accessed=2 * (rows + tenants * rank) * (width + slab),
            transcendentals=0,
        ),
        name="project",
    )(slots, x, own_cols, gathered, gathered)


def adapter_grads(slots, x, own_cols, here, there, tenants):
    rows, width = x.shape
    rank = here.shape[1] // 2
    slab = own_cols.shape[1]
    return pl.pallas_call(
        grads_kernel,
        out_shape=(
            jax.ShapeDtypeStruct((tenants, rank, width + slab), BF16),
            jax.ShapeDtypeStruct((rows, rank), BF16),
        ),
        grid_spec=pltpu.PrefetchScalarGridSpec(
            num_scalar_prefetch=1,
            grid=(1,),
            in_specs=[
                pl.BlockSpec((rows, width), lambda i, s: (0, 0)),
                pl.BlockSpec((rows, slab), lambda i, s: (0, 0)),
                pl.BlockSpec((rows, 2 * rank), lambda i, s: (0, 0)),
                pl.BlockSpec((rows, 2 * rank), lambda i, s: (0, 0)),
            ],
            out_specs=[
                pl.BlockSpec((tenants, rank, width + slab), lambda i, s: (0, 0, 0)),
                pl.BlockSpec((rows, rank), lambda i, s: (0, 0)),
            ],
            scratch_shapes=[pltpu.VMEM((tenants, rank, width + slab), F32)],
        ),
        compiler_params=pltpu.CompilerParams(vmem_limit_bytes=VMEM_LIMIT),
        cost_estimate=pl.CostEstimate(
            flops=2 * rows * rank * (width + slab),
            bytes_accessed=2 * (rows + tenants * rank) * (width + slab),
            transcendentals=0,
        ),
        name="adapter_grads",
    )(slots, x, own_cols, here, there)


def arrivals(n):
    table = []
    for i in range(n):
        order = []
        for k in range(1, n):
            if i >= k:
                order.append(("up", k))
            if i + k < n:
                order.append(("down", k))
        table.append(order)
    return table


def pick(me, choices):
    out = choices[0]
    for i in range(1, len(choices)):
        if any(choices[i] is c for c in choices[:i]) and choices[i] is choices[i - 1]:
            continue
        out = jnp.where(me >= i, choices[i], out)
    return out


def gather_line(piece, n):
    me = lax.axis_index("seq")
    got = {}
    up = down = piece
    for k in range(1, n):
        up_pairs = [(i, i + 1) for i in range(k - 1, n - 1)]
        down_pairs = [(i + 1, i) for i in range(n - k)]
        if {a for a, _ in up_pairs} & {a for a, _ in down_pairs}:
            up = lax.ppermute(up, "seq", up_pairs)
            down = lax.ppermute(down, "seq", down_pairs)
        else:
            both = jnp.where(me >= k - 1, up, down)
            up = down = lax.ppermute(both, "seq", up_pairs + down_pairs)
        got["up", k], got["down", k] = up, down
    table = arrivals(n)
    pieces, owners = [], []
    for j in range(n - 1):
        pieces.append(pick(me, [got[table[i][j]] for i in range(n)]))
        source = [i - k if d == "up" else i + k for i in range(n) for d, k in [table[i][j]]]
        owners.append(jnp.asarray(source, jnp.int32)[me])
    return pieces, owners


def per_device(
    sizes,
    layer_input,
    out_grad,
    value_weight,
    adapter_down,
    adapter_up,
    block_tenant,
    tenant_slot,
    forget_flag,
):
    n, groups = sizes
    token_rows, width = layer_input.shape
    owned, rank, _ = adapter_down.shape
    slab = adapter_up.shape[2]
    tenants = tenant_slot.shape[0]
    depth = value_weight.shape[0]
    swap = lambda axis: functools.partial(lax.ppermute, axis_name=axis, perm=[(0, 1), (1, 0)])

    adapters = jnp.concatenate([adapter_down, adapter_up], axis=2)
    gathered = lax.all_gather(adapters, "seq", axis=0, tiled=True)

    group = lax.axis_index("groups").astype(jnp.int32)
    piece = lax.dynamic_slice_in_dim(value_weight, group * (width // 2), width // 2, 1)
    mine, owners = gather_line(piece, n)
    other = [swap("groups")(p) for p in mine]

    row_sign = (1 - 2 * forget_flag).astype(BF16)
    weighted = out_grad * row_sign[:, None]
    tenant_ids = jnp.arange(tenants, dtype=jnp.int32)
    slots = jnp.sum(
        jnp.where(block_tenant == tenant_ids[None, :], tenant_slot[None, :], 0), axis=1
    ).astype(jnp.int32)
    slab_index = lax.axis_index(("tensor", "pipe"))
    own_cols = lax.dynamic_slice_in_dim(weighted, slab_index * slab, slab, 1)
    me = lax.axis_index("seq")
    ordered = jnp.concatenate(
        [lax.dynamic_slice_in_dim(weighted, o * depth, depth, 1) for o in [me, *owners]], axis=1
    )

    part = project(slots, layer_input, own_cols, gathered)
    here = part
    axes = [a for a in ("pipe", "tensor")]
    for axis in axes[:-1]:
        here = (here.astype(F32) + line_sum_rest(here, axis, sizes)).astype(BF16)
    there = line_sum_rest(here, axes[-1], sizes).astype(BF16)
    table, low_b = adapter_grads(slots, layer_input, own_cols, here, there, tenants)
    got = lax.all_to_all(table, "seq", split_axis=0, concat_axis=0, tiled=True)
    total = jnp.sum(got.astype(F32).reshape(n, owned, rank, width + slab), axis=0)
    down_grad, up_grad = total[:, :, :width], total[:, :, width:]

    half = product(group, slots, low_b, ordered, gathered, value_weight, mine, width)
    full = product(1 - group, slots, low_b, ordered, gathered, value_weight, other, width, half)
    return full, down_grad, up_grad


def line_sum_rest(value, axis, sizes):
    size = lax.axis_size(axis)
    rest = 0.0
    for d in range(1, size):
        rest = rest + lax.ppermute(
            value, axis, [(i, (i + d) % size) for i in range(size)]
        ).astype(F32)
    return rest


def solution(mesh):
    sizes = (mesh.shape["seq"], mesh.shape["groups"])
    return jax.shard_map(
        functools.partial(per_device, sizes),
        mesh=mesh,
        in_specs=(
            P(("groups", "seq"), ("tensor", "pipe")),
            P(("groups", "seq"), None),
            P("seq", ("tensor", "pipe")),
            P("seq", None, ("tensor", "pipe")),
            P("seq", None, ("tensor", "pipe")),
            P(("groups", "seq"), None),
            P(),
            P(("groups", "seq")),
        ),
        out_specs=(
            P(("groups", "seq"), ("tensor", "pipe")),
            P(("groups", "seq"), None, ("tensor", "pipe")),
            P(("groups", "seq"), None, ("tensor", "pipe")),
        ),
        check_vma=False,
    )
```

time: 195 us -> 152 us (0.78)
  waiting for transfers between devices: 127 us -> 90 us
  matrix products: 19.7 us -> 0 us
  blocking collectives: 15.3 us -> 0 us
  Pallas kernels: 0 us -> 11.3 us
  starting transfers between devices: 9.49 us -> 19.1 us
  local copies, waits for them, and re-layouts: 3.26 us -> 7.58 us
  between operations: 13.8 us -> 16.3 us
  other arithmetic: 5.04 us -> 7.49 us
    ppermute x0 -> x10, waiting for transfers between devices: none -> 88.6 us  [the longest x1 30.8 us: gather_line(): up = down = lax.ppermute(both, 'seq', up_pairs + down_pairs)]
    all_to_all x2 -> x1, waiting for transfers between devices: 48.6 us -> 0.01 us  [per_device(): got = lax.all_to_all(table, 'seq', split_axis=0, concat_axis=0, tiled=True)]
    all_gather x2 -> x1, waiting for transfers between devices: 47 us -> 1.34 us  [per_device(): gathered = lax.all_gather(adapters, 'seq', axis=0, tiled=True)]
    psum x1 -> x0, waiting for transfers between devices: 30.4 us -> none  [per_device(): lax.psum(joined.astype(jnp.bfloat16), ('tensor', 'pipe'))]
    dot_general x10 -> x0, matrix products: 19.7 us -> none  [the longest x1 6.1 us: per_device(): jnp.dot(weighted, lax.all_gather(value_weight, 'seq', axis=0, tiled=True)...]
    all_gather x1 -> x0, blocking collectives: 15.3 us -> none  [per_device(): up_piece = lax.all_gather(adapter_up, 'seq', axis=0, tiled=True)]
    ppermute x0 -> x10, starting transfers between devices: none -> 14.7 us  [the longest x2 5.63 us: gather_line(): up = lax.ppermute(up, 'seq', up_pairs)]
    pallas_call x0 -> x4, Pallas kernels: none -> 11.3 us  [the longest x2 7.65 us: product(): pl.pallas_call(functools.partial(product_kernel, len(pieces)), out_shape=...]
  transfers between devices with their start and end apart: 5 -> 12, of which waited for: 5 -> 9; matrix products, arithmetic and copies ran while one was open for 9% -> 6% of each run, Pallas kernels for 0% -> 7%
where the time goes in v1:
time: 152 us
  waiting for transfers between devices  90 us (59%)
  starting transfers between devices  19.1 us (13%)
  between operations  16.3 us (11%)
  Pallas kernels  11.3 us (7%)
  local copies, waits for them, and re-layouts  7.58 us (5%)
  other arithmetic  7.49 us (5%)
    ppermute x1, waiting for transfers between devices, gather_line(): up = down = lax.ppermute(both, 'seq', up_pairs + down_pairs)  30.8 us
    ppermute x3, waiting for transfers between devices, per_device(): other = [swap('groups')(p) for p in mine]  26.3 us
    ppermute x2, waiting for transfers between devices, gather_line(): down = lax.ppermute(down, 'seq', down_pairs)  14.5 us
    ppermute x2, waiting for transfers between devices, gather_line(): up = lax.ppermute(up, 'seq', up_pairs)  12.3 us
    pallas_call x2, Pallas kernels, product(): pl.pallas_call(functools.partial(product_kernel, len(pieces)), out_shape=...  7.65 us
    ppermute x2, starting transfers between devices, gather_line(): up = lax.ppermute(up, 'seq', up_pairs)  5.63 us
    ppermute x2, waiting for transfers between devices, line_sum_rest(): lax.ppermute(value, axis, [(i, (i + d) % size) for i in range(size)])  4.61 us
    all_to_all x1, starting transfers between devices, per_device(): got = lax.all_to_all(table, 'seq', split_axis=0, concat_axis=0, tiled=True)  4.39 us
  transfers between devices with their start and end apart: 12, of which 9 were waited for; matrix products, arithmetic and copies ran while one was open for 6% of the time, Pallas kernels for 7%

profile of v1, /device:TPU:0, one launch (start us, length us, event | category | flops | bytes accessed | tf_op | source)
XLA Modules:
  0.0 151.8 jit_solution(4461602583540142422)
XLA Ops:
  7.2 0.0 copy-start.14
  7.2 0.0 copy-start.13
  7.2 0.0 copy-start.12
  7.2 0.0 copy-start.9
  7.2 0.0 copy-start.6
  7.2 0.0 all-gather.2.cloned.1.call-start
  7.3 1.8 %pad_maximum_fusion.1 = bf16[1,64,2304]{2,1,0:T(8,128)(2,1)} fusion(bf16[1,64,256]{2,1,0:T(8,128)(2,1)} %param.15, bf16[1,64,2048]{2,1,0:T(8,128)(2,1)} %param.14), kind=kLoop, calls=%fused_computation.7 | loop fusion | flops 589824 | bytes 589824 | tf_op jit(solution)/shard_map/concatenate | solution.py:241
  9.0 0.0 all-gather.2.cloned.1.call-update
  9.1 1.9 %constant_dynamic-slice_fusion = bf16[256,1024]{1,0:T(8,128)(2,1)} fusion(bf16[256,2048]{1,0:T(8,128)(2,1)} %refs_3_.3, s32[]{:T(128)S(6)} %select_n.71), kind=kLoop, calls=%fused_computation.12 | loop fusion | bytes 1048580 | tf_op jit(solution)/shard_map/dynamic_slice | solution.py:245
  10.9 4.9 %collective-permute-start.2 = (bf16[256,1024]{1,0:T(8,128)(2,1)}, bf16[256,1024]{1,0:T(8,128)(2,1)S(1)}, u32[]{:S(2)}, u32[]{:S(2)}) collective-permute-start(bf16[256,1024]{1,0:T(8,128)(2,1)} %constant_dynamic-slice_fusion), channel_id=1, source_target_pairs={{0,4},{4,8},{8,12},{1,5},{5,9},{9,13},{2,6},{6,10},{10,14},{3,7},{... | collective-permute-start | bytes 1572872 | tf_op jit(solution)/shard_map/ppermute | solution.py:207
  15.9 1.3 collective-permute-start.3
  17.2 0.0 copy-done.14
  17.2 0.7 dynamic_slice.29
  18.5 0.0 copy-done.13
  18.5 0.6 dynamic_slice.31
  19.7 0.0 copy-done.12
  19.8 0.7 dynamic_slice.33
  21.1 0.0 copy-done.9
  21.2 0.0 copy-done.6
  21.2 0.0 copy-start.10
  21.2 0.0 copy-start.11
  21.2 0.0 copy-start.3
  21.2 0.1 broadcast_multiply_fusion
  21.3 1.0 constant_dynamic-slice_fusion.4
  22.3 12.3 %collective-permute-done.2 = bf16[256,1024]{1,0:T(8,128)(2,1)S(1)} collective-permute-done((bf16[256,1024]{1,0:T(8,128)(2,1)}, bf16[256,1024]{1,0:T(8,128)(2,1)S(1)}, u32[]{:S(2)}, u32[]{:S(2)}) %collective-permute-start.2) | collective-permute-done | bytes 524320 | tf_op jit(solution)/shard_map/ppermute | solution.py:207
  34.6 0.7 collective-permute-start.5
  35.3 14.5 %collective-permute-done.3 = bf16[256,1024]{1,0:T(8,128)(2,1)} collective-permute-done((bf16[256,1024]{1,0:T(8,128)(2,1)}, bf16[256,1024]{1,0:T(8,128)(2,1)}, u32[]{:S(2)}, u32[]{:S(2)}) %collective-permute-start.3) | collective-permute-done | bytes 524320 | tf_op jit(solution)/shard_map/ppermute | solution.py:208
  49.9 1.3 collective-permute-start.6
  51.1 0.0 copy-done.10
  51.2 0.0 copy-done.11
  51.2 0.2 select_reduce_fusion.slots
  51.3 1.3 all-gather.2.cloned.1.call-done.down_ref.up_ref.refs_2_
  52.7 0.0 copy-done.3
  52.7 1.3 copy-done
  54.0 1.3 project.1
  55.3 0.0 copy-done.7
  55.3 0.1 collective-permute-start
  55.4 1.2 collective-permute-done
  56.7 1.6 %collective-permute-start.1 = (bf16[384,128]{1,0:T(8,128)(2,1)S(1)}, bf16[384,128]{1,0:T(8,128)(2,1)S(1)}, u32[]{:S(2)}, u32[]{:S(2)}) collective-permute-start(bf16[384,128]{1,0:T(8,128)(2,1)S(1)} %add_convert_fusion.here_ref), channel_id=1, source_target_pairs={{0,2},{2,0},{1,3},{3,1},{4,6},{6,4},{5,7},{7,5},{8,10},{10,8},{9,1... | collective-permute-start | bytes 294920 | tf_op jit(solution)/shard_map/ppermute | solution.py:282
  58.2 3.4 %collective-permute-done.1.there_ref = bf16[384,128]{1,0:T(8,128)(2,1)S(1)} collective-permute-done((bf16[384,128]{1,0:T(8,128)(2,1)S(1)}, bf16[384,128]{1,0:T(8,128)(2,1)S(1)}, u32[]{:S(2)}, u32[]{:S(2)}) %collective-permute-start.1) | collective-permute-done | bytes 98336 | tf_op jit(solution)/shard_map/ppermute | solution.py:282
  61.6 2.3 %adapter_grads.1 = (bf16[4,64,2304]{2,1,0:T(8,128)(2,1)}, bf16[384,64]{1,0:T(8,128)(2,1)S(1)}) custom-call(s32[3]{0:T(128)S(1)} %select_reduce_fusion.slots, bf16[384,2048]{1,0:T(8,128)(2,1)S(1)} %copy-done.3, bf16[384,256]{1,0:T(8,128)(2,1)S(1)} %get-tuple-element.13.w_ref, bf16[384,128]{1,0:T(8,128)(2,1)S(1)} %add_convert_fusion.here_ref, ...), custom_call_target="tpu_custom_call" | custom-call | flops 113246208 | bytes 2949120 | tf_op jit(solution)/shard_map/adapter_grads/pallas_call | solution.py:146
  63.9 4.4 %all-to-all-start = ((bf16[4,64,2304]{2,1,0:T(8,128)(2,1)}), bf16[4,64,2304]{2,1,0:T(8,128)(2,1)}, u32[]{:S(2)}, u32[]{:S(2)}) async-start(bf16[4,64,2304]{2,1,0:T(8,128)(2,1)} %get-tuple-element.6), calls=%async_computation | async-start | bytes 2359296 | tf_op jit(solution)/shard_map/all_to_all | solution.py:269
  68.3 0.0 collective-permute-done.5
  68.4 0.0 copy-start.4
  68.4 0.0 collective-permute-done.6
  68.4 0.0 copy-start.5
  68.4 0.1 broadcast_select_fusion
  68.5 1.3 collective-permute-start.8
  69.8 30.8 %collective-permute-done.8 = bf16[256,1024]{1,0:T(8,128)(2,1)S(1)} collective-permute-done((bf16[256,1024]{1,0:T(8,128)(2,1)S(1)}, bf16[256,1024]{1,0:T(8,128)(2,1)S(1)}, u32[]{:S(2)}, u32[]{:S(2)}) %collective-permute-start.8) | collective-permute-done | bytes 524320 | tf_op jit(solution)/shard_map/ppermute | solution.py:211
  100.6 2.4 %select_select_fusion = (bf16[256,1024]{1,0:T(8,128)(2,1)S(1)}, bf16[256,1024]{1,0:T(8,128)(2,1)S(1)}, bf16[256,1024]{1,0:T(8,128)(2,1)}) fusion(bf16[256,1024]{1,0:T(8,128)(2,1)S(1)} %collective-permute-done.8, bf16[256,1024]{1,0:T(8,128)(2,1)} %copy-done.4, bf16[256,1024]{1,0:T(8,128)(2,1)} %copy-done.5, pred[]{:T(512)S(6)} %ge.15, pred[]{:T(512)S(6)} %ge.14, ...), kind=kLoop, calls=%fused_computation.2 | loop fusion | flops 1572864 | bytes 4194307 | tf_op jit(solution)/shard_map/jit(_where)/select_n | solution.py:195
  103.1 1.5 collective-permute-start.4
  104.6 0.5 collective-permute-start.7
  105.1 1.5 collective-permute-start.9
  106.6 0.1 pad_add_fusion.1
  106.7 1.3 pad_maximum_fusion.refs_1_
  108.0 3.7 %product.2.refs_7_ = bf16[384,2048]{1,0:T(8,128)(2,1)} custom-call(s32[4]{0:T(128)S(1)} %get-tuple-element.15.scalars, bf16[384,64]{1,0:T(8,128)(2,1)S(1)} %get-tuple-element.5.refs_0_, bf16[384,1024]{1,0:T(8,128)(2,1)S(1)} %pad_maximum_fusion.refs_1_, bf16[4,64,2304]{2,1,0:T(8,128)(2,1)S(1)} %copy-done.1, bf16[256,2048]{1,0:T(8,128)(2,1)S(1)} %copy-done.2, ...), custom_call_target="tpu_custom_call" | custom-call | flops 855638016 | bytes 3407872 | tf_op jit(solution)/shard_map/product/pallas_call | solution.py:94
  111.8 6.5 %collective-permute-done.4.refs_4_ = bf16[256,1024]{1,0:T(8,128)(2,1)} collective-permute-done((bf16[256,1024]{1,0:T(8,128)(2,1)}, bf16[256,1024]{1,0:T(8,128)(2,1)}, u32[]{:S(2)}, u32[]{:S(2)}) %collective-permute-start.4) | collective-permute-done | bytes 524320 | tf_op jit(solution)/shard_map/ppermute | solution.py:247
  118.2 11.2 %collective-permute-done.7.refs_5_ = bf16[256,1024]{1,0:T(8,128)(2,1)} collective-permute-done((bf16[256,1024]{1,0:T(8,128)(2,1)S(1)}, bf16[256,1024]{1,0:T(8,128)(2,1)}, u32[]{:S(2)}, u32[]{:S(2)}) %collective-permute-start.7) | collective-permute-done | bytes 524320 | tf_op jit(solution)/shard_map/ppermute | solution.py:247
  129.5 8.6 %collective-permute-done.9.refs_6_ = bf16[256,1024]{1,0:T(8,128)(2,1)} collective-permute-done((bf16[256,1024]{1,0:T(8,128)(2,1)S(1)}, bf16[256,1024]{1,0:T(8,128)(2,1)}, u32[]{:S(2)}, u32[]{:S(2)}) %collective-permute-start.9) | collective-permute-done | bytes 524320 | tf_op jit(solution)/shard_map/ppermute | solution.py:247
  138.1 3.9 %product.3 = bf16[384,2048]{1,0:T(8,128)(2,1)} custom-call(s32[4]{0:T(128)S(1)} %get-tuple-element.16.scalars, bf16[384,64]{1,0:T(8,128)(2,1)S(1)} %get-tuple-element.5.refs_0_, bf16[384,1024]{1,0:T(8,128)(2,1)S(1)} %pad_maximum_fusion.refs_1_, bf16[4,64,2304]{2,1,0:T(8,128)(2,1)S(1)} %copy-done.1, ...), custom_call_target="tpu_custom_call", output_to_operand_aliasing={{}: (8, {})} | custom-call | flops 855638016 | bytes 3407872 | tf_op jit(solution)/shard_map/product/pallas_call | solution.py:94
  142.0 0.0 all-to-all-done
  142.0 1.5 convert_reduce_fusion
  143.5 0.8 slice.8
  144.3 0.6 slice.9
  (12 shorter events, 0.1 us)
Async XLA Ops:
  7.2 10.0 %copy-start.14 = (s32[4]{0:T(128)S(1)}, s32[4]{0:T(128)}, u32[]{:S(2)}) copy-start(s32[4]{0:T(128)} %constant.45.clone) | copy-start | bytes 52
  7.2 11.3 %copy-start.13 = (s32[4]{0:T(128)S(1)}, s32[4]{0:T(128)}, u32[]{:S(2)}) copy-start(s32[4]{0:T(128)} %constant.46.clone) | copy-start | bytes 52
  7.2 12.6 %copy-start.12 = (s32[4]{0:T(128)S(1)}, s32[4]{0:T(128)}, u32[]{:S(2)}) copy-start(s32[4]{0:T(128)} %constant.47.clone) | copy-start | bytes 52
  7.2 13.9 %copy-start.9 = (s32[384]{0:T(512)S(1)}, s32[384]{0:T(512)}, u32[]{:S(2)}) copy-start(s32[384]{0:T(512)} %param.18) | copy-start | bytes 4612
  7.2 14.0 %copy-start.6 = (bf16[384,1024]{1,0:T(8,128)(2,1)S(1)}, bf16[384,1024]{1,0:T(8,128)(2,1)}, u32[]{:S(2)}) copy-start(bf16[384,1024]{1,0:T(8,128)(2,1)} %param.12) | copy-start | bytes 2359300
  7.2 45.5 %all-gather.2.cloned.1.call-start = ((), (), s32[]{:S(2)}) async-start(), calls=%async_computation.1 | async-start | bytes 1474560 | tf_op jit(solution)/shard_map/all_gather | solution.py:242
  10.9 23.7 %collective-permute-start.2 = (bf16[256,1024]{1,0:T(8,128)(2,1)}, bf16[256,1024]{1,0:T(8,128)(2,1)S(1)}, u32[]{:S(2)}, u32[]{:S(2)}) collective-permute-start(bf16[256,1024]{1,0:T(8,128)(2,1)} %constant_dynamic-slice_fusion), channel_id=1, source_target_pairs={{0,4},{4,8},{8,12},{1,5},{5,9},{9,13},{2,6},{6,10},{10,14},{3,7},{... | collective-permute-start | bytes 1572872 | tf_op jit(solution)/shard_map/ppermute | solution.py:207
  15.9 34.0 %collective-permute-start.3 = (bf16[256,1024]{1,0:T(8,128)(2,1)}, bf16[256,1024]{1,0:T(8,128)(2,1)}, u32[]{:S(2)}, u32[]{:S(2)}) collective-permute-start(bf16[256,1024]{1,0:T(8,128)(2,1)} %constant_dynamic-slice_fusion), channel_id=1, source_target_pairs={{4,0},{8,4},{12,8},{5,1},{9,5},{13,9},{6,2},{10,6},{14,10},{7,3},{... | collective-permute-start | bytes 1572872 | tf_op jit(solution)/shard_map/ppermute | solution.py:208
  21.2 30.0 %copy-start.10 = (s32[4]{0:T(128)S(1)}, s32[4]{0:T(128)}, u32[]{:S(2)}) copy-start(s32[4]{0:T(128)} %param.17) | copy-start | bytes 52
  21.2 30.0 %copy-start.11 = (s32[3,1]{0,1:T(1,128)S(1)}, s32[3,1]{0,1:T(1,128)}, u32[]{:S(2)}) copy-start(s32[3,1]{0,1:T(1,128)} %param.16) | copy-start | bytes 40
  21.2 31.5 %copy-start.3 = (bf16[384,2048]{1,0:T(8,128)(2,1)S(1)}, bf16[384,2048]{1,0:T(8,128)(2,1)}, u32[]{:S(2)}) copy-start(bf16[384,2048]{1,0:T(8,128)(2,1)} %x_ref.3) | copy-start | bytes 4718596
  34.6 20.6 %copy-start.7 = (bf16[256,1024]{1,0:T(8,128)(2,1)}, bf16[256,1024]{1,0:T(8,128)(2,1)S(1)}, u32[]{:S(2)}) copy-start(bf16[256,1024]{1,0:T(8,128)(2,1)S(1)} %collective-permute-done.2) | copy-start | bytes 1572868
  34.6 33.7 %collective-permute-start.5 = (bf16[256,1024]{1,0:T(8,128)(2,1)S(1)}, bf16[256,1024]{1,0:T(8,128)(2,1)S(1)}, u32[]{:S(2)}, u32[]{:S(2)}) collective-permute-start(bf16[256,1024]{1,0:T(8,128)(2,1)S(1)} %collective-permute-done.2), channel_id=1, source_target_pairs={{4,8},{8,12},{5,9},{9,13},{6,10},{10,14},{7,11},{11,15},{20,24},{2... | collective-permute-start | bytes 1572872 | tf_op jit(solution)/shard_map/ppermute | solution.py:207
  49.9 18.5 %collective-permute-start.6 = (bf16[256,1024]{1,0:T(8,128)(2,1)}, bf16[256,1024]{1,0:T(8,128)(2,1)S(1)}, u32[]{:S(2)}, u32[]{:S(2)}) collective-permute-start(bf16[256,1024]{1,0:T(8,128)(2,1)} %collective-permute-done.3), channel_id=1, source_target_pairs={{4,0},{8,4},{5,1},{9,5},{6,2},{10,6},{7,3},{11,7},{20,16},{24,20},... | collective-permute-start | bytes 1572872 | tf_op jit(solution)/shard_map/ppermute | solution.py:208
  52.7 1.3 copy-start
  55.3 1.4 collective-permute-start
  56.7 4.9 %collective-permute-start.1 = (bf16[384,128]{1,0:T(8,128)(2,1)S(1)}, bf16[384,128]{1,0:T(8,128)(2,1)S(1)}, u32[]{:S(2)}, u32[]{:S(2)}) collective-permute-start(bf16[384,128]{1,0:T(8,128)(2,1)S(1)} %add_convert_fusion.here_ref), channel_id=1, source_target_pairs={{0,2},{2,0},{1,3},{3,1},{4,6},{6,4},{5,7},{7,5},{8,10},{10,8},{9,1... | collective-permute-start | bytes 294920 | tf_op jit(solution)/shard_map/ppermute | solution.py:282
  63.9 36.7 %copy-start.8 = (bf16[256,1024]{1,0:T(8,128)(2,1)S(1)}, bf16[256,1024]{1,0:T(8,128)(2,1)}, u32[]{:S(2)}) copy-start(bf16[256,1024]{1,0:T(8,128)(2,1)} %copy-done.7) | copy-start | bytes 1572868
  63.9 78.0 %all-to-all-start = ((bf16[4,64,2304]{2,1,0:T(8,128)(2,1)}), bf16[4,64,2304]{2,1,0:T(8,128)(2,1)}, u32[]{:S(2)}, u32[]{:S(2)}) async-start(bf16[4,64,2304]{2,1,0:T(8,128)(2,1)} %get-tuple-element.6), calls=%async_computation | async-start | bytes 2359296 | tf_op jit(solution)/shard_map/all_to_all | solution.py:269
  68.4 1.4 copy-start.4
  68.4 1.4 copy-start.5
  68.5 32.2 %collective-permute-start.8 = (bf16[256,1024]{1,0:T(8,128)(2,1)S(1)}, bf16[256,1024]{1,0:T(8,128)(2,1)S(1)}, u32[]{:S(2)}, u32[]{:S(2)}) collective-permute-start(bf16[256,1024]{1,0:T(8,128)(2,1)S(1)} %broadcast_select_fusion), channel_id=1, source_target_pairs={{8,12},{4,0},{9,13},{5,1},{10,14},{6,2},{11,15},{7,3},{24,28},{20,... | collective-permute-start | bytes 1572872 | tf_op jit(solution)/shard_map/ppermute | solution.py:211
  100.6 7.4 %copy-start.2 = (bf16[256,2048]{1,0:T(8,128)(2,1)S(1)}, bf16[256,2048]{1,0:T(8,128)(2,1)}, u32[]{:S(2)}) copy-start(bf16[256,2048]{1,0:T(8,128)(2,1)} %refs_3_.3) | copy-start | bytes 3145732
  103.1 5.0 %copy-start.1 = (bf16[4,64,2304]{2,1,0:T(8,128)(2,1)S(1)}, bf16[4,64,2304]{2,1,0:T(8,128)(2,1)}, u32[]{:S(2)}) copy-start(bf16[4,64,2304]{2,1,0:T(8,128)(2,1)} %all-gather.2.cloned.1.call-done.down_ref.up_ref.refs_2_) | copy-start | bytes 3538948
  103.1 15.2 %collective-permute-start.4 = (bf16[256,1024]{1,0:T(8,128)(2,1)}, bf16[256,1024]{1,0:T(8,128)(2,1)}, u32[]{:S(2)}, u32[]{:S(2)}) collective-permute-start(bf16[256,1024]{1,0:T(8,128)(2,1)} %get-tuple-element.14.refs_4_), channel_id=1, source_target_pairs={{0,16},{16,0},{1,17},{17,1},{2,18},{18,2},{3,19},{19,3},{4,20},{20... | collective-permute-start | bytes 1572872 | tf_op jit(solution)/shard_map/ppermute | solution.py:247
  104.6 24.9 %collective-permute-start.7 = (bf16[256,1024]{1,0:T(8,128)(2,1)S(1)}, bf16[256,1024]{1,0:T(8,128)(2,1)}, u32[]{:S(2)}, u32[]{:S(2)}) collective-permute-start(bf16[256,1024]{1,0:T(8,128)(2,1)S(1)} %get-tuple-element.8.refs_5_), channel_id=1, source_target_pairs={{0,16},{16,0},{1,17},{17,1},{2,18},{18,2},{3,19},{19,3},{4,20},{20... | collective-permute-start | bytes 1572872 | tf_op jit(solution)/shard_map/ppermute | solution.py:247
  105.1 33.0 %collective-permute-start.9 = (bf16[256,1024]{1,0:T(8,128)(2,1)S(1)}, bf16[256,1024]{1,0:T(8,128)(2,1)}, u32[]{:S(2)}, u32[]{:S(2)}) collective-permute-start(bf16[256,1024]{1,0:T(8,128)(2,1)S(1)} %get-tuple-element.7.refs_6_), channel_id=1, source_target_pairs={{0,16},{16,0},{1,17},{17,1},{2,18},{18,2},{3,19},{19,3},{4,20},{20... | collective-permute-start | bytes 1572872 | tf_op jit(solution)/shard_map/ppermute | solution.py:247
Sparse Core Ops, SparseCore 0:
  10.2 42.4 all-gather.1

commit v2 on v1

--- a/solution.py
+++ b/solution.py
@@ -13,18 +13,31 @@
 BF16 = jnp.bfloat16
 
 
-def project_kernel(slots, x_ref, w_ref, down_ref, up_ref, out_ref):
-    blocks = slots.shape[0]
+def project_kernel(blocks, scalars, x_ref, w_ref, mine_ref, other_ref, up_ref, out_ref):
     rows = x_ref.shape[0] // blocks
-    rank = down_ref.shape[1]
+    rank, part = mine_ref.shape[1:]
     contract = (((1,), (1,)), ((), ()))
-    for b in range(blocks):
-        s = slots[b]
-        span = pl.ds(b * rows, rows)
-        hidden = lax.dot_general(x_ref[span, :], down_ref[s], contract, preferred_element_type=F32)
-        low = lax.dot_general(w_ref[span, :], up_ref[s], contract, preferred_element_type=F32)
-        out_ref[span, :rank] = hidden.astype(BF16)
-        out_ref[span, rank:] = low.astype(BF16)
+
+    def run(first, second):
+        for b in range(blocks):
+            s = scalars[b]
+            span = slice(b * rows, (b + 1) * rows)
+            hidden = lax.dot_general(
+                x_ref[span, :part], first[s], contract, preferred_element_type=F32
+            ) + lax.dot_general(
+                x_ref[span, part:], second[s], contract, preferred_element_type=F32
+            )
+            low = lax.dot_general(w_ref[span, :], up_ref[s], contract, preferred_element_type=F32)
+            out_ref[span, :rank] = hidden.astype(BF16)
+            out_ref[span, rank:] = low.astype(BF16)
+
+    @pl.when(scalars[blocks] == 0)
+    def _():
+        run(mine_ref, other_ref)
+
+    @pl.when(scalars[blocks] != 0)
+    def _():
+        run(other_ref, mine_ref)
 
 
 def grads_kernel(slots, x_ref, w_ref, here_ref, there_ref, table_ref, low_ref, acc_ref):
@@ -49,56 +62,61 @@
     table_ref[...] = acc_ref[...].astype(BF16)
 
 
-def product_kernel(count, scalars, *refs):
+def product_kernel(count, blocks, scalars, *refs):
     low_ref, weighted_ref, down_ref, own_ref = refs[:4]
-    pieces, out_ref = refs[4 : 4 + count], refs[-1]
+    pieces, out_ref, acc_ref = refs[4 : 4 + count], refs[-2], refs[-1]
     rows, depth = low_ref.shape[0], own_ref.shape[0]
-    blocks = scalars.shape[0] - 1
     block_rows = rows // blocks
-    total = jnp.dot(weighted_ref[:, :depth], own_ref[...], preferred_element_type=F32)
-    for j, piece in enumerate(pieces):
-        total += jnp.dot(
-            weighted_ref[:, (j + 1) * depth : (j + 2) * depth],
-            piece[...],
-            preferred_element_type=F32,
-        )
     for b in range(blocks):
         span = slice(b * block_rows, (b + 1) * block_rows)
-        term = jnp.dot(low_ref[span, :], down_ref[scalars[b]], preferred_element_type=F32)
-        out_ref[span, :] = (total[span] + term).astype(BF16)
-
-
-def product(half, slots, low_b, weighted, gathered, own, pieces, width, into=None):
+        acc_ref[span, :] = jnp.dot(
+            low_ref[span, :], down_ref[scalars[b]], preferred_element_type=F32
+        ) + jnp.dot(weighted_ref[span, :depth], own_ref[...], preferred_element_type=F32)
+    for j, piece in enumerate(pieces):
+
+        @pl.when(scalars[blocks + 1 + j] > 0)
+        def _(j=j, piece=piece):
+            acc_ref[...] += jnp.dot(
+                weighted_ref[:, (j + 1) * depth : (j + 2) * depth],
+                piece[...],
+                preferred_element_type=F32,
+            )
+
+    out_ref[...] = acc_ref[...].astype(BF16)
+
+
+def product(half, slots, valid, low_b, weighted, down, own, pieces, width, into=None):
     rows, rank = low_b.shape
-    tenants = gathered.shape[0]
+    tenants = down.shape[0]
     depth = own.shape[0]
     part = width // 2
     tile = min(512, part)
     tiles = part // tile
-    scalars = jnp.concatenate([slots, half[None]])
     blocks = slots.shape[0]
+    scalars = jnp.concatenate([slots, half[None], valid])
     whole = lambda i, s: (0, 0)
     column = lambda i, s: (0, s[blocks] * tiles + i)
     specs = [
         pl.BlockSpec((rows, rank), whole),
         pl.BlockSpec(weighted.shape, whole),
-        pl.BlockSpec((tenants, rank, tile), lambda i, s: (0, 0, s[blocks] * tiles + i)),
+        pl.BlockSpec((tenants, rank, tile), lambda i, s: (0, 0, i)),
         pl.BlockSpec((depth, tile), column),
     ] + [pl.BlockSpec((depth, tile), lambda i, s: (0, i)) for _ in pieces]
-    operands = [low_b, weighted, gathered, own, *pieces]
+    operands = [low_b, weighted, down, own, *pieces]
     aliases = {}
     if into is not None:
         specs.append(pl.BlockSpec(memory_space=pl.ANY))
         operands.append(into)
         aliases = {len(operands): 0}
     return pl.pallas_call(
-        functools.partial(product_kernel, len(pieces)),
+        functools.partial(product_kernel, len(pieces), blocks),
         out_shape=jax.ShapeDtypeStruct((rows, width), BF16),
         grid_spec=pltpu.PrefetchScalarGridSpec(
             num_scalar_prefetch=1,
             grid=(tiles,),
             in_specs=specs,
             out_specs=pl.BlockSpec((rows, tile), column),
+            scratch_shapes=[pltpu.VMEM((rows, tile), F32)],
         ),
         input_output_aliases=aliases,
         compiler_params=pltpu.CompilerParams(vmem_limit_bytes=VMEM_LIMIT),
@@ -111,12 +129,12 @@
     )(scalars, *operands)
 
 
-def project(slots, x, own_cols, gathered):
+def project(group, slots, x, own_cols, received, other):
     rows, width = x.shape
-    tenants, rank = gathered.shape[:2]
+    tenants, rank, part = other.shape
     slab = own_cols.shape[1]
     return pl.pallas_call(
-        project_kernel,
+        functools.partial(project_kernel, slots.shape[0]),
         out_shape=jax.ShapeDtypeStruct((rows, 2 * rank), BF16),
         grid_spec=pltpu.PrefetchScalarGridSpec(
             num_scalar_prefetch=1,
@@ -124,8 +142,9 @@
             in_specs=[
                 pl.BlockSpec((rows, width), lambda i, s: (0, 0)),
                 pl.BlockSpec((rows, slab), lambda i, s: (0, 0)),
-                pl.BlockSpec((tenants, rank, width), lambda i, s: (0, 0, 0)),
-                pl.BlockSpec((tenants, rank, slab), lambda i, s: (0, 0, width // slab)),
+                pl.BlockSpec((tenants, rank, part), lambda i, s: (0, 0, 0)),
+                pl.BlockSpec((tenants, rank, part), lambda i, s: (0, 0, 0)),
+                pl.BlockSpec((tenants, rank, slab), lambda i, s: (0, 0, part // slab)),
             ],
             out_specs=pl.BlockSpec((rows, 2 * rank), lambda i, s: (0, 0)),
         ),
@@ -136,7 +155,7 @@
             transcendentals=0,
         ),
         name="project",
-    )(slots, x, own_cols, gathered, gathered)
+    )(jnp.concatenate([slots, group[None]]), x, own_cols, received, other, received)
 
 
 def adapter_grads(slots, x, own_cols, here, there, tenants):
@@ -174,49 +193,64 @@
     )(slots, x, own_cols, here, there)
 
 
-def arrivals(n):
-    table = []
-    for i in range(n):
-        order = []
-        for k in range(1, n):
-            if i >= k:
-                order.append(("up", k))
-            if i + k < n:
-                order.append(("down", k))
-        table.append(order)
-    return table
-
-
-def pick(me, choices):
-    out = choices[0]
-    for i in range(1, len(choices)):
-        if any(choices[i] is c for c in choices[:i]) and choices[i] is choices[i - 1]:
-            continue
-        out = jnp.where(me >= i, choices[i], out)
-    return out
-
-
-def gather_line(piece, n):
-    me = lax.axis_index("seq")
-    got = {}
+def sum_kernel(got_ref, down_ref, up_ref):
+    width = down_ref.shape[2]
+    total = got_ref[0].astype(F32)
+    for k in range(1, got_ref.shape[0]):
+        total += got_ref[k].astype(F32)
+    down_ref[0] = total[:, :width]
+    up_ref[0] = total[:, width:]
+
+
+def owner_sums(got, width):
+    _, rank, both = got.shape
+    return pl.pallas_call(
+        sum_kernel,
+        out_shape=(
+            jax.ShapeDtypeStruct((1, rank, width), F32),
+            jax.ShapeDtypeStruct((1, rank, both - width), F32),
+        ),
+        compiler_params=pltpu.CompilerParams(vmem_limit_bytes=VMEM_LIMIT),
+        cost_estimate=pl.CostEstimate(
+            flops=got.size, bytes_accessed=2 * got.size, transcendentals=0
+        ),
+        name="owner_sums",
+    )(got)
+
+
+def gather_line(piece, n, groups):
+    me = lax.axis_index("seq").astype(jnp.int32)
+    mine, other, owner, valid = [], [], [], []
     up = down = piece
+
+    def keep(value, pairs, source):
+        targets = [b for _, b in pairs]
+        swaps = [
+            (g * n + t, (groups - 1 - g) * n + t) for g in range(groups) for t in targets
+        ]
+        mine.append(value)
+        other.append(lax.ppermute(value, ("groups", "seq"), swaps))
+        low, high = min(targets), max(targets)
+        has = (me >= low) & (me <= high)
+        if len(targets) < high - low + 1:
+            gap = [t for t in range(low, high) if t not in targets]
+            has = has & ((me < gap[0]) | (me > gap[-1]))
+        owner.append(jnp.where(has, source, 0))
+        valid.append(has.astype(jnp.int32))
+
     for k in range(1, n):
         up_pairs = [(i, i + 1) for i in range(k - 1, n - 1)]
         down_pairs = [(i + 1, i) for i in range(n - k)]
         if {a for a, _ in up_pairs} & {a for a, _ in down_pairs}:
             up = lax.ppermute(up, "seq", up_pairs)
             down = lax.ppermute(down, "seq", down_pairs)
+            keep(up, up_pairs, me - k)
+            keep(down, down_pairs, me + k)
         else:
             both = jnp.where(me >= k - 1, up, down)
             up = down = lax.ppermute(both, "seq", up_pairs + down_pairs)
-        got["up", k], got["down", k] = up, down
-    table = arrivals(n)
-    pieces, owners = [], []
-    for j in range(n - 1):
-        pieces.append(pick(me, [got[table[i][j]] for i in range(n)]))
-        source = [i - k if d == "up" else i + k for i in range(n) for d, k in [table[i][j]]]
-        owners.append(jnp.asarray(source, jnp.int32)[me])
-    return pieces, owners
+            keep(up, up_pairs + down_pairs, jnp.where(me >= k, me - k, me + k))
+    return mine, other, owner, jnp.stack(valid)
 
 
 def per_device(
@@ -232,19 +266,27 @@
 ):
     n, groups = sizes
     token_rows, width = layer_input.shape
-    owned, rank, _ = adapter_down.shape
+    rank = adapter_down.shape[1]
     slab = adapter_up.shape[2]
     tenants = tenant_slot.shape[0]
     depth = value_weight.shape[0]
     swap = lambda axis: functools.partial(lax.ppermute, axis_name=axis, perm=[(0, 1), (1, 0)])
 
-    adapters = jnp.concatenate([adapter_down, adapter_up], axis=2)
-    gathered = lax.all_gather(adapters, "seq", axis=0, tiled=True)
-
+    half = width // 2
     group = lax.axis_index("groups").astype(jnp.int32)
-    piece = lax.dynamic_slice_in_dim(value_weight, group * (width // 2), width // 2, 1)
-    mine, owners = gather_line(piece, n)
-    other = [swap("groups")(p) for p in mine]
+    down_half = lax.dynamic_slice_in_dim(adapter_down, group * half, half, 2)
+    adapters = jnp.concatenate([down_half, adapter_up], axis=2)
+    received = lax.all_to_all(
+        jnp.broadcast_to(adapters, (n,) + adapters.shape).reshape(tenants, rank, half + slab),
+        "seq",
+        split_axis=0,
+        concat_axis=0,
+        tiled=True,
+    )
+    swapped = swap("groups")(received[:, :, :half])
+
+    piece = lax.dynamic_slice_in_dim(value_weight, group * half, half, 1)
+    mine, other, owners, valid = gather_line(piece, n, groups)
 
     row_sign = (1 - 2 * forget_flag).astype(BF16)
     weighted = out_grad * row_sign[:, None]
@@ -259,7 +301,7 @@
         [lax.dynamic_slice_in_dim(weighted, o * depth, depth, 1) for o in [me, *owners]], axis=1
     )
 
-    part = project(slots, layer_input, own_cols, gathered)
+    part = project(group, slots, layer_input, own_cols, received, swapped)
     here = part
     axes = [a for a in ("pipe", "tensor")]
     for axis in axes[:-1]:
@@ -267,11 +309,14 @@
     there = line_sum_rest(here, axes[-1], sizes).astype(BF16)
     table, low_b = adapter_grads(slots, layer_input, own_cols, here, there, tenants)
     got = lax.all_to_all(table, "seq", split_axis=0, concat_axis=0, tiled=True)
-    total = jnp.sum(got.astype(F32).reshape(n, owned, rank, width + slab), axis=0)
-    down_grad, up_grad = total[:, :, :width], total[:, :, width:]
-
-    half = product(group, slots, low_b, ordered, gathered, value_weight, mine, width)
-    full = product(1 - group, slots, low_b, ordered, gathered, value_weight, other, width, half)
+    down_grad, up_grad = owner_sums(got, width)
+
+    first = product(
+        group, slots, valid, low_b, ordered, received, value_weight, mine, width
+    )
+    full = product(
+        1 - group, slots, valid, low_b, ordered, swapped, value_weight, other, width, first
+    )
     return full, down_grad, up_grad
 
 

time: 152 us -> 114 us (0.75)
  waiting for transfers between devices: 90 us -> 44.8 us
  starting transfers between devices: 19.1 us -> 36.4 us
  between operations: 16.3 us -> 0.93 us
  other arithmetic: 7.49 us -> 2.37 us
  local copies, waits for them, and re-layouts: 7.58 us -> 12.7 us
  Pallas kernels: 11.3 us -> 15.6 us
    ppermute x3 -> x6, waiting for transfers between devices: 26.3 us -> 10.8 us  [the longest x5 5.5 us: keep(): other.append(lax.ppermute(value, ('groups', 'seq'), swaps))]
    ppermute x2, waiting for transfers between devices: 12.3 us -> 0.01 us  [gather_line(): up = lax.ppermute(up, 'seq', up_pairs)]
    ppermute x1, waiting for transfers between devices: 30.8 us -> 18.7 us  [gather_line(): up = down = lax.ppermute(both, 'seq', up_pairs + down_pairs)]
    ppermute x2, waiting for transfers between devices: 14.5 us -> 2.61 us  [gather_line(): down = lax.ppermute(down, 'seq', down_pairs)]
    ppermute x3 -> x6, starting transfers between devices: 3.53 us -> 13.7 us  [the longest x5 12.2 us: keep(): other.append(lax.ppermute(value, ('groups', 'seq'), swaps))]
    all_to_all x0 -> x1, waiting for transfers between devices: none -> 9 us  [per_device(): lax.all_to_all(jnp.broadcast_to(adapters, (n,) + adapters.shape).reshape(...]
    unnamed x30 -> x27, local copies, waits for them, and re-layouts: 1.35 us -> 8.18 us
    all_to_all x0 -> x1, starting transfers between devices: none -> 6.45 us  [per_device(): lax.all_to_all(jnp.broadcast_to(adapters, (n,) + adapters.shape).reshape(...]
  transfers between devices with their start and end apart: 12 -> 15, of which waited for: 9 -> 6; matrix products, arithmetic and copies ran while one was open for 6% -> 9% of each run, Pallas kernels for 7% -> 13%
where the time goes in v2:
time: 114 us; the launch traced here: 113 us
  waiting for transfers between devices  44.8 us (39%)
  starting transfers between devices  36.4 us (32%)
  Pallas kernels  15.6 us (14%)
  local copies, waits for them, and re-layouts  12.7 us (11%)
  other arithmetic  2.37 us (2%)
    ppermute x1, waiting for transfers between devices, gather_line(): up = down = lax.ppermute(both, 'seq', up_pairs + down_pairs)  18.7 us
    ppermute x5, starting transfers between devices, keep(): other.append(lax.ppermute(value, ('groups', 'seq'), swaps))  12.2 us
    pallas_call x2, Pallas kernels, product(): pl.pallas_call(functools.partial(product_kernel, len(pieces), blocks), ou...  11.1 us
    all_to_all x1, waiting for transfers between devices, per_device(): lax.all_to_all(jnp.broadcast_to(adapters, (n,) + adapters.shape).reshape(...  9 us
    unnamed x27, local copies, waits for them, and re-layouts  8.18 us
    all_to_all x1, starting transfers between devices, per_device(): lax.all_to_all(jnp.broadcast_to(adapters, (n,) + adapters.shape).reshape(...  6.45 us
    ppermute x2, starting transfers between devices, gather_line(): up = lax.ppermute(up, 'seq', up_pairs)  6.2 us
    ppermute x5, waiting for transfers between devices, keep(): other.append(lax.ppermute(value, ('groups', 'seq'), swaps))  5.5 us
  transfers between devices with their start and end apart: 15, of which 6 were waited for; matrix products, arithmetic and copies ran while one was open for 9% of the time, Pallas kernels for 13%

profile of v2, /device:TPU:0, one launch (start us, length us, event | category | flops | bytes accessed | tf_op | source)
XLA Modules:
  0.0 112.9 jit_solution(12830790632498508883)
XLA Ops:
  0.6 0.0 copy-start
  0.7 0.9 copy-done
  1.6 0.0 copy-start.1
  1.6 0.9 maximum_bitcast_fusion
  2.5 0.9 reshape.12
  3.4 6.4 %all-to-all-start = ((bf16[4,64,1280]{2,1,0:T(8,128)(2,1)}), bf16[4,64,1280]{2,1,0:T(8,128)(2,1)S(1)}, u32[]{:S(2)}, u32[]{:S(2)}) async-start(bf16[4,64,1280]{2,1,0:T(8,128)(2,1)} %reshape.12), calls=%async_computation | async-start | bytes 1310720 | tf_op jit(solution)/shard_map/all_to_all | solution.py:279
  9.8 0.0 copy-done.1
  9.8 0.9 constant_dynamic-slice_fusion
  10.7 4.7 %collective-permute-start.3 = (bf16[256,1024]{1,0:T(8,128)(2,1)}, bf16[256,1024]{1,0:T(8,128)(2,1)}, u32[]{:S(2)}, u32[]{:S(2)}) collective-permute-start(bf16[256,1024]{1,0:T(8,128)(2,1)} %constant_dynamic-slice_fusion), channel_id=1, source_target_pairs={{0,4},{4,8},{8,12},{1,5},{5,9},{9,13},{2,6},{6,10},{10,14},{3,7},{... | collective-permute-start | bytes 1572872 | tf_op jit(solution)/shard_map/ppermute | solution.py:245
  15.4 1.3 %collective-permute-start.5 = (bf16[256,1024]{1,0:T(8,128)(2,1)}, bf16[256,1024]{1,0:T(8,128)(2,1)}, u32[]{:S(2)}, u32[]{:S(2)}) collective-permute-start(bf16[256,1024]{1,0:T(8,128)(2,1)} %constant_dynamic-slice_fusion), channel_id=1, source_target_pairs={{4,0},{8,4},{12,8},{5,1},{9,5},{13,9},{6,2},{10,6},{14,10},{7,3},{... | collective-permute-start | bytes 1572872 | tf_op jit(solution)/shard_map/ppermute | solution.py:246
  16.7 0.0 copy-done.8
  16.7 0.0 copy-done.7
  16.8 0.1 broadcast_multiply_fusion
  16.9 0.0 copy-start.6
  16.9 0.0 copy-start.9
  16.9 0.0 copy-start.10
  16.9 0.7 dynamic-slice_dynamic-update-slice_fusion.5
  17.6 0.8 dynamic-slice_dynamic-update-slice_fusion.4
  18.4 0.0 copy-done.6
  18.4 0.7 dynamic-slice_dynamic-update-slice_fusion.3
  19.2 9.0 %all-to-all-done.mine_ref.up_ref.refs_2_ = bf16[4,64,1280]{2,1,0:T(8,128)(2,1)S(1)} async-done(((bf16[4,64,1280]{2,1,0:T(8,128)(2,1)}), bf16[4,64,1280]{2,1,0:T(8,128)(2,1)S(1)}, u32[]{:S(2)}, u32[]{:S(2)}) %all-to-all-start) | async-done | bytes 655392 | tf_op jit(solution)/shard_map/all_to_all | solution.py:279
  28.2 0.9 slice.4
  29.0 1.5 %collective-permute-start = (bf16[4,64,1024]{2,1,0:T(8,128)(2,1)}, bf16[4,64,1024]{2,1,0:T(8,128)(2,1)}, u32[]{:S(2)}, u32[]{:S(2)}) collective-permute-start(bf16[4,64,1024]{2,1,0:T(8,128)(2,1)} %slice.4), channel_id=1, source_target_pairs={{0,16},{16,0},{1,17},{17,1},{2,18},{18,2},{3,19},{19,3},{4,20},{20... | collective-permute-start | bytes 1572872 | tf_op jit(solution)/shard_map/ppermute | solution.py:286
  30.5 0.0 copy-done.9
  30.6 0.2 select_reduce_fusion.slots
  30.8 0.1 pad_add_fusion.scalars
  30.9 1.6 %dynamic-slice_dynamic-update-slice_fusion.2 = bf16[384,1536]{1,0:T(8,128)(2,1)} fusion(bf16[384,1536]{1,0:T(8,128)(2,1)} %dynamic-slice_dynamic-update-slice_fusion.3, bf16[384,1024]{1,0:T(8,128)(2,1)} %copy-done.6, s32[]{:T(128)S(6)} %select_n.66), kind=kLoop, calls=%fused_computation.4 | loop fusion | bytes 393220
  32.5 1.6 %dynamic-slice_dynamic-update-slice_fusion.1 = bf16[384,1536]{1,0:T(8,128)(2,1)} fusion(bf16[384,1536]{1,0:T(8,128)(2,1)} %dynamic-slice_dynamic-update-slice_fusion.2, bf16[384,1024]{1,0:T(8,128)(2,1)} %copy-done.6, s32[]{:T(128)S(6)} %select_n.68), kind=kLoop, calls=%fused_computation.3 | loop fusion | bytes 393220
  34.1 1.8 %dynamic-slice_dynamic-update-slice_fusion = (bf16[384,1536]{1,0:T(8,128)(2,1)}, bf16[384,256]{1,0:T(8,128)(2,1)S(1)}) fusion(bf16[384,1536]{1,0:T(8,128)(2,1)} %dynamic-slice_dynamic-update-slice_fusion.1, bf16[384,1024]{1,0:T(8,128)(2,1)} %copy-done.6, s32[]{:T(128)S(6)} %select_n.71, s32[]{:T(128)S(6)} %select_n.58), kind=kLoop, calls=%fused_computation.2 | loop fusion | bytes 786440 | tf_op jit(solution)/shard_map/concatenate | solution.py:300
  35.9 5.3 %collective-permute-done.other_ref.refs_2_ = bf16[4,64,1024]{2,1,0:T(8,128)(2,1)} collective-permute-done((bf16[4,64,1024]{2,1,0:T(8,128)(2,1)}, bf16[4,64,1024]{2,1,0:T(8,128)(2,1)}, u32[]{:S(2)}, u32[]{:S(2)}) %collective-permute-start) | collective-permute-done | bytes 524320 | tf_op jit(solution)/shard_map/ppermute | solution.py:286
  41.2 2.3 %project.1 = bf16[384,128]{1,0:T(8,128)(2,1)S(1)} custom-call(s32[4]{0:T(128)S(1)} %pad_add_fusion.scalars, bf16[384,2048]{1,0:T(8,128)(2,1)S(1)} %copy-done.2, bf16[384,256]{1,0:T(8,128)(2,1)S(1)} %get-tuple-element.12.w_ref, bf16[4,64,1280]{2,1,0:T(8,128)(2,1)S(1)} %all-to-all-done.mine_ref.up_ref.refs_2_, ...), custom_call_target="tpu_custom_call" | custom-call | flops 113246208 | bytes 2949120 | tf_op jit(solution)/shard_map/project/pallas_call | solution.py:136
  43.5 0.1 collective-permute-start.1
  43.6 0.0 collective-permute-done.3.refs_4_
  43.6 1.5 %collective-permute-start.7 = (bf16[256,1024]{1,0:T(8,128)(2,1)}, bf16[256,1024]{1,0:T(8,128)(2,1)}, u32[]{:S(2)}, u32[]{:S(2)}) collective-permute-start(bf16[256,1024]{1,0:T(8,128)(2,1)} %collective-permute-done.3.refs_4_), channel_id=1, source_target_pairs={{4,8},{8,12},{5,9},{9,13},{6,10},{10,14},{7,11},{11,15},{20,24},{2... | collective-permute-start | bytes 1572872 | tf_op jit(solution)/shard_map/ppermute | solution.py:245
  45.0 0.0 collective-permute-done.5.refs_5_
  45.0 1.3 %collective-permute-start.9 = (bf16[256,1024]{1,0:T(8,128)(2,1)}, bf16[256,1024]{1,0:T(8,128)(2,1)}, u32[]{:S(2)}, u32[]{:S(2)}) collective-permute-start(bf16[256,1024]{1,0:T(8,128)(2,1)} %collective-permute-done.5.refs_5_), channel_id=1, source_target_pairs={{4,0},{8,4},{5,1},{9,5},{6,2},{10,6},{7,3},{11,7},{20,16},{24,20},... | collective-permute-start | bytes 1572872 | tf_op jit(solution)/shard_map/ppermute | solution.py:246
  46.3 0.0 collective-permute-done.1
  46.4 1.6 %collective-permute-start.2 = (bf16[384,128]{1,0:T(8,128)(2,1)S(1)}, bf16[384,128]{1,0:T(8,128)(2,1)S(1)}, u32[]{:S(2)}, u32[]{:S(2)}) collective-permute-start(bf16[384,128]{1,0:T(8,128)(2,1)S(1)} %add_convert_fusion.here_ref), channel_id=1, source_target_pairs={{0,2},{2,0},{1,3},{3,1},{4,6},{6,4},{5,7},{7,5},{8,10},{10,8},{9,1... | collective-permute-start | bytes 294920 | tf_op jit(solution)/shard_map/ppermute | solution.py:327
  47.9 3.7 %collective-permute-done.2.there_ref = bf16[384,128]{1,0:T(8,128)(2,1)S(1)} collective-permute-done((bf16[384,128]{1,0:T(8,128)(2,1)S(1)}, bf16[384,128]{1,0:T(8,128)(2,1)S(1)}, u32[]{:S(2)}, u32[]{:S(2)}) %collective-permute-start.2) | collective-permute-done | bytes 98336 | tf_op jit(solution)/shard_map/ppermute | solution.py:327
  51.6 1.3 %adapter_grads.1 = (bf16[4,64,2304]{2,1,0:T(8,128)(2,1)S(1)}, bf16[384,64]{1,0:T(8,128)(2,1)S(1)}) custom-call(s32[3]{0:T(128)S(1)} %select_reduce_fusion.slots, bf16[384,2048]{1,0:T(8,128)(2,1)S(1)} %copy-done.2, bf16[384,256]{1,0:T(8,128)(2,1)S(1)} %get-tuple-element.12.w_ref, bf16[384,128]{1,0:T(8,128)(2,1)S(1)} %add_convert_fusion.here_ref, ...), custom_call_target="tpu_custom_call" | custom-call | flops 113246208 | bytes 2949120 | tf_op jit(solution)/shard_map/adapter_grads/pallas_call | solution.py:165
  53.0 1.0 copy-done.3
  54.0 0.6 copy-done.4
  54.6 4.6 %all-to-all-start.1 = ((bf16[4,64,2304]{2,1,0:T(8,128)(2,1)}), bf16[4,64,2304]{2,1,0:T(8,128)(2,1)S(1)}, u32[]{:S(2)}, u32[]{:S(2)}) async-start(bf16[4,64,2304]{2,1,0:T(8,128)(2,1)} %copy-done.3), calls=%async_computation.1 | async-start | bytes 2359296 | tf_op jit(solution)/shard_map/all_to_all | solution.py:311
  59.3 0.0 collective-permute-done.7.refs_6_
  59.3 2.6 %collective-permute-done.9.refs_7_ = bf16[256,1024]{1,0:T(8,128)(2,1)} collective-permute-done((bf16[256,1024]{1,0:T(8,128)(2,1)}, bf16[256,1024]{1,0:T(8,128)(2,1)}, u32[]{:S(2)}, u32[]{:S(2)}) %collective-permute-start.9) | collective-permute-done | bytes 524320 | tf_op jit(solution)/shard_map/ppermute | solution.py:246
  61.9 1.1 broadcast_select_fusion
  63.0 1.3 %collective-permute-start.11 = (bf16[256,1024]{1,0:T(8,128)(2,1)S(1)}, bf16[256,1024]{1,0:T(8,128)(2,1)}, u32[]{:S(2)}, u32[]{:S(2)}) collective-permute-start(bf16[256,1024]{1,0:T(8,128)(2,1)S(1)} %broadcast_select_fusion), channel_id=1, source_target_pairs={{8,12},{4,0},{9,13},{5,1},{10,14},{6,2},{11,15},{7,3},{24,28},{20,... | collective-permute-start | bytes 1572872 | tf_op jit(solution)/shard_map/ppermute | solution.py:251
  64.3 1.5 %collective-permute-start.4 = (bf16[256,1024]{1,0:T(8,128)(2,1)}, bf16[256,1024]{1,0:T(8,128)(2,1)}, u32[]{:S(2)}, u32[]{:S(2)}) collective-permute-start(bf16[256,1024]{1,0:T(8,128)(2,1)} %collective-permute-done.3.refs_4_), channel_id=1, source_target_pairs={{4,20},{8,24},{12,28},{20,4},{24,8},{28,12},{5,21},{9,25},{13,29},... | collective-permute-start | bytes 1572872 | tf_op jit(solution)/shard_map/ppermute | solution.py:232
  65.7 3.4 %collective-permute-start.6 = (bf16[256,1024]{1,0:T(8,128)(2,1)}, bf16[256,1024]{1,0:T(8,128)(2,1)}, u32[]{:S(2)}, u32[]{:S(2)}) collective-permute-start(bf16[256,1024]{1,0:T(8,128)(2,1)} %collective-permute-done.5.refs_5_), channel_id=1, source_target_pairs={{0,16},{4,20},{8,24},{16,0},{20,4},{24,8},{1,17},{5,21},{9,25},{17... | collective-permute-start | bytes 1572872 | tf_op jit(solution)/shard_map/ppermute | solution.py:232
  69.2 2.4 %collective-permute-start.10 = (bf16[256,1024]{1,0:T(8,128)(2,1)}, bf16[256,1024]{1,0:T(8,128)(2,1)}, u32[]{:S(2)}, u32[]{:S(2)}) collective-permute-start(bf16[256,1024]{1,0:T(8,128)(2,1)} %collective-permute-done.9.refs_7_), channel_id=1, source_target_pairs={{0,16},{4,20},{16,0},{20,4},{1,17},{5,21},{17,1},{21,5},{2,18},{6,... | collective-permute-start | bytes 1572872 | tf_op jit(solution)/shard_map/ppermute | solution.py:232
  71.6 1.5 %collective-permute-start.8 = (bf16[256,1024]{1,0:T(8,128)(2,1)}, bf16[256,1024]{1,0:T(8,128)(2,1)}, u32[]{:S(2)}, u32[]{:S(2)}) collective-permute-start(bf16[256,1024]{1,0:T(8,128)(2,1)} %collective-permute-done.7.refs_6_), channel_id=1, source_target_pairs={{8,24},{12,28},{24,8},{28,12},{9,25},{13,29},{25,9},{29,13},{10,26... | collective-permute-start | bytes 1572872 | tf_op jit(solution)/shard_map/ppermute | solution.py:232
  73.1 18.7 %collective-permute-done.11.refs_8_ = bf16[256,1024]{1,0:T(8,128)(2,1)} collective-permute-done((bf16[256,1024]{1,0:T(8,128)(2,1)S(1)}, bf16[256,1024]{1,0:T(8,128)(2,1)}, u32[]{:S(2)}, u32[]{:S(2)}) %collective-permute-start.11) | collective-permute-done | bytes 524320 | tf_op jit(solution)/shard_map/ppermute | solution.py:251
  91.7 3.4 %collective-permute-start.12 = (bf16[256,1024]{1,0:T(8,128)(2,1)}, bf16[256,1024]{1,0:T(8,128)(2,1)}, u32[]{:S(2)}, u32[]{:S(2)}) collective-permute-start(bf16[256,1024]{1,0:T(8,128)(2,1)} %collective-permute-done.11.refs_8_), channel_id=1, source_target_pairs={{12,28},{0,16},{28,12},{16,0},{13,29},{1,17},{29,13},{17,1},{14,30... | collective-permute-start | bytes 1572872 | tf_op jit(solution)/shard_map/ppermute | solution.py:232
  95.2 0.1 concatenate.24.scalars
  95.3 0.1 concatenate.19.scalars
  95.3 5.5 %product.2.refs_9_ = bf16[384,2048]{1,0:T(8,128)(2,1)} custom-call(s32[9]{0:T(128)S(1)} %concatenate.24.scalars, bf16[384,64]{1,0:T(8,128)(2,1)S(1)} %copy-done.5, bf16[384,1536]{1,0:T(8,128)(2,1)} %get-tuple-element.11.refs_1_, bf16[4,64,1280]{2,1,0:T(8,128)(2,1)S(1)} %all-to-all-done.mine_ref.up_ref.refs_2_, bf16[256,2048]{1,0:T(8,128)(2,1)S(1)} %copy-done.1, ...), custom_call_target="tpu_custom_call" | custom-call | flops 1258291200 | bytes 4456448 | tf_op jit(solution)/shard_map/product/pallas_call | solution.py:111
  100.9 0.0 collective-permute-done.4.refs_4_
  100.9 0.0 collective-permute-done.6.refs_5_
  100.9 0.0 collective-permute-done.10.refs_7_
  100.9 0.0 collective-permute-done.8.refs_6_
  100.9 5.5 %collective-permute-done.12.refs_8_ = bf16[256,1024]{1,0:T(8,128)(2,1)} collective-permute-done((bf16[256,1024]{1,0:T(8,128)(2,1)}, bf16[256,1024]{1,0:T(8,128)(2,1)}, u32[]{:S(2)}, u32[]{:S(2)}) %collective-permute-start.12) | collective-permute-done | bytes 524320 | tf_op jit(solution)/shard_map/ppermute | solution.py:232
  106.4 5.5 %product.3 = bf16[384,2048]{1,0:T(8,128)(2,1)} custom-call(s32[9]{0:T(128)S(1)} %concatenate.19.scalars, bf16[384,64]{1,0:T(8,128)(2,1)S(1)} %copy-done.5, bf16[384,1536]{1,0:T(8,128)(2,1)} %get-tuple-element.11.refs_1_, bf16[4,64,1024]{2,1,0:T(8,128)(2,1)} %collective-permute-done.other_ref.refs_2_, ...), custom_call_target="tpu_custom_call", output_to_operand_aliasing={{}: (10, {})} | custom-call | flops 1258291200 | bytes 4456448 | tf_op jit(solution)/shard_map/product/pallas_call | solution.py:111
  111.9 0.0 all-to-all-done.1.got_ref
  111.9 0.9 owner_sums.1
  (12 shorter events, 0.1 us)
Async XLA Ops:
  0.6 1.0 copy-start
  1.6 8.2 %copy-start.1 = (bf16[256,2048]{1,0:T(8,128)(2,1)S(1)}, bf16[256,2048]{1,0:T(8,128)(2,1)}, u32[]{:S(2)}) copy-start(bf16[256,2048]{1,0:T(8,128)(2,1)} %refs_3_.3) | copy-start | bytes 3145732
  3.4 13.4 %copy-start.8 = (s32[384]{0:T(512)S(1)}, s32[384]{0:T(512)}, u32[]{:S(2)}) copy-start(s32[384]{0:T(512)} %param.15) | copy-start | bytes 4612
  3.4 13.4 %copy-start.7 = (bf16[384,1024]{1,0:T(8,128)(2,1)S(1)}, bf16[384,1024]{1,0:T(8,128)(2,1)}, u32[]{:S(2)}) copy-start(bf16[384,1024]{1,0:T(8,128)(2,1)} %param.9) | copy-start | bytes 2359300
  3.4 24.8 %all-to-all-start = ((bf16[4,64,1280]{2,1,0:T(8,128)(2,1)}), bf16[4,64,1280]{2,1,0:T(8,128)(2,1)S(1)}, u32[]{:S(2)}, u32[]{:S(2)}) async-start(bf16[4,64,1280]{2,1,0:T(8,128)(2,1)} %reshape.12), calls=%async_computation | async-start | bytes 1310720 | tf_op jit(solution)/shard_map/all_to_all | solution.py:279
  10.7 32.9 %collective-permute-start.3 = (bf16[256,1024]{1,0:T(8,128)(2,1)}, bf16[256,1024]{1,0:T(8,128)(2,1)}, u32[]{:S(2)}, u32[]{:S(2)}) collective-permute-start(bf16[256,1024]{1,0:T(8,128)(2,1)} %constant_dynamic-slice_fusion), channel_id=1, source_target_pairs={{0,4},{4,8},{8,12},{1,5},{5,9},{9,13},{2,6},{6,10},{10,14},{3,7},{... | collective-permute-start | bytes 1572872 | tf_op jit(solution)/shard_map/ppermute | solution.py:245
  15.4 29.6 %collective-permute-start.5 = (bf16[256,1024]{1,0:T(8,128)(2,1)}, bf16[256,1024]{1,0:T(8,128)(2,1)}, u32[]{:S(2)}, u32[]{:S(2)}) collective-permute-start(bf16[256,1024]{1,0:T(8,128)(2,1)} %constant_dynamic-slice_fusion), channel_id=1, source_target_pairs={{4,0},{8,4},{12,8},{5,1},{9,5},{13,9},{6,2},{10,6},{14,10},{7,3},{... | collective-permute-start | bytes 1572872 | tf_op jit(solution)/shard_map/ppermute | solution.py:246
  16.9 1.5 %copy-start.6 = (bf16[384,1024]{1,0:T(8,128)(2,1)}, bf16[384,1024]{1,0:T(8,128)(2,1)S(1)}, u32[]{:S(2)}) copy-start(bf16[384,1024]{1,0:T(8,128)(2,1)S(1)} %broadcast_multiply_fusion) | copy-start | bytes 2359300
  16.9 13.7 %copy-start.9 = (s32[4]{0:T(128)S(1)}, s32[4]{0:T(128)}, u32[]{:S(2)}) copy-start(s32[4]{0:T(128)} %param.14) | copy-start | bytes 52
  16.9 13.6 %copy-start.10 = (s32[3,1]{0,1:T(1,128)S(1)}, s32[3,1]{0,1:T(1,128)}, u32[]{:S(2)}) copy-start(s32[3,1]{0,1:T(1,128)} %param.13) | copy-start | bytes 40
  19.2 22.0 %copy-start.2 = (bf16[384,2048]{1,0:T(8,128)(2,1)S(1)}, bf16[384,2048]{1,0:T(8,128)(2,1)}, u32[]{:S(2)}) copy-start(bf16[384,2048]{1,0:T(8,128)(2,1)} %x_ref.3) | copy-start | bytes 4718596
  29.0 12.2 %collective-permute-start = (bf16[4,64,1024]{2,1,0:T(8,128)(2,1)}, bf16[4,64,1024]{2,1,0:T(8,128)(2,1)}, u32[]{:S(2)}, u32[]{:S(2)}) collective-permute-start(bf16[4,64,1024]{2,1,0:T(8,128)(2,1)} %slice.4), channel_id=1, source_target_pairs={{0,16},{16,0},{1,17},{17,1},{2,18},{18,2},{3,19},{19,3},{4,20},{20... | collective-permute-start | bytes 1572872 | tf_op jit(solution)/shard_map/ppermute | solution.py:286
  43.5 2.9 %collective-permute-start.1 = (bf16[384,128]{1,0:T(8,128)(2,1)S(1)}, bf16[384,128]{1,0:T(8,128)(2,1)S(1)}, u32[]{:S(2)}, u32[]{:S(2)}) collective-permute-start(bf16[384,128]{1,0:T(8,128)(2,1)S(1)} %project.1), channel_id=1, source_target_pairs={{0,1},{1,0},{2,3},{3,2},{4,5},{5,4},{6,7},{7,6},{8,9},{9,8},{10,11... | collective-permute-start | bytes 294920 | tf_op jit(solution)/shard_map/ppermute | solution.py:327
  43.6 15.7 %collective-permute-start.7 = (bf16[256,1024]{1,0:T(8,128)(2,1)}, bf16[256,1024]{1,0:T(8,128)(2,1)}, u32[]{:S(2)}, u32[]{:S(2)}) collective-permute-start(bf16[256,1024]{1,0:T(8,128)(2,1)} %collective-permute-done.3.refs_4_), channel_id=1, source_target_pairs={{4,8},{8,12},{5,9},{9,13},{6,10},{10,14},{7,11},{11,15},{20,24},{2... | collective-permute-start | bytes 1572872 | tf_op jit(solution)/shard_map/ppermute | solution.py:245
  45.0 16.8 %collective-permute-start.9 = (bf16[256,1024]{1,0:T(8,128)(2,1)}, bf16[256,1024]{1,0:T(8,128)(2,1)}, u32[]{:S(2)}, u32[]{:S(2)}) collective-permute-start(bf16[256,1024]{1,0:T(8,128)(2,1)} %collective-permute-done.5.refs_5_), channel_id=1, source_target_pairs={{4,0},{8,4},{5,1},{9,5},{6,2},{10,6},{7,3},{11,7},{20,16},{24,20},... | collective-permute-start | bytes 1572872 | tf_op jit(solution)/shard_map/ppermute | solution.py:246
  46.4 5.2 %collective-permute-start.2 = (bf16[384,128]{1,0:T(8,128)(2,1)S(1)}, bf16[384,128]{1,0:T(8,128)(2,1)S(1)}, u32[]{:S(2)}, u32[]{:S(2)}) collective-permute-start(bf16[384,128]{1,0:T(8,128)(2,1)S(1)} %add_convert_fusion.here_ref), channel_id=1, source_target_pairs={{0,2},{2,0},{1,3},{3,1},{4,6},{6,4},{5,7},{7,5},{8,10},{10,8},{9,1... | collective-permute-start | bytes 294920 | tf_op jit(solution)/shard_map/ppermute | solution.py:327
  53.0 1.0 copy-start.3
  54.0 0.6 copy-start.4
  54.6 57.3 %all-to-all-start.1 = ((bf16[4,64,2304]{2,1,0:T(8,128)(2,1)}), bf16[4,64,2304]{2,1,0:T(8,128)(2,1)S(1)}, u32[]{:S(2)}, u32[]{:S(2)}) async-start(bf16[4,64,2304]{2,1,0:T(8,128)(2,1)} %copy-done.3), calls=%async_computation.1 | async-start | bytes 2359296 | tf_op jit(solution)/shard_map/all_to_all | solution.py:311
  59.3 36.1 %copy-start.5 = (bf16[384,64]{1,0:T(8,128)(2,1)S(1)}, bf16[384,64]{1,0:T(8,128)(2,1)}, u32[]{:S(2)}) copy-start(bf16[384,64]{1,0:T(8,128)(2,1)} %copy-done.4) | copy-start | bytes 147460
  63.0 28.8 %collective-permute-start.11 = (bf16[256,1024]{1,0:T(8,128)(2,1)S(1)}, bf16[256,1024]{1,0:T(8,128)(2,1)}, u32[]{:S(2)}, u32[]{:S(2)}) collective-permute-start(bf16[256,1024]{1,0:T(8,128)(2,1)S(1)} %broadcast_select_fusion), channel_id=1, source_target_pairs={{8,12},{4,0},{9,13},{5,1},{10,14},{6,2},{11,15},{7,3},{24,28},{20,... | collective-permute-start | bytes 1572872 | tf_op jit(solution)/shard_map/ppermute | solution.py:251
  64.3 36.6 %collective-permute-start.4 = (bf16[256,1024]{1,0:T(8,128)(2,1)}, bf16[256,1024]{1,0:T(8,128)(2,1)}, u32[]{:S(2)}, u32[]{:S(2)}) collective-permute-start(bf16[256,1024]{1,0:T(8,128)(2,1)} %collective-permute-done.3.refs_4_), channel_id=1, source_target_pairs={{4,20},{8,24},{12,28},{20,4},{24,8},{28,12},{5,21},{9,25},{13,29},... | collective-permute-start | bytes 1572872 | tf_op jit(solution)/shard_map/ppermute | solution.py:232
  65.7 35.1 %collective-permute-start.6 = (bf16[256,1024]{1,0:T(8,128)(2,1)}, bf16[256,1024]{1,0:T(8,128)(2,1)}, u32[]{:S(2)}, u32[]{:S(2)}) collective-permute-start(bf16[256,1024]{1,0:T(8,128)(2,1)} %collective-permute-done.5.refs_5_), channel_id=1, source_target_pairs={{0,16},{4,20},{8,24},{16,0},{20,4},{24,8},{1,17},{5,21},{9,25},{17... | collective-permute-start | bytes 1572872 | tf_op jit(solution)/shard_map/ppermute | solution.py:232
  69.2 31.7 %collective-permute-start.10 = (bf16[256,1024]{1,0:T(8,128)(2,1)}, bf16[256,1024]{1,0:T(8,128)(2,1)}, u32[]{:S(2)}, u32[]{:S(2)}) collective-permute-start(bf16[256,1024]{1,0:T(8,128)(2,1)} %collective-permute-done.9.refs_7_), channel_id=1, source_target_pairs={{0,16},{4,20},{16,0},{20,4},{1,17},{5,21},{17,1},{21,5},{2,18},{6,... | collective-permute-start | bytes 1572872 | tf_op jit(solution)/shard_map/ppermute | solution.py:232
  71.6 29.3 %collective-permute-start.8 = (bf16[256,1024]{1,0:T(8,128)(2,1)}, bf16[256,1024]{1,0:T(8,128)(2,1)}, u32[]{:S(2)}, u32[]{:S(2)}) collective-permute-start(bf16[256,1024]{1,0:T(8,128)(2,1)} %collective-permute-done.7.refs_6_), channel_id=1, source_target_pairs={{8,24},{12,28},{24,8},{28,12},{9,25},{13,29},{25,9},{29,13},{10,26... | collective-permute-start | bytes 1572872 | tf_op jit(solution)/shard_map/ppermute | solution.py:232
  91.7 14.7 %collective-permute-start.12 = (bf16[256,1024]{1,0:T(8,128)(2,1)}, bf16[256,1024]{1,0:T(8,128)(2,1)}, u32[]{:S(2)}, u32[]{:S(2)}) collective-permute-start(bf16[256,1024]{1,0:T(8,128)(2,1)} %collective-permute-done.11.refs_8_), channel_id=1, source_target_pairs={{12,28},{0,16},{28,12},{16,0},{13,29},{1,17},{29,13},{17,1},{14,30... | collective-permute-start | bytes 1572872 | tf_op jit(solution)/shard_map/ppermute | solution.py:232

commit v3 on v2

--- a/solution.py
+++ b/solution.py
@@ -40,8 +40,7 @@
         run(other_ref, mine_ref)
 
 
-def grads_kernel(slots, x_ref, w_ref, here_ref, there_ref, table_ref, low_ref, acc_ref):
-    blocks = slots.shape[0]
+def grads_kernel(blocks, slots, x_ref, w_ref, here_ref, there_ref, table_ref, low_ref, acc_ref):
     rows, width = x_ref.shape[0] // blocks, x_ref.shape[1]
     rank = low_ref.shape[1]
     contract = (((0,), (0,)), ((), ()))
@@ -62,86 +61,146 @@
     table_ref[...] = acc_ref[...].astype(BF16)
 
 
-def product_kernel(count, blocks, scalars, *refs):
-    low_ref, weighted_ref, down_ref, own_ref = refs[:4]
-    pieces, out_ref, acc_ref = refs[4 : 4 + count], refs[-2], refs[-1]
-    rows, depth = low_ref.shape[0], own_ref.shape[0]
-    block_rows = rows // blocks
-    for b in range(blocks):
-        span = slice(b * block_rows, (b + 1) * block_rows)
-        acc_ref[span, :] = jnp.dot(
-            low_ref[span, :], down_ref[scalars[b]], preferred_element_type=F32
-        ) + jnp.dot(weighted_ref[span, :depth], own_ref[...], preferred_element_type=F32)
+def product_kernel(plan, scalars, *refs):
+    count, blocks, opens, aligned = plan
+    refs = list(refs)
+    weighted_ref = refs.pop(0)
+    acc_ref, out_ref = refs.pop(), refs.pop()
+    if opens:
+        low_ref, down_ref, own_ref = refs[:3]
+        pieces = refs[3 : 3 + count]
+        depth = own_ref.shape[0]
+        block_rows = low_ref.shape[0] // blocks
+        own = take_columns(weighted_ref, scalars[blocks + 1], 0, depth, aligned)
+        acc_ref[...] = jnp.dot(own, own_ref[...], preferred_element_type=F32)
+        for b in range(blocks):
+            span = slice(b * block_rows, (b + 1) * block_rows)
+            acc_ref[span, :] += jnp.dot(
+                low_ref[span, :], down_ref[scalars[b]], preferred_element_type=F32
+            )
+    else:
+        pieces = refs[1 : 1 + count]
+        depth = pieces[0].shape[0]
+        acc_ref[...] = refs[0][...]
     for j, piece in enumerate(pieces):
-
-        @pl.when(scalars[blocks + 1 + j] > 0)
-        def _(j=j, piece=piece):
-            acc_ref[...] += jnp.dot(
-                weighted_ref[:, (j + 1) * depth : (j + 2) * depth],
-                piece[...],
-                preferred_element_type=F32,
-            )
-
-    out_ref[...] = acc_ref[...].astype(BF16)
-
-
-def product(half, slots, valid, low_b, weighted, down, own, pieces, width, into=None):
-    rows, rank = low_b.shape
-    tenants = down.shape[0]
-    depth = own.shape[0]
+        owner = scalars[blocks + 2 + j]
+
+        @pl.when(owner >= 0)
+        def _(j=j, piece=piece, owner=owner):
+            columns = take_columns(weighted_ref, owner, j + 1, depth, aligned)
+            acc_ref[...] += jnp.dot(columns, piece[...], preferred_element_type=F32)
+
+    out_ref[...] = acc_ref[...].astype(out_ref.dtype)
+
+
+def take_columns(ref, owner, position, depth, aligned):
+    if aligned:
+        return ref[:, pl.ds(pl.multiple_of(owner * depth, 128), depth)]
+    return ref[:, position * depth : (position + 1) * depth]
+
+
+def product(half, slots, me, owners, weighted, pieces, start, width, into=None, partial=False):
+    opens = isinstance(start, tuple)
+    rows = weighted.shape[0]
+    depth = pieces[0].shape[0]
     part = width // 2
     tile = min(512, part)
     tiles = part // tile
     blocks = slots.shape[0]
-    scalars = jnp.concatenate([slots, half[None], valid])
+    aligned = depth % 128 == 0
+    if not aligned:
+        begins = [me] + [jnp.maximum(o, 0) for o in owners]
+        weighted = jnp.concatenate(
+            [lax.dynamic_slice_in_dim(weighted, o * depth, depth, 1) for o in begins], axis=1
+        )
+    scalars = jnp.stack([*slots, half, me, *owners])
     whole = lambda i, s: (0, 0)
+    here = lambda i, s: (0, i)
     column = lambda i, s: (0, s[blocks] * tiles + i)
-    specs = [
-        pl.BlockSpec((rows, rank), whole),
-        pl.BlockSpec(weighted.shape, whole),
-        pl.BlockSpec((tenants, rank, tile), lambda i, s: (0, 0, i)),
-        pl.BlockSpec((depth, tile), column),
-    ] + [pl.BlockSpec((depth, tile), lambda i, s: (0, i)) for _ in pieces]
-    operands = [low_b, weighted, down, own, *pieces]
+    specs = [pl.BlockSpec(weighted.shape, whole)]
+    operands = [weighted]
+    if opens:
+        low_b, down, own = start
+        specs += [
+            pl.BlockSpec(low_b.shape, whole),
+            pl.BlockSpec((*down.shape[:2], tile), lambda i, s: (0, 0, i)),
+            pl.BlockSpec((depth, tile), column),
+        ]
+        operands += [low_b, down, own]
+    else:
+        specs.append(pl.BlockSpec((rows, tile), here))
+        operands.append(start)
+    specs += [pl.BlockSpec((depth, tile), here) for _ in pieces]
+    operands += pieces
     aliases = {}
     if into is not None:
         specs.append(pl.BlockSpec(memory_space=pl.ANY))
         operands.append(into)
         aliases = {len(operands): 0}
+    shape = jax.ShapeDtypeStruct((rows, part), F32) if partial else jax.ShapeDtypeStruct((rows, width), BF16)
     return pl.pallas_call(
-        functools.partial(product_kernel, len(pieces), blocks),
-        out_shape=jax.ShapeDtypeStruct((rows, width), BF16),
+        functools.partial(product_kernel, (len(pieces), blocks, opens, aligned)),
+        out_shape=shape,
         grid_spec=pltpu.PrefetchScalarGridSpec(
             num_scalar_prefetch=1,
             grid=(tiles,),
             in_specs=specs,
-            out_specs=pl.BlockSpec((rows, tile), column),
+            out_specs=pl.BlockSpec((rows, tile), here if partial else column),
             scratch_shapes=[pltpu.VMEM((rows, tile), F32)],
         ),
         input_output_aliases=aliases,
         compiler_params=pltpu.CompilerParams(vmem_limit_bytes=VMEM_LIMIT),
         cost_estimate=pl.CostEstimate(
-            flops=2 * rows * part * (weighted.shape[1] + rank),
-            bytes_accessed=2 * (part * (weighted.shape[1] + tenants * rank + rows)),
+            flops=2 * rows * part * depth * (len(pieces) + 1),
+            bytes_accessed=2 * (part * (depth * (len(pieces) + 1) + rows)),
             transcendentals=0,
         ),
         name="product",
     )(scalars, *operands)
 
 
-def project(group, slots, x, own_cols, received, other):
+def payload_kernel(scalars, down_ref, up_ref, out_ref):
+    part = down_ref.shape[2]
+    for k in range(out_ref.shape[0] // down_ref.shape[0]):
+        span = slice(k * down_ref.shape[0], (k + 1) * down_ref.shape[0])
+        out_ref[span, :, :part] = down_ref[...]
+        out_ref[span, :, part:] = up_ref[...]
+
+
+def payload(group, down, up, n):
+    owned, rank, width = down.shape
+    slab, part = up.shape[2], width // 2
+    return pl.pallas_call(
+        payload_kernel,
+        out_shape=jax.ShapeDtypeStruct((n * owned, rank, part + slab), BF16),
+        grid_spec=pltpu.PrefetchScalarGridSpec(
+            num_scalar_prefetch=1,
+            grid=(1,),
+            in_specs=[
+                pl.BlockSpec((owned, rank, part), lambda i, s: (0, 0, s[0])),
+                pl.BlockSpec((owned, rank, slab), lambda i, s: (0, 0, 0)),
+            ],
+            out_specs=pl.BlockSpec((n * owned, rank, part + slab), lambda i, s: (0, 0, 0)),
+        ),
+        compiler_params=pltpu.CompilerParams(vmem_limit_bytes=VMEM_LIMIT),
+        name="payload",
+    )(group[None], down, up)
+
+
+def project(group, slab_index, slots, x, weighted, received, other):
     rows, width = x.shape
     tenants, rank, part = other.shape
-    slab = own_cols.shape[1]
+    slab = received.shape[2] - part
+    blocks = slots.shape[0]
     return pl.pallas_call(
-        functools.partial(project_kernel, slots.shape[0]),
+        functools.partial(project_kernel, blocks),
         out_shape=jax.ShapeDtypeStruct((rows, 2 * rank), BF16),
         grid_spec=pltpu.PrefetchScalarGridSpec(
             num_scalar_prefetch=1,
             grid=(1,),
             in_specs=[
                 pl.BlockSpec((rows, width), lambda i, s: (0, 0)),
-                pl.BlockSpec((rows, slab), lambda i, s: (0, 0)),
+                pl.BlockSpec((rows, slab), lambda i, s: (0, s[blocks + 1])),
                 pl.BlockSpec((tenants, rank, part), lambda i, s: (0, 0, 0)),
                 pl.BlockSpec((tenants, rank, part), lambda i, s: (0, 0, 0)),
                 pl.BlockSpec((tenants, rank, slab), lambda i, s: (0, 0, part // slab)),
@@ -155,15 +214,15 @@
             transcendentals=0,
         ),
         name="project",
-    )(jnp.concatenate([slots, group[None]]), x, own_cols, received, other, received)
-
-
-def adapter_grads(slots, x, own_cols, here, there, tenants):
+    )(jnp.stack([*slots, group, slab_index]), x, weighted, received, other, received)
+
+
+def adapter_grads(slab_index, slots, x, weighted, here, there, tenants, slab):
     rows, width = x.shape
     rank = here.shape[1] // 2
-    slab = own_cols.shape[1]
+    blocks = slots.shape[0]
     return pl.pallas_call(
-        grads_kernel,
+        functools.partial(grads_kernel, blocks),
         out_shape=(
             jax.ShapeDtypeStruct((tenants, rank, width + slab), BF16),
             jax.ShapeDtypeStruct((rows, rank), BF16),
@@ -173,7 +232,7 @@
             grid=(1,),
             in_specs=[
                 pl.BlockSpec((rows, width), lambda i, s: (0, 0)),
-                pl.BlockSpec((rows, slab), lambda i, s: (0, 0)),
+                pl.BlockSpec((rows, slab), lambda i, s: (0, s[blocks])),
                 pl.BlockSpec((rows, 2 * rank), lambda i, s: (0, 0)),
                 pl.BlockSpec((rows, 2 * rank), lambda i, s: (0, 0)),
             ],
@@ -190,7 +249,7 @@
             transcendentals=0,
         ),
         name="adapter_grads",
-    )(slots, x, own_cols, here, there)
+    )(jnp.stack([*slots, slab_index]), x, weighted, here, there)
 
 
 def sum_kernel(got_ref, down_ref, up_ref):
@@ -220,7 +279,7 @@
 
 def gather_line(piece, n, groups):
     me = lax.axis_index("seq").astype(jnp.int32)
-    mine, other, owner, valid = [], [], [], []
+    mine, other, owner = [], [], []
     up = down = piece
 
     def keep(value, pairs, source):
@@ -229,28 +288,30 @@
             (g * n + t, (groups - 1 - g) * n + t) for g in range(groups) for t in targets
         ]
         mine.append(value)
-        other.append(lax.ppermute(value, ("groups", "seq"), swaps))
+        with jax.named_scope("swap_w"):
+            other.append(lax.ppermute(value, ("groups", "seq"), swaps))
         low, high = min(targets), max(targets)
         has = (me >= low) & (me <= high)
         if len(targets) < high - low + 1:
             gap = [t for t in range(low, high) if t not in targets]
             has = has & ((me < gap[0]) | (me > gap[-1]))
-        owner.append(jnp.where(has, source, 0))
-        valid.append(has.astype(jnp.int32))
+        owner.append(jnp.where(has, source, -1))
 
     for k in range(1, n):
         up_pairs = [(i, i + 1) for i in range(k - 1, n - 1)]
         down_pairs = [(i + 1, i) for i in range(n - k)]
         if {a for a, _ in up_pairs} & {a for a, _ in down_pairs}:
-            up = lax.ppermute(up, "seq", up_pairs)
-            down = lax.ppermute(down, "seq", down_pairs)
+            with jax.named_scope(f"line_{k}"):
+                up = lax.ppermute(up, "seq", up_pairs)
+                down = lax.ppermute(down, "seq", down_pairs)
             keep(up, up_pairs, me - k)
             keep(down, down_pairs, me + k)
         else:
             both = jnp.where(me >= k - 1, up, down)
-            up = down = lax.ppermute(both, "seq", up_pairs + down_pairs)
+            with jax.named_scope(f"line_{k}"):
+                up = down = lax.ppermute(both, "seq", up_pairs + down_pairs)
             keep(up, up_pairs + down_pairs, jnp.where(me >= k, me - k, me + k))
-    return mine, other, owner, jnp.stack(valid)
+    return mine, other, owner
 
 
 def per_device(
@@ -274,19 +335,14 @@
 
     half = width // 2
     group = lax.axis_index("groups").astype(jnp.int32)
-    down_half = lax.dynamic_slice_in_dim(adapter_down, group * half, half, 2)
-    adapters = jnp.concatenate([down_half, adapter_up], axis=2)
     received = lax.all_to_all(
-        jnp.broadcast_to(adapters, (n,) + adapters.shape).reshape(tenants, rank, half + slab),
-        "seq",
-        split_axis=0,
-        concat_axis=0,
-        tiled=True,
+        payload(group, adapter_down, adapter_up, n), "seq", split_axis=0, concat_axis=0, tiled=True
     )
-    swapped = swap("groups")(received[:, :, :half])
+    with jax.named_scope("swap_a"):
+        swapped = swap("groups")(received[:, :, :half])
 
     piece = lax.dynamic_slice_in_dim(value_weight, group * half, half, 1)
-    mine, other, owners, valid = gather_line(piece, n, groups)
+    mine, other, owners = gather_line(piece, n, groups)
 
     row_sign = (1 - 2 * forget_flag).astype(BF16)
     weighted = out_grad * row_sign[:, None]
@@ -294,29 +350,36 @@
     slots = jnp.sum(
         jnp.where(block_tenant == tenant_ids[None, :], tenant_slot[None, :], 0), axis=1
     ).astype(jnp.int32)
-    slab_index = lax.axis_index(("tensor", "pipe"))
-    own_cols = lax.dynamic_slice_in_dim(weighted, slab_index * slab, slab, 1)
-    me = lax.axis_index("seq")
-    ordered = jnp.concatenate(
-        [lax.dynamic_slice_in_dim(weighted, o * depth, depth, 1) for o in [me, *owners]], axis=1
-    )
-
-    part = project(group, slots, layer_input, own_cols, received, swapped)
+    slab_index = lax.axis_index(("tensor", "pipe")).astype(jnp.int32)
+    me = lax.axis_index("seq").astype(jnp.int32)
+
+    part = project(group, slab_index, slots, layer_input, weighted, received, swapped)
     here = part
     axes = [a for a in ("pipe", "tensor")]
     for axis in axes[:-1]:
         here = (here.astype(F32) + line_sum_rest(here, axis, sizes)).astype(BF16)
     there = line_sum_rest(here, axes[-1], sizes).astype(BF16)
-    table, low_b = adapter_grads(slots, layer_input, own_cols, here, there, tenants)
+    there, _ = lax.optimization_barrier((there, (mine[:4], other[:1])))
+    table, low_b = adapter_grads(
+        slab_index, slots, layer_input, weighted, here, there, tenants, slab
+    )
     got = lax.all_to_all(table, "seq", split_axis=0, concat_axis=0, tiled=True)
     down_grad, up_grad = owner_sums(got, width)
 
-    first = product(
-        group, slots, valid, low_b, ordered, received, value_weight, mine, width
+    opening = lambda down: (low_b, down, value_weight)
+    first = product(group, slots, me, owners, weighted, mine, opening(received), width)
+    rest = product(
+        1 - group,
+        slots,
+        me,
+        owners[:-1],
+        weighted,
+        other[:-1],
+        opening(swapped),
+        width,
+        partial=True,
     )
-    full = product(
-        1 - group, slots, valid, low_b, ordered, swapped, value_weight, other, width, first
-    )
+    full = product(1 - group, slots, me, owners[-1:], weighted, other[-1:], rest, width, first)
     return full, down_grad, up_grad
 
 

time: 114 us -> 116 us (1.018)
  waiting for transfers between devices: 44.8 us -> 51 us
  local copies, waits for them, and re-layouts: 12.7 us -> 9.47 us
  starting transfers between devices: 36.4 us -> 33.6 us
  Pallas kernels: 15.6 us -> 17.5 us
    ppermute x2, waiting for transfers between devices: 2.61 us -> 11.2 us  [gather_line(): down = lax.ppermute(down, 'seq', down_pairs)]
    ppermute x5, waiting for transfers between devices: 5.5 us -> 0.68 us  [keep(): other.append(lax.ppermute(value, ('groups', 'seq'), swaps))]
    all_to_all x1, waiting for transfers between devices: 9 us -> 11.5 us  [per_device(): lax.all_to_all(payload(group, adapter_down, adapter_up, n), 'seq', split_...]
    ppermute x2, waiting for transfers between devices: 3.69 us -> 1.29 us  [line_sum_rest(): lax.ppermute(value, axis, [(i, (i + d) % size) for i in range(size)])]
    ppermute x1, waiting for transfers between devices: 18.7 us -> 20.8 us  [gather_line(): up = down = lax.ppermute(both, 'seq', up_pairs + down_pairs)]
    concatenate x3 -> x0, local copies, waits for them, and re-layouts: 1.94 us -> none  [the longest x1 1.77 us: per_device(): jnp.concatenate([lax.dynamic_slice_in_dim(weighted, o * depth, depth, 1)...]
    ppermute x5, starting transfers between devices: 12.2 us -> 10.4 us  [keep(): other.append(lax.ppermute(value, ('groups', 'seq'), swaps))]
    pallas_call x1, Pallas kernels: 0.92 us -> 2.19 us  [owner_sums(): pl.pallas_call(sum_kernel, out_shape=(jax.ShapeDtypeStruct((1, rank, widt...]
  transfers between devices with their start and end apart: 15 -> 15, of which waited for: 6 -> 7; matrix products, arithmetic and copies ran while one was open for 9% -> 4% of each run, Pallas kernels for 13% -> 11%
where the time goes in v3:
time: 116 us; the launch traced here: 115 us
  waiting for transfers between devices  51 us (44%)
  starting transfers between devices  33.6 us (29%)
  Pallas kernels  17.5 us (15%)
  local copies, waits for them, and re-layouts  9.47 us (8%)
  other arithmetic  2.8 us (2%)
    ppermute x1, waiting for transfers between devices, gather_line(): up = down = lax.ppermute(both, 'seq', up_pairs + down_pairs)  20.8 us
    pallas_call x3, Pallas kernels, product(): pl.pallas_call(functools.partial(product_kernel, (len(pieces), blocks, op...  11.8 us
    all_to_all x1, waiting for transfers between devices, per_device(): lax.all_to_all(payload(group, adapter_down, adapter_up, n), 'seq', split_...  11.5 us
    ppermute x2, waiting for transfers between devices, gather_line(): down = lax.ppermute(down, 'seq', down_pairs)  11.2 us
    ppermute x5, starting transfers between devices, keep(): other.append(lax.ppermute(value, ('groups', 'seq'), swaps))  10.4 us
    unnamed x24, local copies, waits for them, and re-layouts  7.59 us
    all_to_all x1, starting transfers between devices, per_device(): lax.all_to_all(payload(group, adapter_down, adapter_up, n), 'seq', split_...  6.45 us
    ppermute x1, waiting for transfers between devices, per_device(): swapped = swap('groups')(received[:, :, :half])  5.66 us
  transfers between devices with their start and end apart: 15, of which 7 were waited for; matrix products, arithmetic and copies ran while one was open for 4% of the time, Pallas kernels for 11%

profile of v3, /device:TPU:0, one launch (start us, length us, event | category | flops | bytes accessed | tf_op | source)
XLA Modules:
  0.0 115.3 jit_solution(9763081467386674612)
XLA Ops:
  0.6 0.0 copy-start
  0.6 0.0 copy-start.7
  0.7 1.0 copy-done.7
  1.7 0.0 copy-start.8
  1.7 0.8 copy-done.8
  2.4 0.9 payload.1
  3.3 6.4 %all-to-all-start = ((bf16[4,64,1280]{2,1,0:T(8,128)(2,1)}), bf16[4,64,1280]{2,1,0:T(8,128)(2,1)S(1)}, u32[]{:S(2)}, u32[]{:S(2)}) async-start(bf16[4,64,1280]{2,1,0:T(8,128)(2,1)} %payload.1), calls=%async_computation | async-start | bytes 1310720 | tf_op jit(solution)/shard_map/all_to_all | solution.py:338
  9.8 0.0 copy-done
  9.8 0.9 constant_dynamic-slice_fusion
  10.6 4.7 %collective-permute-start.3 = (bf16[256,1024]{1,0:T(8,128)(2,1)}, bf16[256,1024]{1,0:T(8,128)(2,1)}, u32[]{:S(2)}, u32[]{:S(2)}) collective-permute-start(bf16[256,1024]{1,0:T(8,128)(2,1)} %constant_dynamic-slice_fusion), channel_id=1, source_target_pairs={{0,4},{4,8},{8,12},{1,5},{5,9},{9,13},{2,6},{6,10},{10,14},{3,7},{... | collective-permute-start | bytes 1572872 | tf_op jit(solution)/shard_map/line_1/ppermute | solution.py:305
  15.4 1.3 %collective-permute-start.4 = (bf16[256,1024]{1,0:T(8,128)(2,1)}, bf16[256,1024]{1,0:T(8,128)(2,1)}, u32[]{:S(2)}, u32[]{:S(2)}) collective-permute-start(bf16[256,1024]{1,0:T(8,128)(2,1)} %constant_dynamic-slice_fusion), channel_id=1, source_target_pairs={{4,0},{8,4},{12,8},{5,1},{9,5},{13,9},{6,2},{10,6},{14,10},{7,3},{... | collective-permute-start | bytes 1572872 | tf_op jit(solution)/shard_map/line_1/ppermute | solution.py:306
  16.7 11.5 %all-to-all-done.mine_ref.up_ref.refs_2_ = bf16[4,64,1280]{2,1,0:T(8,128)(2,1)S(1)} async-done(((bf16[4,64,1280]{2,1,0:T(8,128)(2,1)}), bf16[4,64,1280]{2,1,0:T(8,128)(2,1)S(1)}, u32[]{:S(2)}, u32[]{:S(2)}) %all-to-all-start) | async-done | bytes 655392 | tf_op jit(solution)/shard_map/all_to_all | solution.py:338
  28.1 0.9 slice.9
  29.0 1.5 %collective-permute-start = (bf16[4,64,1024]{2,1,0:T(8,128)(2,1)}, bf16[4,64,1024]{2,1,0:T(8,128)(2,1)S(1)}, u32[]{:S(2)}, u32[]{:S(2)}) collective-permute-start(bf16[4,64,1024]{2,1,0:T(8,128)(2,1)} %slice.9), channel_id=1, source_target_pairs={{0,16},{16,0},{1,17},{17,1},{2,18},{18,2},{3,19},{19,3},{4,20},{20... | collective-permute-start | bytes 1572872 | tf_op jit(solution)/shard_map/swap_a/ppermute | solution.py:342
  30.5 0.0 copy-done.9
  30.5 0.0 copy-done.10
  30.5 0.0 copy-done.11
  30.5 0.2 select_reduce_fusion
  30.7 1.3 %broadcast_multiply_fusion.w_ref.refs_0_ = bf16[384,1024]{1,0:T(8,128)(2,1)S(1)} fusion(bf16[384,1024]{1,0:T(8,128)(2,1)} %param.9, bf16[384]{0:T(512)(128)(2,1)S(1)} %subtract_convert_fusion), kind=kLoop, calls=%fused_computation.1 | loop fusion | flops 393216 | bytes 1573632 | tf_op jit(solution)/shard_map/mul | solution.py:348
  32.0 0.0 collective-permute-done.3.refs_4_
  32.0 0.7 collective-permute-start.5
  32.7 0.7 collective-permute-start.7
  33.4 0.6 collective-permute-done.4.refs_5_
  34.0 1.3 %collective-permute-start.6 = (bf16[256,1024]{1,0:T(8,128)(2,1)}, bf16[256,1024]{1,0:T(8,128)(2,1)}, u32[]{:S(2)}, u32[]{:S(2)}) collective-permute-start(bf16[256,1024]{1,0:T(8,128)(2,1)} %collective-permute-done.4.refs_5_), channel_id=1, source_target_pairs={{4,0},{8,4},{5,1},{9,5},{6,2},{10,6},{7,3},{11,7},{20,16},{24,20},... | collective-permute-start | bytes 1572872 | tf_op jit(solution)/shard_map/line_2/ppermute | solution.py:306
  35.3 0.1 pad_add_fusion.2.scalars
  35.4 5.7 %collective-permute-done.other_ref.refs_2_ = bf16[4,64,1024]{2,1,0:T(8,128)(2,1)S(1)} collective-permute-done((bf16[4,64,1024]{2,1,0:T(8,128)(2,1)}, bf16[4,64,1024]{2,1,0:T(8,128)(2,1)S(1)}, u32[]{:S(2)}, u32[]{:S(2)}) %collective-permute-start) | collective-permute-done | bytes 524320 | tf_op jit(solution)/shard_map/swap_a/ppermute | solution.py:342
  41.0 1.4 %copy-done.1 = bf16[384,2048]{1,0:T(8,128)(2,1)S(1)} copy-done((bf16[384,2048]{1,0:T(8,128)(2,1)S(1)}, bf16[384,2048]{1,0:T(8,128)(2,1)}, u32[]{:S(2)}) %copy-start.1) | copy-done | bytes 1572888
  42.4 1.3 %project.1 = bf16[384,128]{1,0:T(8,128)(2,1)S(1)} custom-call(s32[5]{0:T(128)S(1)} %pad_add_fusion.2.scalars, bf16[384,2048]{1,0:T(8,128)(2,1)S(1)} %copy-done.1, bf16[384,1024]{1,0:T(8,128)(2,1)S(1)} %broadcast_multiply_fusion.w_ref.refs_0_, bf16[4,64,1280]{2,1,0:T(8,128)(2,1)S(1)} %all-to-all-done.mine_ref.up_ref.refs_2_, ...), custom_call_target="tpu_custom_call" | custom-call | flops 113246208 | bytes 2949120 | tf_op jit(solution)/shard_map/project/pallas_call | solution.py:195
  43.7 0.1 collective-permute-start.1
  43.8 1.3 %collective-permute-done.1 = bf16[384,128]{1,0:T(8,128)(2,1)S(1)} collective-permute-done((bf16[384,128]{1,0:T(8,128)(2,1)S(1)}, bf16[384,128]{1,0:T(8,128)(2,1)S(1)}, u32[]{:S(2)}, u32[]{:S(2)}) %collective-permute-start.1) | collective-permute-done | bytes 98336 | tf_op jit(solution)/shard_map/ppermute | solution.py:390
  45.1 1.6 %collective-permute-start.2 = (bf16[384,128]{1,0:T(8,128)(2,1)S(1)}, bf16[384,128]{1,0:T(8,128)(2,1)S(1)}, u32[]{:S(2)}, u32[]{:S(2)}) collective-permute-start(bf16[384,128]{1,0:T(8,128)(2,1)S(1)} %add_convert_fusion.here_ref), channel_id=1, source_target_pairs={{0,2},{2,0},{1,3},{3,1},{4,6},{6,4},{5,7},{7,5},{8,10},{10,8},{9,1... | collective-permute-start | bytes 294920 | tf_op jit(solution)/shard_map/ppermute | solution.py:390
  46.7 0.1 pad_add_fusion.1.slots
  46.8 0.0 collective-permute-done.5.refs_6_
  46.8 10.6 %collective-permute-done.6.refs_7_ = bf16[256,1024]{1,0:T(8,128)(2,1)} collective-permute-done((bf16[256,1024]{1,0:T(8,128)(2,1)}, bf16[256,1024]{1,0:T(8,128)(2,1)}, u32[]{:S(2)}, u32[]{:S(2)}) %collective-permute-start.6) | collective-permute-done | bytes 524320 | tf_op jit(solution)/shard_map/line_2/ppermute | solution.py:306
  57.3 0.0 collective-permute-done.7.refs_4_
  57.3 0.8 copy-done.3
  58.1 0.0 collective-permute-done.2.there_ref
  58.1 1.3 %adapter_grads.1 = (bf16[4,64,2304]{2,1,0:T(8,128)(2,1)S(1)}, bf16[384,64]{1,0:T(8,128)(2,1)S(1)}) custom-call(s32[4]{0:T(128)S(1)} %pad_add_fusion.1.slots, bf16[384,2048]{1,0:T(8,128)(2,1)S(1)} %copy-done.1, bf16[384,1024]{1,0:T(8,128)(2,1)S(1)} %broadcast_multiply_fusion.w_ref.refs_0_, bf16[384,128]{1,0:T(8,128)(2,1)S(1)} %add_convert_fusion.here_ref, ...), custom_call_target="tpu_custom_call" | custom-call | flops 113246208 | bytes 2949120 | tf_op jit(solution)/shard_map/adapter_grads/pallas_call | solution.py:224
  59.4 0.0 copy-start.2
  59.4 1.0 copy-done.2
  60.5 0.6 copy-done.5
  61.1 4.3 %all-to-all-start.1 = ((bf16[4,64,2304]{2,1,0:T(8,128)(2,1)}), bf16[4,64,2304]{2,1,0:T(8,128)(2,1)}, u32[]{:S(2)}, u32[]{:S(2)}) async-start(bf16[4,64,2304]{2,1,0:T(8,128)(2,1)} %copy-done.2), calls=%async_computation.1 | async-start | bytes 2359296 | tf_op jit(solution)/shard_map/all_to_all | solution.py:366
  65.4 1.1 broadcast_select_fusion
  66.5 1.3 %collective-permute-start.11 = (bf16[256,1024]{1,0:T(8,128)(2,1)S(1)}, bf16[256,1024]{1,0:T(8,128)(2,1)}, u32[]{:S(2)}, u32[]{:S(2)}) collective-permute-start(bf16[256,1024]{1,0:T(8,128)(2,1)S(1)} %broadcast_select_fusion), channel_id=1, source_target_pairs={{8,12},{4,0},{9,13},{5,1},{10,14},{6,2},{11,15},{7,3},{24,28},{20,... | collective-permute-start | bytes 1572872 | tf_op jit(solution)/shard_map/line_3/ppermute | solution.py:312
  67.8 2.4 %collective-permute-start.8 = (bf16[256,1024]{1,0:T(8,128)(2,1)}, bf16[256,1024]{1,0:T(8,128)(2,1)}, u32[]{:S(2)}, u32[]{:S(2)}) collective-permute-start(bf16[256,1024]{1,0:T(8,128)(2,1)} %collective-permute-done.4.refs_5_), channel_id=1, source_target_pairs={{0,16},{4,20},{8,24},{16,0},{20,4},{24,8},{1,17},{5,21},{9,25},{17... | collective-permute-start | bytes 1572872 | tf_op jit(solution)/shard_map/swap_w/ppermute | solution.py:292
  70.2 3.4 %collective-permute-start.10 = (bf16[256,1024]{1,0:T(8,128)(2,1)}, bf16[256,1024]{1,0:T(8,128)(2,1)}, u32[]{:S(2)}, u32[]{:S(2)}) collective-permute-start(bf16[256,1024]{1,0:T(8,128)(2,1)} %collective-permute-done.6.refs_7_), channel_id=1, source_target_pairs={{0,16},{4,20},{16,0},{20,4},{1,17},{5,21},{17,1},{21,5},{2,18},{6,... | collective-permute-start | bytes 1572872 | tf_op jit(solution)/shard_map/swap_w/ppermute | solution.py:292
  73.7 1.5 %collective-permute-start.9 = (bf16[256,1024]{1,0:T(8,128)(2,1)S(1)}, bf16[256,1024]{1,0:T(8,128)(2,1)}, u32[]{:S(2)}, u32[]{:S(2)}) collective-permute-start(bf16[256,1024]{1,0:T(8,128)(2,1)S(1)} %collective-permute-done.5.refs_6_), channel_id=1, source_target_pairs={{8,24},{12,28},{24,8},{28,12},{9,25},{13,29},{25,9},{29,13},{10,26... | collective-permute-start | bytes 1572872 | tf_op jit(solution)/shard_map/swap_w/ppermute | solution.py:292
  75.1 20.8 %collective-permute-done.11.refs_8_ = bf16[256,1024]{1,0:T(8,128)(2,1)} collective-permute-done((bf16[256,1024]{1,0:T(8,128)(2,1)S(1)}, bf16[256,1024]{1,0:T(8,128)(2,1)}, u32[]{:S(2)}, u32[]{:S(2)}) %collective-permute-start.11) | collective-permute-done | bytes 524320 | tf_op jit(solution)/shard_map/line_3/ppermute | solution.py:312
  95.9 2.4 %collective-permute-start.12 = (bf16[256,1024]{1,0:T(8,128)(2,1)}, bf16[256,1024]{1,0:T(8,128)(2,1)}, u32[]{:S(2)}, u32[]{:S(2)}) collective-permute-start(bf16[256,1024]{1,0:T(8,128)(2,1)} %collective-permute-done.11.refs_8_), channel_id=1, source_target_pairs={{12,28},{0,16},{28,12},{16,0},{13,29},{1,17},{29,13},{17,1},{14,30... | collective-permute-start | bytes 1572872 | tf_op jit(solution)/shard_map/swap_w/ppermute | solution.py:292
  98.3 0.1 stack.65.scalars
  98.4 0.1 stack.60.scalars
  98.5 0.1 pad_add_fusion.scalars
  98.6 0.0 collective-permute-done.8.refs_5_
  98.6 0.0 collective-permute-done.10.refs_7_
  98.6 0.0 collective-permute-done.9.refs_6_
  98.6 0.0 copy-start.4
  98.6 1.0 copy-done.4
  99.7 0.9 copy-done.6
  100.6 3.8 %product.3.refs_1_ = f32[384,1024]{1,0:T(8,128)S(1)} custom-call(s32[9]{0:T(128)S(1)} %stack.60.scalars, bf16[384,1024]{1,0:T(8,128)(2,1)S(1)} %broadcast_multiply_fusion.w_ref.refs_0_, bf16[384,64]{1,0:T(8,128)(2,1)S(1)} %copy-done.6, bf16[4,64,1024]{2,1,0:T(8,128)(2,1)S(1)} %collective-permute-done.other_ref.refs_2_, bf16[256,2048]{1,0:T(8,128)(2,1)S(1)} %copy-done, ...), custom_call_target="tpu_custom_call" | custom-call | flops 1006632960 | bytes 3407872 | tf_op jit(solution)/shard_map/product/pallas_call | solution.py:141
  104.3 5.0 %product.4.refs_3_ = bf16[384,2048]{1,0:T(8,128)(2,1)} custom-call(s32[10]{0:T(128)S(1)} %stack.65.scalars, bf16[384,1024]{1,0:T(8,128)(2,1)S(1)} %broadcast_multiply_fusion.w_ref.refs_0_, bf16[384,64]{1,0:T(8,128)(2,1)S(1)} %copy-done.6, bf16[4,64,1280]{2,1,0:T(8,128)(2,1)S(1)} %all-to-all-done.mine_ref.up_ref.refs_2_, bf16[256,2048]{1,0:T(8,128)(2,1)S(1)} %copy-done, ...), custom_call_target="tpu_custom_call" | custom-call | flops 1207959552 | bytes 3932160 | tf_op jit(solution)/shard_map/product/pallas_call | solution.py:141
  109.3 0.7 collective-permute-done.12.refs_2_
  110.0 3.0 %product.5 = bf16[384,2048]{1,0:T(8,128)(2,1)} custom-call(s32[6]{0:T(128)S(1)} %pad_add_fusion.scalars, bf16[384,1024]{1,0:T(8,128)(2,1)S(1)} %broadcast_multiply_fusion.w_ref.refs_0_, f32[384,1024]{1,0:T(8,128)S(1)} %product.3.refs_1_, bf16[256,1024]{1,0:T(8,128)(2,1)} %collective-permute-done.12.refs_2_, ...), custom_call_target="tpu_custom_call", output_to_operand_aliasing={{}: (4, {})} | custom-call | flops 402653184 | bytes 1835008 | tf_op jit(solution)/shard_map/product/pallas_call | solution.py:141
  113.1 0.0 all-to-all-done.1.got_ref
  113.1 2.2 %owner_sums.1 = (f32[1,64,2048]{2,1,0:T(8,128)}, f32[1,64,256]{2,1,0:T(8,128)}) custom-call(bf16[4,64,2304]{2,1,0:T(8,128)(2,1)} %all-to-all-done.1.got_ref), custom_call_target="tpu_custom_call" | custom-call | flops 589824 | bytes 1179648 | tf_op jit(solution)/shard_map/owner_sums/pallas_call | solution.py:266
  (9 shorter events, 0.0 us)
Async XLA Ops:
  0.6 9.1 %copy-start = (bf16[256,2048]{1,0:T(8,128)(2,1)S(1)}, bf16[256,2048]{1,0:T(8,128)(2,1)}, u32[]{:S(2)}) copy-start(bf16[256,2048]{1,0:T(8,128)(2,1)} %refs_3_.3) | copy-start | bytes 3145732
  0.6 1.0 copy-start.7
  1.7 0.8 copy-start.8
  3.3 27.2 %copy-start.9 = (s32[384]{0:T(512)S(1)}, s32[384]{0:T(512)}, u32[]{:S(2)}) copy-start(s32[384]{0:T(512)} %param.15) | copy-start | bytes 4612
  3.3 27.2 %copy-start.10 = (s32[4]{0:T(128)S(1)}, s32[4]{0:T(128)}, u32[]{:S(2)}) copy-start(s32[4]{0:T(128)} %param.14) | copy-start | bytes 52
  3.3 27.2 %copy-start.11 = (s32[3,1]{0,1:T(1,128)S(1)}, s32[3,1]{0,1:T(1,128)}, u32[]{:S(2)}) copy-start(s32[3,1]{0,1:T(1,128)} %param.13) | copy-start | bytes 40
  3.3 24.8 %all-to-all-start = ((bf16[4,64,1280]{2,1,0:T(8,128)(2,1)}), bf16[4,64,1280]{2,1,0:T(8,128)(2,1)S(1)}, u32[]{:S(2)}, u32[]{:S(2)}) async-start(bf16[4,64,1280]{2,1,0:T(8,128)(2,1)} %payload.1), calls=%async_computation | async-start | bytes 1310720 | tf_op jit(solution)/shard_map/all_to_all | solution.py:338
  10.6 21.3 %collective-permute-start.3 = (bf16[256,1024]{1,0:T(8,128)(2,1)}, bf16[256,1024]{1,0:T(8,128)(2,1)}, u32[]{:S(2)}, u32[]{:S(2)}) collective-permute-start(bf16[256,1024]{1,0:T(8,128)(2,1)} %constant_dynamic-slice_fusion), channel_id=1, source_target_pairs={{0,4},{4,8},{8,12},{1,5},{5,9},{9,13},{2,6},{6,10},{10,14},{3,7},{... | collective-permute-start | bytes 1572872 | tf_op jit(solution)/shard_map/line_1/ppermute | solution.py:305
  15.4 18.6 %collective-permute-start.4 = (bf16[256,1024]{1,0:T(8,128)(2,1)}, bf16[256,1024]{1,0:T(8,128)(2,1)}, u32[]{:S(2)}, u32[]{:S(2)}) collective-permute-start(bf16[256,1024]{1,0:T(8,128)(2,1)} %constant_dynamic-slice_fusion), channel_id=1, source_target_pairs={{4,0},{8,4},{12,8},{5,1},{9,5},{13,9},{6,2},{10,6},{14,10},{7,3},{... | collective-permute-start | bytes 1572872 | tf_op jit(solution)/shard_map/line_1/ppermute | solution.py:306
  29.0 12.1 %collective-permute-start = (bf16[4,64,1024]{2,1,0:T(8,128)(2,1)}, bf16[4,64,1024]{2,1,0:T(8,128)(2,1)S(1)}, u32[]{:S(2)}, u32[]{:S(2)}) collective-permute-start(bf16[4,64,1024]{2,1,0:T(8,128)(2,1)} %slice.9), channel_id=1, source_target_pairs={{0,16},{16,0},{1,17},{17,1},{2,18},{18,2},{3,19},{19,3},{4,20},{20... | collective-permute-start | bytes 1572872 | tf_op jit(solution)/shard_map/swap_a/ppermute | solution.py:342
  32.0 14.8 %collective-permute-start.5 = (bf16[256,1024]{1,0:T(8,128)(2,1)}, bf16[256,1024]{1,0:T(8,128)(2,1)S(1)}, u32[]{:S(2)}, u32[]{:S(2)}) collective-permute-start(bf16[256,1024]{1,0:T(8,128)(2,1)} %collective-permute-done.3.refs_4_), channel_id=1, source_target_pairs={{4,8},{8,12},{5,9},{9,13},{6,10},{10,14},{7,11},{11,15},{20,24},{2... | collective-permute-start | bytes 1572872 | tf_op jit(solution)/shard_map/line_2/ppermute | solution.py:305
  32.7 24.6 %collective-permute-start.7 = (bf16[256,1024]{1,0:T(8,128)(2,1)}, bf16[256,1024]{1,0:T(8,128)(2,1)S(1)}, u32[]{:S(2)}, u32[]{:S(2)}) collective-permute-start(bf16[256,1024]{1,0:T(8,128)(2,1)} %collective-permute-done.3.refs_4_), channel_id=1, source_target_pairs={{4,20},{8,24},{12,28},{20,4},{24,8},{28,12},{5,21},{9,25},{13,29},... | collective-permute-start | bytes 1572872 | tf_op jit(solution)/shard_map/swap_w/ppermute | solution.py:292
  34.0 23.3 %collective-permute-start.6 = (bf16[256,1024]{1,0:T(8,128)(2,1)}, bf16[256,1024]{1,0:T(8,128)(2,1)}, u32[]{:S(2)}, u32[]{:S(2)}) collective-permute-start(bf16[256,1024]{1,0:T(8,128)(2,1)} %collective-permute-done.4.refs_5_), channel_id=1, source_target_pairs={{4,0},{8,4},{5,1},{9,5},{6,2},{10,6},{7,3},{11,7},{20,16},{24,20},... | collective-permute-start | bytes 1572872 | tf_op jit(solution)/shard_map/line_2/ppermute | solution.py:306
  41.0 1.4 %copy-start.1 = (bf16[384,2048]{1,0:T(8,128)(2,1)S(1)}, bf16[384,2048]{1,0:T(8,128)(2,1)}, u32[]{:S(2)}) copy-start(bf16[384,2048]{1,0:T(8,128)(2,1)} %x_ref.3) | copy-start | bytes 4718596
  43.7 1.4 %collective-permute-start.1 = (bf16[384,128]{1,0:T(8,128)(2,1)S(1)}, bf16[384,128]{1,0:T(8,128)(2,1)S(1)}, u32[]{:S(2)}, u32[]{:S(2)}) collective-permute-start(bf16[384,128]{1,0:T(8,128)(2,1)S(1)} %project.1), channel_id=1, source_target_pairs={{0,1},{1,0},{2,3},{3,2},{4,5},{5,4},{6,7},{7,6},{8,9},{9,8},{10,11... | collective-permute-start | bytes 294920 | tf_op jit(solution)/shard_map/ppermute | solution.py:390
  45.1 13.0 %collective-permute-start.2 = (bf16[384,128]{1,0:T(8,128)(2,1)S(1)}, bf16[384,128]{1,0:T(8,128)(2,1)S(1)}, u32[]{:S(2)}, u32[]{:S(2)}) collective-permute-start(bf16[384,128]{1,0:T(8,128)(2,1)S(1)} %add_convert_fusion.here_ref), channel_id=1, source_target_pairs={{0,2},{2,0},{1,3},{3,1},{4,6},{6,4},{5,7},{7,5},{8,10},{10,8},{9,1... | collective-permute-start | bytes 294920 | tf_op jit(solution)/shard_map/ppermute | solution.py:390
  57.3 0.8 copy-start.3
  59.4 1.0 copy-start.2
  60.5 0.6 copy-start.5
  61.1 52.0 %all-to-all-start.1 = ((bf16[4,64,2304]{2,1,0:T(8,128)(2,1)}), bf16[4,64,2304]{2,1,0:T(8,128)(2,1)}, u32[]{:S(2)}, u32[]{:S(2)}) async-start(bf16[4,64,2304]{2,1,0:T(8,128)(2,1)} %copy-done.2), calls=%async_computation.1 | async-start | bytes 2359296 | tf_op jit(solution)/shard_map/all_to_all | solution.py:366
  66.5 29.4 %collective-permute-start.11 = (bf16[256,1024]{1,0:T(8,128)(2,1)S(1)}, bf16[256,1024]{1,0:T(8,128)(2,1)}, u32[]{:S(2)}, u32[]{:S(2)}) collective-permute-start(bf16[256,1024]{1,0:T(8,128)(2,1)S(1)} %broadcast_select_fusion), channel_id=1, source_target_pairs={{8,12},{4,0},{9,13},{5,1},{10,14},{6,2},{11,15},{7,3},{24,28},{20,... | collective-permute-start | bytes 1572872 | tf_op jit(solution)/shard_map/line_3/ppermute | solution.py:312
  67.8 30.8 %collective-permute-start.8 = (bf16[256,1024]{1,0:T(8,128)(2,1)}, bf16[256,1024]{1,0:T(8,128)(2,1)}, u32[]{:S(2)}, u32[]{:S(2)}) collective-permute-start(bf16[256,1024]{1,0:T(8,128)(2,1)} %collective-permute-done.4.refs_5_), channel_id=1, source_target_pairs={{0,16},{4,20},{8,24},{16,0},{20,4},{24,8},{1,17},{5,21},{9,25},{17... | collective-permute-start | bytes 1572872 | tf_op jit(solution)/shard_map/swap_w/ppermute | solution.py:292
  70.2 28.4 %collective-permute-start.10 = (bf16[256,1024]{1,0:T(8,128)(2,1)}, bf16[256,1024]{1,0:T(8,128)(2,1)}, u32[]{:S(2)}, u32[]{:S(2)}) collective-permute-start(bf16[256,1024]{1,0:T(8,128)(2,1)} %collective-permute-done.6.refs_7_), channel_id=1, source_target_pairs={{0,16},{4,20},{16,0},{20,4},{1,17},{5,21},{17,1},{21,5},{2,18},{6,... | collective-permute-start | bytes 1572872 | tf_op jit(solution)/shard_map/swap_w/ppermute | solution.py:292
  73.7 24.9 %collective-permute-start.9 = (bf16[256,1024]{1,0:T(8,128)(2,1)S(1)}, bf16[256,1024]{1,0:T(8,128)(2,1)}, u32[]{:S(2)}, u32[]{:S(2)}) collective-permute-start(bf16[256,1024]{1,0:T(8,128)(2,1)S(1)} %collective-permute-done.5.refs_6_), channel_id=1, source_target_pairs={{8,24},{12,28},{24,8},{28,12},{9,25},{13,29},{25,9},{29,13},{10,26... | collective-permute-start | bytes 1572872 | tf_op jit(solution)/shard_map/swap_w/ppermute | solution.py:292
  95.9 14.1 %collective-permute-start.12 = (bf16[256,1024]{1,0:T(8,128)(2,1)}, bf16[256,1024]{1,0:T(8,128)(2,1)}, u32[]{:S(2)}, u32[]{:S(2)}) collective-permute-start(bf16[256,1024]{1,0:T(8,128)(2,1)} %collective-permute-done.11.refs_8_), channel_id=1, source_target_pairs={{12,28},{0,16},{28,12},{16,0},{13,29},{1,17},{29,13},{17,1},{14,30... | collective-permute-start | bytes 1572872 | tf_op jit(solution)/shard_map/swap_w/ppermute | solution.py:292
  98.6 1.0 copy-start.4
  99.7 0.9 copy-start.6

commit v4 on v3

v4 whole, which is shorter than its diff:
```python
import functools

import jax
import jax.numpy as jnp
from jax import lax
from jax.experimental import pallas as pl
from jax.experimental.pallas import tpu as pltpu
from jax.sharding import PartitionSpec as P

SCALE = 2.0
VMEM_LIMIT = 48 << 20
F32 = jnp.float32
BF16 = jnp.bfloat16


ROWS_BY_ROWS = (((1,), (1,)), ((), ()))
COLUMNS_BY_COLUMNS = (((0,), (0,)), ((), ()))


def low_kernel(blocks, scalars, w_ref, up_ref, out_ref):
    rows = w_ref.shape[0] // blocks
    for b in range(blocks):
        span = slice(b * rows, (b + 1) * rows)
        out_ref[span, :] = lax.dot_general(
            w_ref[span, :], up_ref[scalars[b]], ROWS_BY_ROWS, preferred_element_type=F32
        ).astype(BF16)


def hidden_kernel(blocks, scalars, x_ref, mine_ref, other_ref, out_ref):
    rows = x_ref.shape[0] // blocks
    part = mine_ref.shape[2]

    def run(first, second):
        for b in range(blocks):
            s = scalars[b]
            span = slice(b * rows, (b + 1) * rows)
            hidden = lax.dot_general(
                x_ref[span, :part], first[s], ROWS_BY_ROWS, preferred_element_type=F32
            ) + lax.dot_general(
                x_ref[span, part:], second[s], ROWS_BY_ROWS, preferred_element_type=F32
            )
            out_ref[span, :] = hidden.astype(BF16)

    @pl.when(scalars[blocks] == 0)
    def _():
        run(mine_ref, other_ref)

    @pl.when(scalars[blocks] != 0)
    def _():
        run(other_ref, mine_ref)


def grads_kernel(blocks, scale_rank, scalars, x_ref, here_ref, there_ref, table_ref, *rest):
    acc_ref = rest[-1]
    rows = x_ref.shape[0] // blocks
    total = here_ref[...].astype(F32) + there_ref[...].astype(F32)
    ranks = (SCALE * total if scale_rank else total).astype(BF16)
    if scale_rank:
        rest[0][...] = ranks
    acc_ref[...] = jnp.zeros_like(acc_ref)
    for b in range(blocks):
        span = slice(b * rows, (b + 1) * rows)
        acc_ref[scalars[b]] += lax.dot_general(
            ranks[span], x_ref[span, :], COLUMNS_BY_COLUMNS, preferred_element_type=F32
        )
    table = acc_ref[...] if scale_rank else SCALE * acc_ref[...]
    table_ref[...] = table.astype(BF16)


def product_kernel(plan, scalars, *refs):
    count, blocks, opens, aligned = plan
    refs = list(refs)
    weighted_ref = refs.pop(0)
    acc_ref, out_ref = refs.pop(), refs.pop()
    if opens:
        low_ref, down_ref, own_ref = refs[:3]
        pieces = refs[3 : 3 + count]
        depth = own_ref.shape[0]
        block_rows = low_ref.shape[0] // blocks
        own = take_columns(weighted_ref, scalars[blocks + 1], 0, depth, aligned)
        acc_ref[...] = jnp.dot(own, own_ref[...], preferred_element_type=F32)
        for b in range(blocks):
            span = slice(b * block_rows, (b + 1) * block_rows)
            acc_ref[span, :] += jnp.dot(
                low_ref[span, :], down_ref[scalars[b]], preferred_element_type=F32
            )
    else:
        pieces = refs[1 : 1 + count]
        depth = pieces[0].shape[0]
        acc_ref[...] = refs[0][...]
    for j, piece in enumerate(pieces):
        owner = scalars[blocks + 2 + j]

        @pl.when(owner >= 0)
        def _(j=j, piece=piece, owner=owner):
            columns = take_columns(weighted_ref, owner, j + 1, depth, aligned)
            acc_ref[...] += jnp.dot(columns, piece[...], preferred_element_type=F32)

    out_ref[...] = acc_ref[...].astype(out_ref.dtype)


def take_columns(ref, owner, position, depth, aligned):
    if aligned:
        return ref[:, pl.ds(pl.multiple_of(owner * depth, 128), depth)]
    return ref[:, position * depth : (position + 1) * depth]


def product(half, slots, me, owners, weighted, pieces, start, width, into=None, partial=False):
    opens = isinstance(start, tuple)
    rows = weighted.shape[0]
    depth = pieces[0].shape[0]
    part = width // 2
    tile = min(512, part)
    tiles = part // tile
    blocks = slots.shape[0]
    aligned = depth % 128 == 0
    if not aligned:
        begins = [me] + [jnp.maximum(o, 0) for o in owners]
        weighted = jnp.concatenate(
            [lax.dynamic_slice_in_dim(weighted, o * depth, depth, 1) for o in begins], axis=1
        )
    scalars = jnp.stack([*slots, half, me, *owners])
    whole = lambda i, s: (0, 0)
    here = lambda i, s: (0, i)
    column = lambda i, s: (0, s[blocks] * tiles + i)
    specs = [pl.BlockSpec(weighted.shape, whole)]
    operands = [weighted]
    if opens:
        low_b, down, own = start
        specs += [
            pl.BlockSpec(low_b.shape, whole),
            pl.BlockSpec((*down.shape[:2], tile), lambda i, s: (0, 0, i)),
            pl.BlockSpec((depth, tile), column),
        ]
        operands += [low_b, down, own]
    else:
        specs.append(pl.BlockSpec((rows, tile), here))
        operands.append(start)
    specs += [pl.BlockSpec((depth, tile), here) for _ in pieces]
    operands += pieces
    aliases = {}
    if into is not None:
        specs.append(pl.BlockSpec(memory_space=pl.ANY))
        operands.append(into)
        aliases = {len(operands): 0}
    shape = jax.ShapeDtypeStruct((rows, part), F32) if partial else jax.ShapeDtypeStruct((rows, width), BF16)
    return pl.pallas_call(
        functools.partial(product_kernel, (len(pieces), blocks, opens, aligned)),
        out_shape=shape,
        grid_spec=pltpu.PrefetchScalarGridSpec(
            num_scalar_prefetch=1,
            grid=(tiles,),
            in_specs=specs,
            out_specs=pl.BlockSpec((rows, tile), here if partial else column),
            scratch_shapes=[pltpu.VMEM((rows, tile), F32)],
        ),
        input_output_aliases=aliases,
        compiler_params=pltpu.CompilerParams(vmem_limit_bytes=VMEM_LIMIT),
        cost_estimate=pl.CostEstimate(
            flops=2 * rows * part * depth * (len(pieces) + 1),
            bytes_accessed=2 * (part * (depth * (len(pieces) + 1) + rows)),
            transcendentals=0,
        ),
        name="product",
    )(scalars, *operands)


def call(kernel, name, out_shape, scalars, operands, specs=None, scratch=(), flops=0, moved=0):
    whole = lambda shape: pl.BlockSpec(shape, lambda i, s: (0,) * len(shape))
    specs = specs or [whole(o.shape) for o in operands]
    single = isinstance(out_shape, jax.ShapeDtypeStruct)
    return pl.pallas_call(
        kernel,
        out_shape=out_shape,
        grid_spec=pltpu.PrefetchScalarGridSpec(
            num_scalar_prefetch=1,
            grid=(1,),
            in_specs=specs,
            out_specs=whole(out_shape.shape) if single else [whole(o.shape) for o in out_shape],
            scratch_shapes=list(scratch),
        ),
        compiler_params=pltpu.CompilerParams(vmem_limit_bytes=VMEM_LIMIT),
        cost_estimate=pl.CostEstimate(flops=flops, bytes_accessed=moved, transcendentals=0),
        name=name,
    )(scalars, *operands)


def bf16(*shape):
    return jax.ShapeDtypeStruct(shape, BF16)


def low_partial(slab_index, slots, weighted, up):
    rows, (_, rank, slab) = weighted.shape[0], up.shape
    blocks = slots.shape[0]
    specs = [
        pl.BlockSpec((rows, slab), lambda i, s: (0, s[blocks])),
        pl.BlockSpec(up.shape, lambda i, s: (0, 0, 0)),
    ]
    return call(
        functools.partial(low_kernel, blocks),
        "low_partial",
        bf16(rows, rank),
        jnp.stack([*slots, slab_index]),
        [weighted, up],
        specs,
        flops=2 * rows * rank * slab,
        moved=2 * (rows * slab + up.size),
    )


def hidden_partial(group, slots, x, mine, other):
    rows, width = x.shape
    rank = mine.shape[1]
    return call(
        functools.partial(hidden_kernel, slots.shape[0]),
        "hidden_partial",
        bf16(rows, rank),
        jnp.stack([*slots, group]),
        [x, mine, other],
        flops=2 * rows * rank * width,
        moved=2 * (x.size + 2 * mine.size),
    )


def down_table(slots, x, here, there, tenants):
    rows, width = x.shape
    rank = here.shape[1]
    return call(
        functools.partial(grads_kernel, slots.shape[0], True),
        "down_table",
        (bf16(tenants, rank, width), bf16(rows, rank)),
        slots,
        [x, here, there],
        scratch=[pltpu.VMEM((tenants, rank, width), F32)],
        flops=2 * rows * rank * width,
        moved=2 * (x.size + tenants * rank * width),
    )


def up_table(slab_index, slots, weighted, here, there, tenants, slab):
    rows, rank = here.shape
    blocks = slots.shape[0]
    specs = [pl.BlockSpec((rows, slab), lambda i, s: (0, s[blocks]))]
    specs += [pl.BlockSpec((rows, rank), lambda i, s: (0, 0))] * 2
    return call(
        functools.partial(grads_kernel, blocks, False),
        "up_table",
        bf16(tenants, rank, slab),
        jnp.stack([*slots, slab_index]),
        [weighted, here, there],
        specs,
        scratch=[pltpu.VMEM((tenants, rank, slab), F32)],
        flops=2 * rows * rank * slab,
        moved=2 * (rows * slab + tenants * rank * slab),
    )


def owner_sum(got, n):
    owned = got.shape[0] // n
    return jnp.sum(got.astype(F32).reshape(n, owned, *got.shape[1:]), axis=0)


def everyone(value, n):
    copies = jnp.broadcast_to(value, (n,) + value.shape).reshape(-1, *value.shape[1:])
    return lax.all_to_all(copies, "seq", split_axis=0, concat_axis=0, tiled=True)


def edge_pairs(parity, k, n):
    pairs = []
    for i in range(parity, n - 1, 2):
        if i >= k - 1:
            pairs.append((i, i + 1))
        if i + 1 <= n - k:
            pairs.append((i + 1, i))
    return pairs


def swap_pairs(pairs, n, groups):
    targets = [b for _, b in pairs]
    return [(g * n + t, (groups - 1 - g) * n + t) for g in range(groups) for t in targets]


def after(value, *others):
    return lax.optimization_barrier((value, others))[0]


def psum_halves(value):
    here = (value.astype(F32) + rest_of(value, "pipe")).astype(BF16)
    return here, rest_of(here, "tensor").astype(BF16)


def rest_of(value, axis):
    size = lax.axis_size(axis)
    rest = 0.0
    for d in range(1, size):
        pairs = [(i, (i + d) % size) for i in range(size)]
        with jax.named_scope(f"psum_{axis}"):
            rest = rest + lax.ppermute(value, axis, pairs).astype(F32)
    return rest


def per_device(
    sizes,
    layer_input,
    out_grad,
    value_weight,
    adapter_down,
    adapter_up,
    block_tenant,
    tenant_slot,
    forget_flag,
):
    n, groups = sizes
    token_rows, width = layer_input.shape
    rank = adapter_down.shape[1]
    slab = adapter_up.shape[2]
    tenants = tenant_slot.shape[0]
    depth = value_weight.shape[0]
    swap = lambda axis: functools.partial(lax.ppermute, axis_name=axis, perm=[(0, 1), (1, 0)])

    half = width // 2
    group = lax.axis_index("groups").astype(jnp.int32)
    me = lax.axis_index("seq").astype(jnp.int32)
    slab_index = lax.axis_index(("tensor", "pipe")).astype(jnp.int32)
    columns = lambda a: lax.dynamic_slice_in_dim(a, group * half, half, a.ndim - 1)

    with jax.named_scope("all_up"):
        up = everyone(adapter_up, n)
    row_sign = (1 - 2 * forget_flag).astype(BF16)
    weighted = out_grad * row_sign[:, None]
    tenant_ids = jnp.arange(tenants, dtype=jnp.int32)
    slots = jnp.sum(
        jnp.where(block_tenant == tenant_ids[None, :], tenant_slot[None, :], 0), axis=1
    ).astype(jnp.int32)

    arrived, owners, pairs_of = [], [], []
    last = [columns(value_weight)] * 2
    for k in range(1, n):
        new = [None, None]
        for parity in (0, 1):
            pairs = edge_pairs(parity, k, n)
            if not pairs:
                continue
            with jax.named_scope(f"line_{k}_{parity}"):
                new[parity] = lax.ppermute(last[1 - parity], "seq", pairs)
            from_left = me % 2 != parity
            owner = jnp.where(from_left, me - k, me + k)
            arrived.append(new[parity])
            pairs_of.append(pairs)
            owners.append(jnp.where((owner >= 0) & (owner < n), owner, -1))
        last = new
    swapped = []
    for value, pairs in zip(arrived, pairs_of):
        with jax.named_scope("swap_w"):
            swapped.append(lax.ppermute(value, ("groups", "seq"), swap_pairs(pairs, n, groups)))

    with jax.named_scope("all_down"):
        own_half = after(columns(adapter_down), up)
        down_mine = everyone(own_half, n)

    with jax.named_scope("low"):
        here, there = psum_halves(low_partial(slab_index, slots, weighted, up))
        there = after(there, arrived[:2], down_mine)
        table, low_b = down_table(slots, layer_input, here, there, tenants)
        got_down = lax.all_to_all(table, "seq", split_axis=0, concat_axis=0, tiled=True)

    with jax.named_scope("swap_a"):
        down_other = swap("groups")(down_mine)
        down_other = after(down_other, arrived[2:4], swapped[0])
    with jax.named_scope("hidden"):
        here, there = psum_halves(
            hidden_partial(group, slots, layer_input, down_mine, down_other)
        )
        there = after(there, got_down, arrived[4:5], swapped[1:2])
        table = up_table(slab_index, slots, weighted, here, there, tenants, slab)
        got_up = lax.all_to_all(table, "seq", split_axis=0, concat_axis=0, tiled=True)

    opening = lambda down: (low_b, down, value_weight)
    first = product(group, slots, me, owners, weighted, arrived, opening(down_mine), width)
    rest = product(
        1 - group,
        slots,
        me,
        owners[:-1],
        weighted,
        swapped[:-1],
        opening(down_other),
        width,
        partial=True,
    )
    full = product(1 - group, slots, me, owners[-1:], weighted, swapped[-1:], rest, width, first)
    return full, owner_sum(got_down, n), owner_sum(got_up, n)


def solution(mesh):
    sizes = (mesh.shape["seq"], mesh.shape["groups"])
    return jax.shard_map(
        functools.partial(per_device, sizes),
        mesh=mesh,
        in_specs=(
            P(("groups", "seq"), ("tensor", "pipe")),
            P(("groups", "seq"), None),
            P("seq", ("tensor", "pipe")),
            P("seq", None, ("tensor", "pipe")),
            P("seq", None, ("tensor", "pipe")),
            P(("groups", "seq"), None),
            P(),
            P(("groups", "seq")),
        ),
        out_specs=(
            P(("groups", "seq"), ("tensor", "pipe")),
            P(("groups", "seq"), None, ("tensor", "pipe")),
            P(("groups", "seq"), None, ("tensor", "pipe")),
        ),
        check_vma=False,
    )
```

time: 116 us -> 119 us (1.026)
  starting transfers between devices: 33.6 us -> 40.4 us
  waiting for transfers between devices: 51 us -> 44.3 us
  other arithmetic: 2.8 us -> 6.22 us
  Pallas kernels: 17.5 us -> 16.2 us
    ppermute x13 -> x15, waiting for transfers between devices: 39.6 us -> 27.7 us  [the longest x5 24.5 us: per_device(): new[parity] = lax.ppermute(last[1 - parity], 'seq', pairs)]
    all_to_all x2 -> x4, starting transfers between devices: 10.7 us -> 16.6 us  [the longest x2 8.77 us: everyone(): lax.all_to_all(copies, 'seq', split_axis=0, concat_axis=0, tiled=True)]
    all_to_all x2 -> x4, waiting for transfers between devices: 11.5 us -> 16.6 us  [the longest x2 16.6 us: everyone(): lax.all_to_all(copies, 'seq', split_axis=0, concat_axis=0, tiled=True)]
    reduce_sum x0 -> x2, other arithmetic: none -> 2.87 us  [owner_sum(): return jnp.sum(got.astype(F32).reshape(n, owned, *got.shape[1:]), axis=0)]
    reshape x0 -> x2, local copies, waits for them, and re-layouts: none -> 2.27 us  [everyone(): jnp.broadcast_to(value, (n,) + value.shape).reshape(-1, *value.shape[1:])]
    unnamed x24 -> x20, local copies, waits for them, and re-layouts: 7.59 us -> 5.78 us
    pallas_call x4, Pallas kernels: 5.65 us -> 4.43 us  [call(): pl.pallas_call(kernel, out_shape=out_shape, grid_spec=pltpu.PrefetchScala...]
    ppermute x13 -> x15, starting transfers between devices: 22.8 us -> 23.8 us  [the longest x5 11.4 us: per_device(): lax.ppermute(value, ('groups', 'seq'), swap_pairs(pairs, n, groups))]
  transfers between devices with their start and end apart: 15 -> 19, of which waited for: 7 -> 6; matrix products, arithmetic and copies ran while one was open for 4% -> 7% of each run, Pallas kernels for 11% -> 14%
where the time goes in v4:
time: 119 us; the launch traced here: 118 us
  waiting for transfers between devices  44.3 us (37%)
  starting transfers between devices  40.4 us (34%)
  Pallas kernels  16.2 us (14%)
  local copies, waits for them, and re-layouts  10.1 us (8%)
  other arithmetic  6.22 us (5%)
    ppermute x5, waiting for transfers between devices, per_device(): new[parity] = lax.ppermute(last[1 - parity], 'seq', pairs)  24.5 us
    all_to_all x2, waiting for transfers between devices, everyone(): lax.all_to_all(copies, 'seq', split_axis=0, concat_axis=0, tiled=True)  16.6 us
    pallas_call x3, Pallas kernels, product(): pl.pallas_call(functools.partial(product_kernel, (len(pieces), blocks, op...  11.8 us
    ppermute x5, starting transfers between devices, per_device(): lax.ppermute(value, ('groups', 'seq'), swap_pairs(pairs, n, groups))  11.4 us
    all_to_all x2, starting transfers between devices, everyone(): lax.all_to_all(copies, 'seq', split_axis=0, concat_axis=0, tiled=True)  8.77 us
    ppermute x5, starting transfers between devices, per_device(): new[parity] = lax.ppermute(last[1 - parity], 'seq', pairs)  8.67 us
    all_to_all x2, starting transfers between devices, per_device(): lax.all_to_all(table, 'seq', split_axis=0, concat_axis=0, tiled=True)  7.87 us
    unnamed x20, local copies, waits for them, and re-layouts  5.78 us
  transfers between devices with their start and end apart: 19, of which 6 were waited for; matrix products, arithmetic and copies ran while one was open for 7% of the time, Pallas kernels for 14%

profile of v4, /device:TPU:0, one launch (start us, length us, event | category | flops | bytes accessed | tf_op | source)
XLA Modules:
  0.0 118.2 jit_solution(11766956083503916223)
XLA Ops:
  0.6 0.0 copy-start
  0.7 1.9 %constant_dynamic-slice_fusion.1 = bf16[256,1024]{1,0:T(8,128)(2,1)} fusion(bf16[256,2048]{1,0:T(8,128)(2,1)} %refs_3_.3, s32[]{:T(128)S(6)} %select_n.66), kind=kLoop, calls=%fused_computation.12 | loop fusion | bytes 1048580 | tf_op jit(solution)/shard_map/dynamic_slice | solution.py:325
  2.6 3.0 %collective-permute-start.2 = (bf16[256,1024]{1,0:T(8,128)(2,1)}, bf16[256,1024]{1,0:T(8,128)(2,1)}, u32[]{:S(2)}, u32[]{:S(2)}) collective-permute-start(bf16[256,1024]{1,0:T(8,128)(2,1)} %constant_dynamic-slice_fusion.1), channel_id=1, source_target_pairs={{0,4},{4,0},{8,12},{12,8},{1,5},{5,1},{9,13},{13,9},{2,6},{6,2},{1... | collective-permute-start | bytes 1572872 | tf_op jit(solution)/shard_map/line_1_0/ppermute | solution.py:345
  5.6 1.5 %collective-permute-start.3 = (bf16[256,1024]{1,0:T(8,128)(2,1)}, bf16[256,1024]{1,0:T(8,128)(2,1)}, u32[]{:S(2)}, u32[]{:S(2)}) collective-permute-start(bf16[256,1024]{1,0:T(8,128)(2,1)} %constant_dynamic-slice_fusion.1), channel_id=1, source_target_pairs={{4,8},{8,4},{5,9},{9,5},{6,10},{10,6},{7,11},{11,7},{20,24},{24,20... | collective-permute-start | bytes 1572872 | tf_op jit(solution)/shard_map/line_1_1/ppermute | solution.py:345
  7.1 1.4 %reshape.20 = bf16[4,64,256]{2,1,0:T(8,128)(2,1)} broadcast(bf16[64,256]{1,0:T(8,128)(2,1)} %bitcast.17), dimensions={1,2} | broadcast | bytes 163840 | tf_op jit(solution)/shard_map/all_up/reshape | solution.py:264
  8.5 4.9 %all-to-all-start = ((bf16[4,64,256]{2,1,0:T(8,128)(2,1)}), bf16[4,64,256]{2,1,0:T(8,128)(2,1)S(1)}, u32[]{:S(2)}, u32[]{:S(2)}) async-start(bf16[4,64,256]{2,1,0:T(8,128)(2,1)} %reshape.20), calls=%async_computation | async-start | bytes 262144 | tf_op jit(solution)/shard_map/all_up/all_to_all | solution.py:265
  13.3 0.9 select_reduce_fusion.scalars
  14.2 0.1 pad_add_fusion.2
  14.3 10.4 %all-to-all-done.up_ref = bf16[4,64,256]{2,1,0:T(8,128)(2,1)S(1)} async-done(((bf16[4,64,256]{2,1,0:T(8,128)(2,1)}), bf16[4,64,256]{2,1,0:T(8,128)(2,1)S(1)}, u32[]{:S(2)}, u32[]{:S(2)}) %all-to-all-start) | async-done | bytes 131104 | tf_op jit(solution)/shard_map/all_up/all_to_all | solution.py:265
  24.7 0.9 reshape.21
  25.6 3.9 %all-to-all-start.1 = ((bf16[4,64,1024]{2,1,0:T(8,128)(2,1)}), bf16[4,64,1024]{2,1,0:T(8,128)(2,1)S(1)}, u32[]{:S(2)}, u32[]{:S(2)}) async-start(bf16[4,64,1024]{2,1,0:T(8,128)(2,1)} %reshape.21), calls=%async_computation.1 | async-start | bytes 1048576 | tf_op jit(solution)/shard_map/all_down/all_to_all | solution.py:265
  29.5 1.4 %broadcast_multiply_fusion.w_ref.refs_0_.x_ref = bf16[384,1024]{1,0:T(8,128)(2,1)S(1)} fusion(bf16[384,1024]{1,0:T(8,128)(2,1)} %param.9, bf16[384]{0:T(512)(128)(2,1)S(1)} %subtract_convert_fusion), kind=kLoop, calls=%fused_computation.1 | loop fusion | flops 393216 | bytes 1573632 | tf_op jit(solution)/shard_map/mul | solution.py:330
  30.9 0.7 low_partial.1
  31.6 0.1 collective-permute-start
  31.7 1.3 %collective-permute-done = bf16[384,64]{1,0:T(8,128)(2,1)S(1)} collective-permute-done((bf16[384,64]{1,0:T(8,128)(2,1)S(1)}, bf16[384,64]{1,0:T(8,128)(2,1)S(1)}, u32[]{:S(2)}, u32[]{:S(2)}) %collective-permute-start) | collective-permute-done | bytes 49184 | tf_op jit(solution)/shard_map/low/psum_pipe/ppermute | solution.py:298
  33.0 1.6 %collective-permute-start.1 = (bf16[384,64]{1,0:T(8,128)(2,1)S(1)}, bf16[384,64]{1,0:T(8,128)(2,1)S(1)}, u32[]{:S(2)}, u32[]{:S(2)}) collective-permute-start(bf16[384,64]{1,0:T(8,128)(2,1)S(1)} %add_convert_fusion.1.here_ref), channel_id=1, source_target_pairs={{0,2},{2,0},{1,3},{3,1},{4,6},{6,4},{5,7},{7,5},{8,10},{10,8},{9,1... | collective-permute-start | bytes 147464 | tf_op jit(solution)/shard_map/low/psum_tensor/ppermute | solution.py:298
  34.6 0.0 collective-permute-done.2.refs_4_
  34.6 1.5 %collective-permute-start.6 = (bf16[256,1024]{1,0:T(8,128)(2,1)}, bf16[256,1024]{1,0:T(8,128)(2,1)}, u32[]{:S(2)}, u32[]{:S(2)}) collective-permute-start(bf16[256,1024]{1,0:T(8,128)(2,1)} %collective-permute-done.2.refs_4_), channel_id=1, source_target_pairs={{4,8},{8,4},{5,9},{9,5},{6,10},{10,6},{7,11},{11,7},{20,24},{24,20... | collective-permute-start | bytes 1572872 | tf_op jit(solution)/shard_map/line_2_1/ppermute | solution.py:345
  36.1 1.9 %collective-permute-done.1.there_ref = bf16[384,64]{1,0:T(8,128)(2,1)S(1)} collective-permute-done((bf16[384,64]{1,0:T(8,128)(2,1)S(1)}, bf16[384,64]{1,0:T(8,128)(2,1)S(1)}, u32[]{:S(2)}, u32[]{:S(2)}) %collective-permute-start.1) | collective-permute-done | bytes 49184 | tf_op jit(solution)/shard_map/low/psum_tensor/ppermute | solution.py:298
  37.9 0.0 collective-permute-done.3.refs_5_
  37.9 6.1 %all-to-all-done.1.refs_2_.mine_ref = bf16[4,64,1024]{2,1,0:T(8,128)(2,1)S(1)} async-done(((bf16[4,64,1024]{2,1,0:T(8,128)(2,1)}), bf16[4,64,1024]{2,1,0:T(8,128)(2,1)S(1)}, u32[]{:S(2)}, u32[]{:S(2)}) %all-to-all-start.1) | async-done | bytes 524320 | tf_op jit(solution)/shard_map/all_down/all_to_all | solution.py:265
  44.1 1.2 down_table.1
  45.2 1.0 copy-done.6
  46.2 4.3 %all-to-all-start.2 = ((bf16[4,64,2048]{2,1,0:T(8,128)(2,1)}), bf16[4,64,2048]{2,1,0:T(8,128)(2,1)}, u32[]{:S(2)}, u32[]{:S(2)}) async-start(bf16[4,64,2048]{2,1,0:T(8,128)(2,1)} %copy-done.6), calls=%async_computation.2 | async-start | bytes 2097152 | tf_op jit(solution)/shard_map/low/all_to_all | solution.py:365
  50.5 0.0 copy-start.1
  50.5 1.4 %collective-permute-start.5 = (bf16[256,1024]{1,0:T(8,128)(2,1)}, bf16[256,1024]{1,0:T(8,128)(2,1)}, u32[]{:S(2)}, u32[]{:S(2)}) collective-permute-start(bf16[256,1024]{1,0:T(8,128)(2,1)} %collective-permute-done.3.refs_5_), channel_id=1, source_target_pairs={{4,0},{8,12},{5,1},{9,13},{6,2},{10,14},{7,3},{11,15},{20,16},{24,... | collective-permute-start | bytes 1572872 | tf_op jit(solution)/shard_map/line_2_0/ppermute | solution.py:345
  51.9 1.6 %collective-permute-start.7 = (bf16[256,1024]{1,0:T(8,128)(2,1)}, bf16[256,1024]{1,0:T(8,128)(2,1)S(1)}, u32[]{:S(2)}, u32[]{:S(2)}) collective-permute-start(bf16[256,1024]{1,0:T(8,128)(2,1)} %collective-permute-done.2.refs_4_), channel_id=1, source_target_pairs={{4,20},{0,16},{12,28},{8,24},{20,4},{16,0},{28,12},{24,8},{5,21},{... | collective-permute-start | bytes 1572872 | tf_op jit(solution)/shard_map/swap_w/ppermute | solution.py:355
  53.5 0.5 collective-permute-start.4
  54.0 0.0 collective-permute-done.6.refs_7_
  54.0 1.3 %collective-permute-start.11 = (bf16[256,1024]{1,0:T(8,128)(2,1)}, bf16[256,1024]{1,0:T(8,128)(2,1)}, u32[]{:S(2)}, u32[]{:S(2)}) collective-permute-start(bf16[256,1024]{1,0:T(8,128)(2,1)} %collective-permute-done.6.refs_7_), channel_id=1, source_target_pairs={{4,0},{8,12},{5,1},{9,13},{6,2},{10,14},{7,3},{11,15},{20,16},{24,... | collective-permute-start | bytes 1572872 | tf_op jit(solution)/shard_map/line_3_0/ppermute | solution.py:345
  55.3 1.5 %collective-permute-start.8 = (bf16[256,1024]{1,0:T(8,128)(2,1)}, bf16[256,1024]{1,0:T(8,128)(2,1)}, u32[]{:S(2)}, u32[]{:S(2)}) collective-permute-start(bf16[256,1024]{1,0:T(8,128)(2,1)} %collective-permute-done.3.refs_5_), channel_id=1, source_target_pairs={{8,24},{4,20},{24,8},{20,4},{9,25},{5,21},{25,9},{21,5},{10,26},{6... | collective-permute-start | bytes 1572872 | tf_op jit(solution)/shard_map/swap_w/ppermute | solution.py:355
  56.8 23.6 %collective-permute-done.5.refs_6_ = bf16[256,1024]{1,0:T(8,128)(2,1)} collective-permute-done((bf16[256,1024]{1,0:T(8,128)(2,1)}, bf16[256,1024]{1,0:T(8,128)(2,1)}, u32[]{:S(2)}, u32[]{:S(2)}) %collective-permute-start.5) | collective-permute-done | bytes 524320 | tf_op jit(solution)/shard_map/line_2_0/ppermute | solution.py:345
  80.4 1.5 %collective-permute-start.10 = (bf16[256,1024]{1,0:T(8,128)(2,1)}, bf16[256,1024]{1,0:T(8,128)(2,1)}, u32[]{:S(2)}, u32[]{:S(2)}) collective-permute-start(bf16[256,1024]{1,0:T(8,128)(2,1)} %collective-permute-done.6.refs_7_), channel_id=1, source_target_pairs={{8,24},{4,20},{24,8},{20,4},{9,25},{5,21},{25,9},{21,5},{10,26},{6... | collective-permute-start | bytes 1572872 | tf_op jit(solution)/shard_map/swap_w/ppermute | solution.py:355
  81.9 0.0 collective-permute-done.7.refs_4_
  81.9 0.8 copy-done.7
  82.7 3.4 %collective-permute-start.9 = (bf16[256,1024]{1,0:T(8,128)(2,1)}, bf16[256,1024]{1,0:T(8,128)(2,1)}, u32[]{:S(2)}, u32[]{:S(2)}) collective-permute-start(bf16[256,1024]{1,0:T(8,128)(2,1)} %collective-permute-done.5.refs_6_), channel_id=1, source_target_pairs={{0,16},{12,28},{16,0},{28,12},{1,17},{13,29},{17,1},{29,13},{2,18}... | collective-permute-start | bytes 1572872 | tf_op jit(solution)/shard_map/swap_w/ppermute | solution.py:355
  86.1 0.0 collective-permute-done.4.refs_2_.other_ref
  86.1 0.0 copy-start.3
  86.2 1.4 %copy-done.3 = bf16[384,2048]{1,0:T(8,128)(2,1)S(1)} copy-done((bf16[384,2048]{1,0:T(8,128)(2,1)S(1)}, bf16[384,2048]{1,0:T(8,128)(2,1)}, u32[]{:S(2)}) %copy-start.3) | copy-done | bytes 1572888
  87.6 1.1 hidden_partial.1
  88.7 0.1 collective-permute-start.13
  88.8 0.9 collective-permute-done.11.refs_8_
  89.6 3.4 %collective-permute-start.12 = (bf16[256,1024]{1,0:T(8,128)(2,1)}, bf16[256,1024]{1,0:T(8,128)(2,1)}, u32[]{:S(2)}, u32[]{:S(2)}) collective-permute-start(bf16[256,1024]{1,0:T(8,128)(2,1)} %collective-permute-done.11.refs_8_), channel_id=1, source_target_pairs={{0,16},{12,28},{16,0},{28,12},{1,17},{13,29},{17,1},{29,13},{2,18}... | collective-permute-start | bytes 1572872 | tf_op jit(solution)/shard_map/swap_w/ppermute | solution.py:355
  93.1 0.1 pad_add_fusion.scalars
  93.2 0.1 stack.65.scalars
  93.2 0.1 stack.61.scalars
  93.3 0.0 collective-permute-done.13
  93.3 0.9 add_convert_fusion.here_ref
  94.3 1.6 %collective-permute-start.14 = (bf16[384,64]{1,0:T(8,128)(2,1)S(1)}, bf16[384,64]{1,0:T(8,128)(2,1)S(1)}, u32[]{:S(2)}, u32[]{:S(2)}) collective-permute-start(bf16[384,64]{1,0:T(8,128)(2,1)S(1)} %add_convert_fusion.here_ref), channel_id=1, source_target_pairs={{0,2},{2,0},{1,3},{3,1},{4,6},{6,4},{5,7},{7,5},{8,10},{10,8},{9,1... | collective-permute-start | bytes 147464 | tf_op jit(solution)/shard_map/hidden/psum_tensor/ppermute | solution.py:298
  95.8 5.0 %product.4.refs_3_ = bf16[384,2048]{1,0:T(8,128)(2,1)} custom-call(s32[10]{0:T(128)S(1)} %stack.65.scalars, bf16[384,1024]{1,0:T(8,128)(2,1)S(1)} %broadcast_multiply_fusion.w_ref.refs_0_.x_ref, bf16[384,64]{1,0:T(8,128)(2,1)S(1)} %get-tuple-element.11.refs_1_, bf16[4,64,1024]{2,1,0:T(8,128)(2,1)S(1)} %all-to-all-done.1.refs_2_.mine_ref, ...), custom_call_target="tpu_custom_call" | custom-call | flops 1207959552 | bytes 3932160 | tf_op jit(solution)/shard_map/product/pallas_call | solution.py:147
  100.8 0.0 collective-permute-done.8.refs_5_
  100.9 0.0 collective-permute-done.10.refs_7_
  100.9 0.0 collective-permute-done.9.refs_6_
  100.9 3.7 %product.3.refs_1_ = f32[384,1024]{1,0:T(8,128)S(1)} custom-call(s32[9]{0:T(128)S(1)} %stack.61.scalars, bf16[384,1024]{1,0:T(8,128)(2,1)S(1)} %broadcast_multiply_fusion.w_ref.refs_0_.x_ref, bf16[384,64]{1,0:T(8,128)(2,1)S(1)} %get-tuple-element.11.refs_1_, bf16[4,64,1024]{2,1,0:T(8,128)(2,1)S(1)} %collective-permute-done.4.refs_2_.other_ref, ...), custom_call_target="tpu_custom_call" | custom-call | flops 1006632960 | bytes 3407872 | tf_op jit(solution)/shard_map/product/pallas_call | solution.py:147
  104.6 1.2 copy-done.4
  105.8 0.0 collective-permute-done.14.there_ref
  105.8 0.0 all-to-all-done.2
  105.8 1.4 %up_table.1 = bf16[4,64,256]{2,1,0:T(8,128)(2,1)} custom-call(s32[4]{0:T(128)S(1)} %get-tuple-element.16.scalars, bf16[384,1024]{1,0:T(8,128)(2,1)S(1)} %broadcast_multiply_fusion.w_ref.refs_0_.x_ref, bf16[384,64]{1,0:T(8,128)(2,1)S(1)} %add_convert_fusion.here_ref, bf16[384,64]{1,0:T(8,128)(2,1)S(1)} %collective-permute-done.14.there_ref), custom_call_target="tpu_custom_call" | custom-call | flops 12582912 | bytes 327680 | tf_op jit(solution)/shard_map/hidden/up_table/pallas_call | solution.py:172
  107.3 3.6 %all-to-all-start.3 = ((bf16[4,64,256]{2,1,0:T(8,128)(2,1)}), bf16[4,64,256]{2,1,0:T(8,128)(2,1)S(1)}, u32[]{:S(2)}, u32[]{:S(2)}) async-start(bf16[4,64,256]{2,1,0:T(8,128)(2,1)} %up_table.1), calls=%async_computation.3 | async-start | bytes 262144 | tf_op jit(solution)/shard_map/hidden/all_to_all | solution.py:376
  110.9 1.4 %copy-done.5 = f32[384,1024]{1,0:T(8,128)S(1)} copy-done((f32[384,1024]{1,0:T(8,128)S(1)}, f32[384,1024]{1,0:T(8,128)}, u32[]{:S(2)}) %copy-start.5) | copy-done | bytes 1572888
  112.3 3.0 %product.5 = bf16[384,2048]{1,0:T(8,128)(2,1)} custom-call(s32[6]{0:T(128)S(1)} %pad_add_fusion.scalars, bf16[384,1024]{1,0:T(8,128)(2,1)S(1)} %broadcast_multiply_fusion.w_ref.refs_0_.x_ref, f32[384,1024]{1,0:T(8,128)S(1)} %copy-done.5, bf16[256,1024]{1,0:T(8,128)(2,1)} %collective-permute-done.12.refs_2_, ...), custom_call_target="tpu_custom_call", output_to_operand_aliasing={{}: (4, {})} | custom-call | flops 402653184 | bytes 1835008 | tf_op jit(solution)/shard_map/product/pallas_call | solution.py:147
  115.3 2.2 %convert_reduce_fusion = f32[64,2048]{1,0:T(8,128)} fusion(bf16[4,64,2048]{2,1,0:T(8,128)(2,1)} %all-to-all-done.2), kind=kLoop, calls=%fused_computation | loop fusion | flops 917504 | bytes 1572864 | tf_op jit(solution)/shard_map/reduce_sum | solution.py:260
  117.5 0.0 all-to-all-done.3
  117.5 0.6 convert_reduce_fusion.1
  (16 shorter events, 0.1 us)
Async XLA Ops:
  0.6 13.7 %copy-start = (bf16[1,64,2048]{2,1,0:T(8,128)(2,1)S(1)}, bf16[1,64,2048]{2,1,0:T(8,128)(2,1)}, u32[]{:S(2)}) copy-start(bf16[1,64,2048]{2,1,0:T(8,128)(2,1)} %param.11) | copy-start | bytes 786436
  0.7 28.8 %copy-start.9 = (s32[384]{0:T(512)S(1)}, s32[384]{0:T(512)}, u32[]{:S(2)}) copy-start(s32[384]{0:T(512)} %param.15) | copy-start | bytes 4612
  2.6 32.0 %collective-permute-start.2 = (bf16[256,1024]{1,0:T(8,128)(2,1)}, bf16[256,1024]{1,0:T(8,128)(2,1)}, u32[]{:S(2)}, u32[]{:S(2)}) collective-permute-start(bf16[256,1024]{1,0:T(8,128)(2,1)} %constant_dynamic-slice_fusion.1), channel_id=1, source_target_pairs={{0,4},{4,0},{8,12},{12,8},{1,5},{5,1},{9,13},{13,9},{2,6},{6,2},{1... | collective-permute-start | bytes 1572872 | tf_op jit(solution)/shard_map/line_1_0/ppermute | solution.py:345
  5.6 32.3 %collective-permute-start.3 = (bf16[256,1024]{1,0:T(8,128)(2,1)}, bf16[256,1024]{1,0:T(8,128)(2,1)}, u32[]{:S(2)}, u32[]{:S(2)}) collective-permute-start(bf16[256,1024]{1,0:T(8,128)(2,1)} %constant_dynamic-slice_fusion.1), channel_id=1, source_target_pairs={{4,8},{8,4},{5,9},{9,5},{6,10},{10,6},{7,11},{11,7},{20,24},{24,20... | collective-permute-start | bytes 1572872 | tf_op jit(solution)/shard_map/line_1_1/ppermute | solution.py:345
  8.5 16.3 %all-to-all-start = ((bf16[4,64,256]{2,1,0:T(8,128)(2,1)}), bf16[4,64,256]{2,1,0:T(8,128)(2,1)S(1)}, u32[]{:S(2)}, u32[]{:S(2)}) async-start(bf16[4,64,256]{2,1,0:T(8,128)(2,1)} %reshape.20), calls=%async_computation | async-start | bytes 262144 | tf_op jit(solution)/shard_map/all_up/all_to_all | solution.py:265
  25.6 18.5 %all-to-all-start.1 = ((bf16[4,64,1024]{2,1,0:T(8,128)(2,1)}), bf16[4,64,1024]{2,1,0:T(8,128)(2,1)S(1)}, u32[]{:S(2)}, u32[]{:S(2)}) async-start(bf16[4,64,1024]{2,1,0:T(8,128)(2,1)} %reshape.21), calls=%async_computation.1 | async-start | bytes 1048576 | tf_op jit(solution)/shard_map/all_down/all_to_all | solution.py:265
  29.5 14.6 %copy-start.2 = (bf16[384,2048]{1,0:T(8,128)(2,1)S(1)}, bf16[384,2048]{1,0:T(8,128)(2,1)}, u32[]{:S(2)}) copy-start(bf16[384,2048]{1,0:T(8,128)(2,1)} %x_ref.3) | copy-start | bytes 4718596
  31.6 1.4 %collective-permute-start = (bf16[384,64]{1,0:T(8,128)(2,1)S(1)}, bf16[384,64]{1,0:T(8,128)(2,1)S(1)}, u32[]{:S(2)}, u32[]{:S(2)}) collective-permute-start(bf16[384,64]{1,0:T(8,128)(2,1)S(1)} %low_partial.1), channel_id=1, source_target_pairs={{0,1},{1,0},{2,3},{3,2},{4,5},{5,4},{6,7},{7,6},{8,9},{9,8},{10,11... | collective-permute-start | bytes 147464 | tf_op jit(solution)/shard_map/low/psum_pipe/ppermute | solution.py:298
  33.0 4.9 %collective-permute-start.1 = (bf16[384,64]{1,0:T(8,128)(2,1)S(1)}, bf16[384,64]{1,0:T(8,128)(2,1)S(1)}, u32[]{:S(2)}, u32[]{:S(2)}) collective-permute-start(bf16[384,64]{1,0:T(8,128)(2,1)S(1)} %add_convert_fusion.1.here_ref), channel_id=1, source_target_pairs={{0,2},{2,0},{1,3},{3,1},{4,6},{6,4},{5,7},{7,5},{8,10},{10,8},{9,1... | collective-permute-start | bytes 147464 | tf_op jit(solution)/shard_map/low/psum_tensor/ppermute | solution.py:298
  34.6 19.4 %collective-permute-start.6 = (bf16[256,1024]{1,0:T(8,128)(2,1)}, bf16[256,1024]{1,0:T(8,128)(2,1)}, u32[]{:S(2)}, u32[]{:S(2)}) collective-permute-start(bf16[256,1024]{1,0:T(8,128)(2,1)} %collective-permute-done.2.refs_4_), channel_id=1, source_target_pairs={{4,8},{8,4},{5,9},{9,5},{6,10},{10,6},{7,11},{11,7},{20,24},{24,20... | collective-permute-start | bytes 1572872 | tf_op jit(solution)/shard_map/line_2_1/ppermute | solution.py:345
  45.2 1.0 copy-start.6
  46.2 59.6 %all-to-all-start.2 = ((bf16[4,64,2048]{2,1,0:T(8,128)(2,1)}), bf16[4,64,2048]{2,1,0:T(8,128)(2,1)}, u32[]{:S(2)}, u32[]{:S(2)}) async-start(bf16[4,64,2048]{2,1,0:T(8,128)(2,1)} %copy-done.6), calls=%async_computation.2 | async-start | bytes 2097152 | tf_op jit(solution)/shard_map/low/all_to_all | solution.py:365
  50.5 45.3 %copy-start.1 = (bf16[256,2048]{1,0:T(8,128)(2,1)S(1)}, bf16[256,2048]{1,0:T(8,128)(2,1)}, u32[]{:S(2)}) copy-start(bf16[256,2048]{1,0:T(8,128)(2,1)} %refs_3_.3) | copy-start | bytes 3145732
  50.5 29.9 %collective-permute-start.5 = (bf16[256,1024]{1,0:T(8,128)(2,1)}, bf16[256,1024]{1,0:T(8,128)(2,1)}, u32[]{:S(2)}, u32[]{:S(2)}) collective-permute-start(bf16[256,1024]{1,0:T(8,128)(2,1)} %collective-permute-done.3.refs_5_), channel_id=1, source_target_pairs={{4,0},{8,12},{5,1},{9,13},{6,2},{10,14},{7,3},{11,15},{20,16},{24,... | collective-permute-start | bytes 1572872 | tf_op jit(solution)/shard_map/line_2_0/ppermute | solution.py:345
  51.9 30.0 %collective-permute-start.7 = (bf16[256,1024]{1,0:T(8,128)(2,1)}, bf16[256,1024]{1,0:T(8,128)(2,1)S(1)}, u32[]{:S(2)}, u32[]{:S(2)}) collective-permute-start(bf16[256,1024]{1,0:T(8,128)(2,1)} %collective-permute-done.2.refs_4_), channel_id=1, source_target_pairs={{4,20},{0,16},{12,28},{8,24},{20,4},{16,0},{28,12},{24,8},{5,21},{... | collective-permute-start | bytes 1572872 | tf_op jit(solution)/shard_map/swap_w/ppermute | solution.py:355
  53.5 32.6 %collective-permute-start.4 = (bf16[4,64,1024]{2,1,0:T(8,128)(2,1)S(1)}, bf16[4,64,1024]{2,1,0:T(8,128)(2,1)S(1)}, u32[]{:S(2)}, u32[]{:S(2)}) collective-permute-start(bf16[4,64,1024]{2,1,0:T(8,128)(2,1)S(1)} %all-to-all-done.1.refs_2_.mine_ref), channel_id=1, source_target_pairs={{0,16},{16,0},{1,17},{17,1},{2,18},{18,2},{3,19},{19,3},{4,20},{20... | collective-permute-start | bytes 1572872 | tf_op jit(solution)/shard_map/swap_a/ppermute | solution.py:368
  54.0 35.6 %collective-permute-start.11 = (bf16[256,1024]{1,0:T(8,128)(2,1)}, bf16[256,1024]{1,0:T(8,128)(2,1)}, u32[]{:S(2)}, u32[]{:S(2)}) collective-permute-start(bf16[256,1024]{1,0:T(8,128)(2,1)} %collective-permute-done.6.refs_7_), channel_id=1, source_target_pairs={{4,0},{8,12},{5,1},{9,13},{6,2},{10,14},{7,3},{11,15},{20,16},{24,... | collective-permute-start | bytes 1572872 | tf_op jit(solution)/shard_map/line_3_0/ppermute | solution.py:345
  55.3 45.5 %collective-permute-start.8 = (bf16[256,1024]{1,0:T(8,128)(2,1)}, bf16[256,1024]{1,0:T(8,128)(2,1)}, u32[]{:S(2)}, u32[]{:S(2)}) collective-permute-start(bf16[256,1024]{1,0:T(8,128)(2,1)} %collective-permute-done.3.refs_5_), channel_id=1, source_target_pairs={{8,24},{4,20},{24,8},{20,4},{9,25},{5,21},{25,9},{21,5},{10,26},{6... | collective-permute-start | bytes 1572872 | tf_op jit(solution)/shard_map/swap_w/ppermute | solution.py:355
  80.4 20.4 %collective-permute-start.10 = (bf16[256,1024]{1,0:T(8,128)(2,1)}, bf16[256,1024]{1,0:T(8,128)(2,1)}, u32[]{:S(2)}, u32[]{:S(2)}) collective-permute-start(bf16[256,1024]{1,0:T(8,128)(2,1)} %collective-permute-done.6.refs_7_), channel_id=1, source_target_pairs={{8,24},{4,20},{24,8},{20,4},{9,25},{5,21},{25,9},{21,5},{10,26},{6... | collective-permute-start | bytes 1572872 | tf_op jit(solution)/shard_map/swap_w/ppermute | solution.py:355
  81.9 0.8 copy-start.7
  82.7 18.2 %collective-permute-start.9 = (bf16[256,1024]{1,0:T(8,128)(2,1)}, bf16[256,1024]{1,0:T(8,128)(2,1)}, u32[]{:S(2)}, u32[]{:S(2)}) collective-permute-start(bf16[256,1024]{1,0:T(8,128)(2,1)} %collective-permute-done.5.refs_6_), channel_id=1, source_target_pairs={{0,16},{12,28},{16,0},{28,12},{1,17},{13,29},{17,1},{29,13},{2,18}... | collective-permute-start | bytes 1572872 | tf_op jit(solution)/shard_map/swap_w/ppermute | solution.py:355
  86.1 1.4 %copy-start.3 = (bf16[384,2048]{1,0:T(8,128)(2,1)S(1)}, bf16[384,2048]{1,0:T(8,128)(2,1)}, u32[]{:S(2)}) copy-start(bf16[384,2048]{1,0:T(8,128)(2,1)} %x_ref.3) | copy-start | bytes 4718596
  88.7 4.6 %collective-permute-start.13 = (bf16[384,64]{1,0:T(8,128)(2,1)S(1)}, bf16[384,64]{1,0:T(8,128)(2,1)}, u32[]{:S(2)}, u32[]{:S(2)}) collective-permute-start(bf16[384,64]{1,0:T(8,128)(2,1)S(1)} %hidden_partial.1), channel_id=1, source_target_pairs={{0,1},{1,0},{2,3},{3,2},{4,5},{5,4},{6,7},{7,6},{8,9},{9,8},{10,11... | collective-permute-start | bytes 147464 | tf_op jit(solution)/shard_map/hidden/psum_pipe/ppermute | solution.py:298
  89.6 21.2 %collective-permute-start.12 = (bf16[256,1024]{1,0:T(8,128)(2,1)}, bf16[256,1024]{1,0:T(8,128)(2,1)}, u32[]{:S(2)}, u32[]{:S(2)}) collective-permute-start(bf16[256,1024]{1,0:T(8,128)(2,1)} %collective-permute-done.11.refs_8_), channel_id=1, source_target_pairs={{0,16},{12,28},{16,0},{28,12},{1,17},{13,29},{17,1},{29,13},{2,18}... | collective-permute-start | bytes 1572872 | tf_op jit(solution)/shard_map/swap_w/ppermute | solution.py:355
  94.3 11.6 %collective-permute-start.14 = (bf16[384,64]{1,0:T(8,128)(2,1)S(1)}, bf16[384,64]{1,0:T(8,128)(2,1)S(1)}, u32[]{:S(2)}, u32[]{:S(2)}) collective-permute-start(bf16[384,64]{1,0:T(8,128)(2,1)S(1)} %add_convert_fusion.here_ref), channel_id=1, source_target_pairs={{0,2},{2,0},{1,3},{3,1},{4,6},{6,4},{5,7},{7,5},{8,10},{10,8},{9,1... | collective-permute-start | bytes 147464 | tf_op jit(solution)/shard_map/hidden/psum_tensor/ppermute | solution.py:298
  95.8 5.1 %copy-start.8 = (bf16[256,1024]{1,0:T(8,128)(2,1)S(1)}, bf16[256,1024]{1,0:T(8,128)(2,1)}, u32[]{:S(2)}) copy-start(bf16[256,1024]{1,0:T(8,128)(2,1)} %copy-done.7) | copy-start | bytes 1572868
  104.6 1.2 %copy-start.4 = (f32[384,1024]{1,0:T(8,128)}, f32[384,1024]{1,0:T(8,128)S(1)}, u32[]{:S(2)}) copy-start(f32[384,1024]{1,0:T(8,128)S(1)} %product.3.refs_1_) | copy-start | bytes 4718596
  107.3 10.3 %all-to-all-start.3 = ((bf16[4,64,256]{2,1,0:T(8,128)(2,1)}), bf16[4,64,256]{2,1,0:T(8,128)(2,1)S(1)}, u32[]{:S(2)}, u32[]{:S(2)}) async-start(bf16[4,64,256]{2,1,0:T(8,128)(2,1)} %up_table.1), calls=%async_computation.3 | async-start | bytes 262144 | tf_op jit(solution)/shard_map/hidden/all_to_all | solution.py:376
  110.9 1.4 %copy-start.5 = (f32[384,1024]{1,0:T(8,128)S(1)}, f32[384,1024]{1,0:T(8,128)}, u32[]{:S(2)}) copy-start(f32[384,1024]{1,0:T(8,128)} %copy-done.4) | copy-start | bytes 4718596

commit v5 on v4

v5 whole, which is shorter than its diff:
```python
import functools

import jax
import jax.numpy as jnp
from jax import lax
from jax.experimental import pallas as pl
from jax.experimental.pallas import tpu as pltpu
from jax.sharding import PartitionSpec as P

SCALE = 2.0
VMEM_LIMIT = 48 << 20
F32 = jnp.float32
BF16 = jnp.bfloat16


ROWS_BY_ROWS = (((1,), (1,)), ((), ()))
COLUMNS_BY_COLUMNS = (((0,), (0,)), ((), ()))


def payload_kernel(scalars, down_ref, up_ref, out_ref):
    owned, _, part = down_ref.shape
    for k in range(out_ref.shape[0] // owned):
        span = slice(k * owned, (k + 1) * owned)
        out_ref[span, :, :part] = down_ref[...]
        out_ref[span, :, part:] = up_ref[...]


def project_kernel(blocks, scalars, x_ref, w_ref, mine_ref, other_ref, up_ref, out_ref):
    rows = x_ref.shape[0] // blocks
    rank, part = mine_ref.shape[1:]

    def run(first, second):
        for b in range(blocks):
            s = scalars[b]
            span = slice(b * rows, (b + 1) * rows)
            hidden = lax.dot_general(
                x_ref[span, :part], first[s], ROWS_BY_ROWS, preferred_element_type=F32
            ) + lax.dot_general(
                x_ref[span, part:], second[s], ROWS_BY_ROWS, preferred_element_type=F32
            )
            low = lax.dot_general(
                w_ref[span, :], up_ref[s], ROWS_BY_ROWS, preferred_element_type=F32
            )
            out_ref[span, :rank] = hidden.astype(BF16)
            out_ref[span, rank:] = low.astype(BF16)

    @pl.when(scalars[blocks] == 0)
    def _():
        run(mine_ref, other_ref)

    @pl.when(scalars[blocks] != 0)
    def _():
        run(other_ref, mine_ref)


def grads_kernel(blocks, scalars, x_ref, w_ref, here_ref, there_ref, table_ref, low_ref, acc_ref):
    rows, width = x_ref.shape[0] // blocks, x_ref.shape[1]
    rank = low_ref.shape[1]
    total = here_ref[...].astype(F32) + there_ref[...].astype(F32)
    hidden_b = total[:, :rank].astype(BF16)
    low_b = (SCALE * total[:, rank:]).astype(BF16)
    low_ref[...] = low_b
    acc_ref[...] = jnp.zeros_like(acc_ref)
    for b in range(blocks):
        s = scalars[b]
        span = slice(b * rows, (b + 1) * rows)
        acc_ref[s, :, :width] += lax.dot_general(
            low_b[span], x_ref[span, :], COLUMNS_BY_COLUMNS, preferred_element_type=F32
        )
        acc_ref[s, :, width:] += SCALE * lax.dot_general(
            hidden_b[span], w_ref[span, :], COLUMNS_BY_COLUMNS, preferred_element_type=F32
        )
    table_ref[...] = acc_ref[...].astype(BF16)


def sum_kernel(got_ref, down_ref, up_ref):
    count = got_ref.shape[0] // down_ref.shape[0]
    owned, _, width = down_ref.shape
    total = got_ref[:owned].astype(F32)
    for k in range(1, count):
        total += got_ref[k * owned : (k + 1) * owned].astype(F32)
    down_ref[...] = total[:, :, :width]
    up_ref[...] = total[:, :, width:]


def product_kernel(
    blocks, tiles, scalars, weighted_ref, low_ref, down_ref, own_ref, *refs
):
    out_ref, whole_ref, sems = refs[-3:]
    part = whole_ref.shape[1]
    tile = part // tiles
    pieces = refs[: scalars.shape[0] - blocks - 2]
    half = scalars[blocks]
    rows = weighted_ref.shape[0] // blocks

    def each(t, act):
        columns = pl.ds(t * tile, tile)
        own_columns = pl.ds(pl.multiple_of(half * part + t * tile, 128), tile)
        for j, source in enumerate([own_ref.at[:, own_columns]] + [p.at[:, columns] for p in pieces]):
            begin = scalars[blocks + 1 + j]

            def run(j=j, source=source, begin=begin):
                place = pl.ds(pl.multiple_of(begin, 16), source.shape[0])
                copy = pltpu.make_async_copy(source, whole_ref.at[place, columns], sems.at[t, j])
                copy.start() if act == "start" else copy.wait()

            if j:
                pl.when(begin >= 0)(run)
            else:
                run()

    for t in range(tiles):
        each(t, "start")
    for t in range(tiles):
        each(t, "wait")
        columns = slice(t * tile, (t + 1) * tile)
        total = jnp.dot(weighted_ref[...], whole_ref[:, columns], preferred_element_type=F32)
        for b in range(blocks):
            span = slice(b * rows, (b + 1) * rows)
            term = jnp.dot(
                low_ref[span, :], down_ref[scalars[b], :, columns], preferred_element_type=F32
            )
            out_ref[span, columns] = (total[span] + term).astype(BF16)


def product(half, slots, begins, weighted, low_b, down, own, pieces, into=None):
    rows = weighted.shape[0]
    width = own.shape[1]
    part = width // 2
    tiles = 2 if part % 256 == 0 else 1
    blocks = slots.shape[0]
    whole = lambda i, s: (0, 0)
    specs = [
        pl.BlockSpec(weighted.shape, whole),
        pl.BlockSpec(low_b.shape, whole),
        pl.BlockSpec((*down.shape[:2], part), lambda i, s: (0, 0, 0)),
    ] + [pl.BlockSpec(memory_space=pl.ANY) for _ in [own, *pieces]]
    operands = [weighted, low_b, down, own, *pieces]
    aliases = {}
    if into is not None:
        specs.append(pl.BlockSpec(memory_space=pl.ANY))
        operands.append(into)
        aliases = {len(operands): 0}
    return pl.pallas_call(
        functools.partial(product_kernel, blocks, tiles),
        out_shape=bf16(rows, width),
        grid_spec=pltpu.PrefetchScalarGridSpec(
            num_scalar_prefetch=1,
            grid=(1,),
            in_specs=specs,
            out_specs=pl.BlockSpec((rows, part), lambda i, s: (0, s[blocks])),
            scratch_shapes=[
                pltpu.VMEM((weighted.shape[1], part), BF16),
                pltpu.SemaphoreType.DMA((tiles, len(pieces) + 1)),
            ],
        ),
        input_output_aliases=aliases,
        compiler_params=pltpu.CompilerParams(vmem_limit_bytes=VMEM_LIMIT),
        cost_estimate=pl.CostEstimate(
            flops=24 * rows * part * weighted.shape[1],
            bytes_accessed=2 * part * (weighted.shape[1] + rows),
            transcendentals=0,
        ),
        name="product",
    )(jnp.stack([*slots, half, *begins]), *operands)


def call(kernel, name, out_shape, scalars, operands, specs=None, scratch=(), flops=0, moved=0):
    whole = lambda shape: pl.BlockSpec(shape, lambda i, s: (0,) * len(shape))
    specs = specs or [whole(o.shape) for o in operands]
    single = isinstance(out_shape, jax.ShapeDtypeStruct)
    return pl.pallas_call(
        kernel,
        out_shape=out_shape,
        grid_spec=pltpu.PrefetchScalarGridSpec(
            num_scalar_prefetch=1,
            grid=(1,),
            in_specs=specs,
            out_specs=whole(out_shape.shape) if single else [whole(o.shape) for o in out_shape],
            scratch_shapes=list(scratch),
        ),
        compiler_params=pltpu.CompilerParams(vmem_limit_bytes=VMEM_LIMIT),
        cost_estimate=pl.CostEstimate(flops=flops, bytes_accessed=moved, transcendentals=0),
        name=name,
    )(scalars, *operands)


def bf16(*shape):
    return jax.ShapeDtypeStruct(shape, BF16)


def payload(group, down, up, n):
    owned, rank, width = down.shape
    slab, part = up.shape[2], width // 2
    specs = [
        pl.BlockSpec((owned, rank, part), lambda i, s: (0, 0, s[0])),
        pl.BlockSpec((owned, rank, slab), lambda i, s: (0, 0, 0)),
    ]
    shape = bf16(n * owned, rank, part + slab)
    return call(payload_kernel, "payload", shape, group[None], [down, up], specs)


def project(group, slab_index, slots, x, weighted, received, other):
    rows, width = x.shape
    tenants, rank, part = other.shape
    slab = received.shape[2] - part
    blocks = slots.shape[0]
    whole = lambda i, s: (0, 0, 0)
    specs = [
        pl.BlockSpec((rows, width), lambda i, s: (0, 0)),
        pl.BlockSpec((rows, slab), lambda i, s: (0, s[blocks + 1])),
        pl.BlockSpec((tenants, rank, part), whole),
        pl.BlockSpec((tenants, rank, part), whole),
        pl.BlockSpec((tenants, rank, slab), lambda i, s: (0, 0, part // slab)),
    ]
    return call(
        functools.partial(project_kernel, blocks),
        "project",
        bf16(rows, 2 * rank),
        jnp.stack([*slots, group, slab_index]),
        [x, weighted, received, other, received],
        specs,
        flops=2 * rows * rank * (width + slab),
        moved=2 * (rows + tenants * rank) * (width + slab),
    )


def adapter_grads(slab_index, slots, x, weighted, here, there, tenants, slab):
    rows, width = x.shape
    rank = here.shape[1] // 2
    blocks = slots.shape[0]
    ranks = pl.BlockSpec((rows, 2 * rank), lambda i, s: (0, 0))
    specs = [
        pl.BlockSpec((rows, width), lambda i, s: (0, 0)),
        pl.BlockSpec((rows, slab), lambda i, s: (0, s[blocks])),
        ranks,
        ranks,
    ]
    return call(
        functools.partial(grads_kernel, blocks),
        "adapter_grads",
        (bf16(tenants, rank, width + slab), bf16(rows, rank)),
        jnp.stack([*slots, slab_index]),
        [x, weighted, here, there],
        specs,
        scratch=[pltpu.VMEM((tenants, rank, width + slab), F32)],
        flops=2 * rows * rank * (width + slab),
        moved=2 * (rows + tenants * rank) * (width + slab),
    )


def owner_sums(got, n, width):
    tenants, rank, both = got.shape
    owned = tenants // n
    return pl.pallas_call(
        sum_kernel,
        out_shape=(
            jax.ShapeDtypeStruct((owned, rank, width), F32),
            jax.ShapeDtypeStruct((owned, rank, both - width), F32),
        ),
        compiler_params=pltpu.CompilerParams(vmem_limit_bytes=VMEM_LIMIT),
        cost_estimate=pl.CostEstimate(
            flops=got.size, bytes_accessed=2 * got.size, transcendentals=0
        ),
        name="owner_sums",
    )(got)


def edge_pairs(parity, k, n):
    pairs = []
    for i in range(parity, n - 1, 2):
        if i >= k - 1:
            pairs.append((i, i + 1))
        if i + 1 <= n - k:
            pairs.append((i + 1, i))
    return pairs


def swap_pairs(pairs, n, groups):
    targets = [b for _, b in pairs]
    return [(g * n + t, (groups - 1 - g) * n + t) for g in range(groups) for t in targets]


def after(value, *others):
    return lax.optimization_barrier((value, others))[0]


def pair_sum(value):
    return (value.astype(F32) + rest_of(value, "pipe")).astype(BF16)


def rest_of(value, axis):
    size = lax.axis_size(axis)
    rest = 0.0
    for d in range(1, size):
        pairs = [(i, (i + d) % size) for i in range(size)]
        with jax.named_scope(f"psum_{axis}"):
            rest = rest + lax.ppermute(value, axis, pairs).astype(F32)
    return rest


def per_device(
    sizes,
    layer_input,
    out_grad,
    value_weight,
    adapter_down,
    adapter_up,
    block_tenant,
    tenant_slot,
    forget_flag,
):
    n, groups = sizes
    token_rows, width = layer_input.shape
    rank = adapter_down.shape[1]
    slab = adapter_up.shape[2]
    tenants = tenant_slot.shape[0]
    depth = value_weight.shape[0]
    swap = lambda axis: functools.partial(lax.ppermute, axis_name=axis, perm=[(0, 1), (1, 0)])

    half = width // 2
    group = lax.axis_index("groups").astype(jnp.int32)
    me = lax.axis_index("seq").astype(jnp.int32)
    slab_index = lax.axis_index(("tensor", "pipe")).astype(jnp.int32)
    columns = lambda a: lax.dynamic_slice_in_dim(a, group * half, half, a.ndim - 1)

    with jax.named_scope("adapters"):
        received = lax.all_to_all(
            payload(group, adapter_down, adapter_up, n),
            "seq",
            split_axis=0,
            concat_axis=0,
            tiled=True,
        )
    with jax.named_scope("swap_a"):
        down_other = swap("groups")(received[:, :, :half])

    row_sign = (1 - 2 * forget_flag).astype(BF16)
    weighted = out_grad * row_sign[:, None]
    tenant_ids = jnp.arange(tenants, dtype=jnp.int32)
    slots = jnp.sum(
        jnp.where(block_tenant == tenant_ids[None, :], tenant_slot[None, :], 0), axis=1
    ).astype(jnp.int32)

    depth = value_weight.shape[0]
    arrived, begins, pairs_of = [], [me * depth], []

    def advance(k, last, *before):
        last, new = after(last, before), [None, None]
        for parity in (0, 1):
            pairs = edge_pairs(parity, k, n)
            if not pairs:
                continue
            owner = jnp.where(me % 2 != parity, me - k, me + k)
            with jax.named_scope(f"line_{k}_{parity}"):
                new[parity] = lax.ppermute(last[1 - parity], "seq", pairs)
            arrived.append(new[parity])
            pairs_of.append(pairs)
            begins.append(jnp.where((owner >= 0) & (owner < n), owner * depth, -1))
        return new

    def exchange(j, *before):
        with jax.named_scope(f"swap_w_{j}"):
            return lax.ppermute(
                after(arrived[j], before), ("groups", "seq"), swap_pairs(pairs_of[j], n, groups)
            )

    last = advance(1, [columns(value_weight)] * 2)
    for k in range(2, n - 1):
        last = advance(k, last, received)
    with jax.named_scope("ranks"):
        part = project(group, slab_index, slots, layer_input, weighted, received, down_other)
        here = pair_sum(part)
        advance(n - 1, last, here)
        there = rest_of(here, "tensor").astype(BF16)
        table, low_b = adapter_grads(
            slab_index, slots, layer_input, weighted, here, there, tenants, slab
        )
        got = lax.all_to_all(table, "seq", split_axis=0, concat_axis=0, tiled=True)
    swapped = []
    for j in range(len(arrived)):
        before = [down_other] if j < 2 else [table] if j < 4 else []
        swapped.append(exchange(j, *before))

    common = (slots, begins, weighted, low_b)
    first = product(group, *common, received, value_weight, arrived)
    full = product(1 - group, *common, down_other, value_weight, swapped, first)
    down_grad, up_grad = owner_sums(got, n, width)
    return full, down_grad, up_grad


def solution(mesh):
    sizes = (mesh.shape["seq"], mesh.shape["groups"])
    return jax.shard_map(
        functools.partial(per_device, sizes),
        mesh=mesh,
        in_specs=(
            P(("groups", "seq"), ("tensor", "pipe")),
            P(("groups", "seq"), None),
            P("seq", ("tensor", "pipe")),
            P("seq", None, ("tensor", "pipe")),
            P("seq", None, ("tensor", "pipe")),
            P(("groups", "seq"), None),
            P(),
            P(("groups", "seq")),
        ),
        out_specs=(
            P(("groups", "seq"), ("tensor", "pipe")),
            P(("groups", "seq"), None, ("tensor", "pipe")),
            P(("groups", "seq"), None, ("tensor", "pipe")),
        ),
        check_vma=False,
    )
```

time: 119 us -> 99.5 us (0.84)
  starting transfers between devices: 40.4 us -> 33.8 us
  other arithmetic: 6.22 us -> 2.26 us
  Pallas kernels: 16.2 us -> 12.3 us
  local copies, waits for them, and re-layouts: 10.1 us -> 7.4 us
  waiting for transfers between devices: 44.3 us -> 42.2 us
    pallas_call x3, Pallas kernels: 11.8 us -> 8.85 us  [the longest x2 7.92 us: product(): pl.pallas_call(functools.partial(product_kernel, blocks, tiles), out_shap...]
    all_to_all x4 -> x2, starting transfers between devices: 16.6 us -> 13.7 us  [the longest x1 7.26 us: per_device(): got = lax.all_to_all(table, 'seq', split_axis=0, concat_axis=0, tiled=True)]
    reduce_sum x2 -> x0, other arithmetic: 2.87 us -> none  [owner_sum(): return jnp.sum(got.astype(F32).reshape(n, owned, *got.shape[1:]), axis=0)]
    all_to_all x4 -> x2, waiting for transfers between devices: 16.6 us -> 14 us  [the longest x1 14 us: per_device(): lax.all_to_all(payload(group, adapter_down, adapter_up, n), 'seq', split_...]
    reshape x2 -> x0, local copies, waits for them, and re-layouts: 2.27 us -> none  [everyone(): jnp.broadcast_to(value, (n,) + value.shape).reshape(-1, *value.shape[1:])]
    ppermute x11, waiting for transfers between devices: 24.5 us -> 26.6 us  [the longest x5 13 us: exchange(): lax.ppermute(after(arrived[j], before), ('groups', 'seq'), swap_pairs(pai...]
    ppermute x11, starting transfers between devices: 20.5 us -> 18.5 us  [the longest x5 9.51 us: exchange(): lax.ppermute(after(arrived[j], before), ('groups', 'seq'), swap_pairs(pai...]
    ppermute x4 -> x2, starting transfers between devices: 3.27 us -> 1.57 us  [rest_of(): rest = rest + lax.ppermute(value, axis, pairs).astype(F32)]
  transfers between devices with their start and end apart: 19 -> 15, of which waited for: 6 -> 8; matrix products, arithmetic and copies ran while one was open for 7% -> 4% of each run, Pallas kernels for 14% -> 11%
where the time goes in v5:
time: 99.5 us; the launch traced here: 98.8 us
  waiting for transfers between devices  42.2 us (42%)
  starting transfers between devices  33.8 us (34%)
  Pallas kernels  12.3 us (12%)
  local copies, waits for them, and re-layouts  7.4 us (7%)
  other arithmetic  2.26 us (2%)
    all_to_all x1, waiting for transfers between devices, per_device(): lax.all_to_all(payload(group, adapter_down, adapter_up, n), 'seq', split_...  14 us
    ppermute x5, waiting for transfers between devices, exchange(): lax.ppermute(after(arrived[j], before), ('groups', 'seq'), swap_pairs(pai...  13 us
    ppermute x5, waiting for transfers between devices, advance(): new[parity] = lax.ppermute(last[1 - parity], 'seq', pairs)  9.61 us
    ppermute x5, starting transfers between devices, exchange(): lax.ppermute(after(arrived[j], before), ('groups', 'seq'), swap_pairs(pai...  9.51 us
    pallas_call x2, Pallas kernels, product(): pl.pallas_call(functools.partial(product_kernel, blocks, tiles), out_shap...  7.92 us
    ppermute x5, starting transfers between devices, advance(): new[parity] = lax.ppermute(last[1 - parity], 'seq', pairs)  7.5 us
    all_to_all x1, starting transfers between devices, per_device(): got = lax.all_to_all(table, 'seq', split_axis=0, concat_axis=0, tiled=True)  7.26 us
    all_to_all x1, starting transfers between devices, per_device(): lax.all_to_all(payload(group, adapter_down, adapter_up, n), 'seq', split_...  6.45 us
  transfers between devices with their start and end apart: 15, of which 8 were waited for; matrix products, arithmetic and copies ran while one was open for 4% of the time, Pallas kernels for 11%

profile of v5, /device:TPU:0, one launch (start us, length us, event | category | flops | bytes accessed | tf_op | source)
XLA Modules:
  0.0 98.8 jit_solution(6386493590899421167)
XLA Ops:
  0.6 0.0 copy-start.3
  0.6 0.9 copy-done.3
  1.6 0.0 copy-start.6
  1.6 0.8 copy-done.6
  2.3 0.0 copy-start.4
  2.3 0.9 payload.1
  3.2 0.0 copy-start.9
  3.2 6.4 %all-to-all-start = ((bf16[4,64,1280]{2,1,0:T(8,128)(2,1)}), bf16[4,64,1280]{2,1,0:T(8,128)(2,1)S(1)}, u32[]{:S(2)}, u32[]{:S(2)}) async-start(bf16[4,64,1280]{2,1,0:T(8,128)(2,1)} %payload.1), calls=%async_computation | async-start | bytes 1310720 | tf_op jit(solution)/shard_map/adapters/all_to_all | solution.py:328
  9.7 0.0 copy-done.4
  9.7 0.9 constant_dynamic-slice_fusion
  10.5 0.0 copy-start.10
  10.5 2.0 %collective-permute-start.3 = (bf16[256,1024]{1,0:T(8,128)(2,1)}, bf16[256,1024]{1,0:T(8,128)(2,1)}, u32[]{:S(2)}, u32[]{:S(2)}) collective-permute-start(bf16[256,1024]{1,0:T(8,128)(2,1)} %constant_dynamic-slice_fusion), channel_id=1, source_target_pairs={{0,4},{4,0},{8,12},{12,8},{1,5},{5,1},{9,13},{13,9},{2,6},{6,2},{1... | collective-permute-start | bytes 1572872 | tf_op jit(solution)/shard_map/line_1_0/ppermute | solution.py:356
  12.6 1.4 %collective-permute-start.5 = (bf16[256,1024]{1,0:T(8,128)(2,1)}, bf16[256,1024]{1,0:T(8,128)(2,1)}, u32[]{:S(2)}, u32[]{:S(2)}) collective-permute-start(bf16[256,1024]{1,0:T(8,128)(2,1)} %constant_dynamic-slice_fusion), channel_id=1, source_target_pairs={{4,8},{8,4},{5,9},{9,5},{6,10},{10,6},{7,11},{11,7},{20,24},{24,20... | collective-permute-start | bytes 1572872 | tf_op jit(solution)/shard_map/line_1_1/ppermute | solution.py:356
  14.0 14.0 %all-to-all-done.mine_ref.up_ref.down_ref = bf16[4,64,1280]{2,1,0:T(8,128)(2,1)S(1)} async-done(((bf16[4,64,1280]{2,1,0:T(8,128)(2,1)}), bf16[4,64,1280]{2,1,0:T(8,128)(2,1)S(1)}, u32[]{:S(2)}, u32[]{:S(2)}) %all-to-all-start) | async-done | bytes 655392 | tf_op jit(solution)/shard_map/adapters/all_to_all | solution.py:328
  28.0 0.9 slice.8
  28.9 1.5 %collective-permute-start = (bf16[4,64,1024]{2,1,0:T(8,128)(2,1)}, bf16[4,64,1024]{2,1,0:T(8,128)(2,1)S(1)}, u32[]{:S(2)}, u32[]{:S(2)}) collective-permute-start(bf16[4,64,1024]{2,1,0:T(8,128)(2,1)} %slice.8), channel_id=1, source_target_pairs={{0,16},{16,0},{1,17},{17,1},{2,18},{18,2},{3,19},{19,3},{4,20},{20... | collective-permute-start | bytes 1572872 | tf_op jit(solution)/shard_map/swap_a/ppermute | solution.py:336
  30.4 0.0 copy-done.9
  30.4 1.2 %broadcast_multiply_fusion.w_ref.weighted_ref = bf16[384,1024]{1,0:T(8,128)(2,1)S(1)} fusion(bf16[384,1024]{1,0:T(8,128)(2,1)} %param.9, bf16[384]{0:T(512)(128)(2,1)S(1)} %subtract_convert_fusion), kind=kLoop, calls=%fused_computation | loop fusion | flops 393216 | bytes 1573632 | tf_op jit(solution)/shard_map/mul | solution.py:339
  31.7 2.2 %collective-permute-done.3.refs_0_ = bf16[256,1024]{1,0:T(8,128)(2,1)} collective-permute-done((bf16[256,1024]{1,0:T(8,128)(2,1)}, bf16[256,1024]{1,0:T(8,128)(2,1)}, u32[]{:S(2)}, u32[]{:S(2)}) %collective-permute-start.3) | collective-permute-done | bytes 524320 | tf_op jit(solution)/shard_map/line_1_0/ppermute | solution.py:356
  33.9 0.0 collective-permute-done.5.refs_1_
  33.9 1.3 %collective-permute-start.7 = (bf16[256,1024]{1,0:T(8,128)(2,1)}, bf16[256,1024]{1,0:T(8,128)(2,1)}, u32[]{:S(2)}, u32[]{:S(2)}) collective-permute-start(bf16[256,1024]{1,0:T(8,128)(2,1)} %collective-permute-done.5.refs_1_), channel_id=1, source_target_pairs={{4,0},{8,12},{5,1},{9,13},{6,2},{10,14},{7,3},{11,15},{20,16},{24,... | collective-permute-start | bytes 1572872 | tf_op jit(solution)/shard_map/line_2_0/ppermute | solution.py:356
  35.2 1.5 %collective-permute-start.9 = (bf16[256,1024]{1,0:T(8,128)(2,1)}, bf16[256,1024]{1,0:T(8,128)(2,1)}, u32[]{:S(2)}, u32[]{:S(2)}) collective-permute-start(bf16[256,1024]{1,0:T(8,128)(2,1)} %collective-permute-done.3.refs_0_), channel_id=1, source_target_pairs={{4,8},{8,4},{5,9},{9,5},{6,10},{10,6},{7,11},{11,7},{20,24},{24,20... | collective-permute-start | bytes 1572872 | tf_op jit(solution)/shard_map/line_2_1/ppermute | solution.py:356
  36.7 0.0 copy-done.10
  36.7 0.0 copy-done.11
  36.7 0.2 select_reduce_fusion
  36.8 0.1 pad_add_fusion.1.scalars
  36.9 4.0 %collective-permute-done.other_ref.down_ref = bf16[4,64,1024]{2,1,0:T(8,128)(2,1)S(1)} collective-permute-done((bf16[4,64,1024]{2,1,0:T(8,128)(2,1)}, bf16[4,64,1024]{2,1,0:T(8,128)(2,1)S(1)}, u32[]{:S(2)}, u32[]{:S(2)}) %collective-permute-start) | collective-permute-done | bytes 524320 | tf_op jit(solution)/shard_map/swap_a/ppermute | solution.py:336
  40.9 0.0 copy-done
  40.9 1.3 %project.1 = bf16[384,128]{1,0:T(8,128)(2,1)S(1)} custom-call(s32[5]{0:T(128)S(1)} %pad_add_fusion.1.scalars, bf16[384,2048]{1,0:T(8,128)(2,1)S(1)} %copy-done, bf16[384,1024]{1,0:T(8,128)(2,1)S(1)} %broadcast_multiply_fusion.w_ref.weighted_ref, bf16[4,64,1280]{2,1,0:T(8,128)(2,1)S(1)} %all-to-all-done.mine_ref.up_ref.down_ref, ...), custom_call_target="tpu_custom_call" | custom-call | flops 113246208 | bytes 2949120 | tf_op jit(solution)/shard_map/ranks/project/pallas_call | solution.py:172
  42.2 0.1 collective-permute-start.1
  42.3 1.3 %collective-permute-done.1 = bf16[384,128]{1,0:T(8,128)(2,1)S(1)} collective-permute-done((bf16[384,128]{1,0:T(8,128)(2,1)S(1)}, bf16[384,128]{1,0:T(8,128)(2,1)S(1)}, u32[]{:S(2)}, u32[]{:S(2)}) %collective-permute-start.1) | collective-permute-done | bytes 98336 | tf_op jit(solution)/shard_map/ranks/psum_pipe/ppermute | solution.py:298
  43.6 0.7 add_convert_fusion.here_ref
  44.2 7.4 %collective-permute-done.7.refs_2_ = bf16[256,1024]{1,0:T(8,128)(2,1)} collective-permute-done((bf16[256,1024]{1,0:T(8,128)(2,1)}, bf16[256,1024]{1,0:T(8,128)(2,1)}, u32[]{:S(2)}, u32[]{:S(2)}) %collective-permute-start.7) | collective-permute-done | bytes 524320 | tf_op jit(solution)/shard_map/line_2_0/ppermute | solution.py:356
  51.6 0.0 collective-permute-done.9.refs_3_
  51.6 1.3 %collective-permute-start.11 = (bf16[256,1024]{1,0:T(8,128)(2,1)}, bf16[256,1024]{1,0:T(8,128)(2,1)}, u32[]{:S(2)}, u32[]{:S(2)}) collective-permute-start(bf16[256,1024]{1,0:T(8,128)(2,1)} %collective-permute-done.9.refs_3_), channel_id=1, source_target_pairs={{4,0},{8,12},{5,1},{9,13},{6,2},{10,14},{7,3},{11,15},{20,16},{24,... | collective-permute-start | bytes 1572872 | tf_op jit(solution)/shard_map/ranks/line_3_0/ppermute | solution.py:356
  53.0 0.1 stack.59.scalars
  53.1 0.1 stack.54.scalars
  53.1 1.5 %collective-permute-start.2 = (bf16[384,128]{1,0:T(8,128)(2,1)}, bf16[384,128]{1,0:T(8,128)(2,1)S(1)}, u32[]{:S(2)}, u32[]{:S(2)}) collective-permute-start(bf16[384,128]{1,0:T(8,128)(2,1)} %add_convert_fusion.here_ref), channel_id=1, source_target_pairs={{0,2},{2,0},{1,3},{3,1},{4,6},{6,4},{5,7},{7,5},{8,10},{10,8},{9,1... | collective-permute-start | bytes 294920 | tf_op jit(solution)/shard_map/ranks/psum_tensor/ppermute | solution.py:298
  54.6 0.1 pad_add_fusion.scalars
  54.7 1.5 %collective-permute-start.4 = (bf16[256,1024]{1,0:T(8,128)(2,1)}, bf16[256,1024]{1,0:T(8,128)(2,1)}, u32[]{:S(2)}, u32[]{:S(2)}) collective-permute-start(bf16[256,1024]{1,0:T(8,128)(2,1)} %collective-permute-done.3.refs_0_), channel_id=1, source_target_pairs={{4,20},{0,16},{12,28},{8,24},{20,4},{16,0},{28,12},{24,8},{5,21},{... | collective-permute-start | bytes 1572872 | tf_op jit(solution)/shard_map/swap_w_0/ppermute | solution.py:364
  56.2 1.5 %collective-permute-start.6 = (bf16[256,1024]{1,0:T(8,128)(2,1)}, bf16[256,1024]{1,0:T(8,128)(2,1)}, u32[]{:S(2)}, u32[]{:S(2)}) collective-permute-start(bf16[256,1024]{1,0:T(8,128)(2,1)} %collective-permute-done.5.refs_1_), channel_id=1, source_target_pairs={{8,24},{4,20},{24,8},{20,4},{9,25},{5,21},{25,9},{21,5},{10,26},{6... | collective-permute-start | bytes 1572872 | tf_op jit(solution)/shard_map/swap_w_1/ppermute | solution.py:364
  57.7 0.3 collective-permute-done.2.there_ref
  58.0 0.9 copy-done.2
  58.9 1.3 %adapter_grads.1 = (bf16[4,64,2304]{2,1,0:T(8,128)(2,1)S(1)}, bf16[384,64]{1,0:T(8,128)(2,1)S(1)}) custom-call(s32[4]{0:T(128)S(1)} %pad_add_fusion.scalars, bf16[384,2048]{1,0:T(8,128)(2,1)S(1)} %copy-done, bf16[384,1024]{1,0:T(8,128)(2,1)S(1)} %broadcast_multiply_fusion.w_ref.weighted_ref, bf16[384,128]{1,0:T(8,128)(2,1)S(1)} %copy-done.2, ...), custom_call_target="tpu_custom_call" | custom-call | flops 113246208 | bytes 2949120 | tf_op jit(solution)/shard_map/ranks/adapter_grads/pallas_call | solution.py:172
  60.2 0.0 copy-start.1
  60.2 1.0 %copy-done.1 = bf16[4,64,2304]{2,1,0:T(8,128)(2,1)} copy-done((bf16[4,64,2304]{2,1,0:T(8,128)(2,1)}, bf16[4,64,2304]{2,1,0:T(8,128)(2,1)S(1)}, u32[]{:S(2)}) %copy-start.1) | copy-done | bytes 1179672
  61.2 0.6 copy-done.7
  61.9 7.3 %all-to-all-start.1 = ((bf16[4,64,2304]{2,1,0:T(8,128)(2,1)}), bf16[4,64,2304]{2,1,0:T(8,128)(2,1)S(1)}, u32[]{:S(2)}, u32[]{:S(2)}) async-start(bf16[4,64,2304]{2,1,0:T(8,128)(2,1)} %copy-done.1), calls=%async_computation.1 | async-start | bytes 2359296 | tf_op jit(solution)/shard_map/ranks/all_to_all | solution.py:379
  69.1 0.7 collective-permute-start.10
  69.8 3.4 %collective-permute-start.8 = (bf16[256,1024]{1,0:T(8,128)(2,1)}, bf16[256,1024]{1,0:T(8,128)(2,1)S(1)}, u32[]{:S(2)}, u32[]{:S(2)}) collective-permute-start(bf16[256,1024]{1,0:T(8,128)(2,1)} %collective-permute-done.7.refs_2_), channel_id=1, source_target_pairs={{0,16},{12,28},{16,0},{28,12},{1,17},{13,29},{17,1},{29,13},{2,18}... | collective-permute-start | bytes 1572872 | tf_op jit(solution)/shard_map/swap_w_2/ppermute | solution.py:364
  73.3 0.0 collective-permute-done.11.refs_4_
  73.3 2.4 %collective-permute-start.12 = (bf16[256,1024]{1,0:T(8,128)(2,1)}, bf16[256,1024]{1,0:T(8,128)(2,1)S(1)}, u32[]{:S(2)}, u32[]{:S(2)}) collective-permute-start(bf16[256,1024]{1,0:T(8,128)(2,1)} %collective-permute-done.11.refs_4_), channel_id=1, source_target_pairs={{0,16},{12,28},{16,0},{28,12},{1,17},{13,29},{17,1},{29,13},{2,18}... | collective-permute-start | bytes 1572872 | tf_op jit(solution)/shard_map/swap_w_4/ppermute | solution.py:364
  75.7 0.0 copy-done.8
  75.7 0.0 copy-start.5
  75.7 1.2 %copy-done.5 = bf16[256,2048]{1,0:T(8,128)(2,1)S(1)} copy-done((bf16[256,2048]{1,0:T(8,128)(2,1)S(1)}, bf16[256,2048]{1,0:T(8,128)(2,1)}, u32[]{:S(2)}) %copy-start.5) | copy-done | bytes 1048600
  76.9 4.1 %product.2.refs_5_ = bf16[384,2048]{1,0:T(8,128)(2,1)} custom-call(s32[10]{0:T(128)S(1)} %stack.59.scalars, bf16[384,1024]{1,0:T(8,128)(2,1)S(1)} %broadcast_multiply_fusion.w_ref.weighted_ref, bf16[384,64]{1,0:T(8,128)(2,1)S(1)} %copy-done.8, bf16[4,64,1280]{2,1,0:T(8,128)(2,1)S(1)} %all-to-all-done.mine_ref.up_ref.down_ref, ...), custom_call_target="tpu_custom_call" | custom-call | flops 9663676416 | bytes 2883584 | tf_op jit(solution)/shard_map/product/pallas_call | solution.py:144
  81.0 0.0 collective-permute-done.4.refs_0_
  81.0 0.0 collective-permute-done.6.refs_1_
  81.0 0.0 collective-permute-done.10.refs_3_
  81.0 5.8 %collective-permute-done.8.refs_2_ = bf16[256,1024]{1,0:T(8,128)(2,1)S(1)} collective-permute-done((bf16[256,1024]{1,0:T(8,128)(2,1)}, bf16[256,1024]{1,0:T(8,128)(2,1)S(1)}, u32[]{:S(2)}, u32[]{:S(2)}) %collective-permute-start.8) | collective-permute-done | bytes 524320 | tf_op jit(solution)/shard_map/swap_w_2/ppermute | solution.py:364
  86.8 7.2 %collective-permute-done.12.refs_4_ = bf16[256,1024]{1,0:T(8,128)(2,1)S(1)} collective-permute-done((bf16[256,1024]{1,0:T(8,128)(2,1)}, bf16[256,1024]{1,0:T(8,128)(2,1)S(1)}, u32[]{:S(2)}, u32[]{:S(2)}) %collective-permute-start.12) | collective-permute-done | bytes 524320 | tf_op jit(solution)/shard_map/swap_w_4/ppermute | solution.py:364
  94.0 3.9 %product.3 = bf16[384,2048]{1,0:T(8,128)(2,1)} custom-call(s32[10]{0:T(128)S(1)} %stack.54.scalars, bf16[384,1024]{1,0:T(8,128)(2,1)S(1)} %broadcast_multiply_fusion.w_ref.weighted_ref, bf16[384,64]{1,0:T(8,128)(2,1)S(1)} %copy-done.8, bf16[4,64,1024]{2,1,0:T(8,128)(2,1)S(1)} %collective-permute-done.other_ref.down_ref, ...), custom_call_target="tpu_custom_call", output_to_operand_aliasing={{}: (10, {})} | custom-call | flops 9663676416 | bytes 2883584 | tf_op jit(solution)/shard_map/product/pallas_call | solution.py:144
  97.9 0.0 all-to-all-done.1.got_ref
  97.9 0.9 owner_sums.1
  (6 shorter events, 0.0 us)
Async XLA Ops:
  0.6 1.0 copy-start.3
  1.6 0.8 copy-start.6
  2.3 7.3 %copy-start.4 = (bf16[256,2048]{1,0:T(8,128)(2,1)S(1)}, bf16[256,2048]{1,0:T(8,128)(2,1)}, u32[]{:S(2)}) copy-start(bf16[256,2048]{1,0:T(8,128)(2,1)} %own_ref.3) | copy-start | bytes 3145732
  3.2 27.2 %copy-start.9 = (s32[384]{0:T(512)S(1)}, s32[384]{0:T(512)}, u32[]{:S(2)}) copy-start(s32[384]{0:T(512)} %param.15) | copy-start | bytes 4612
  3.2 24.8 %all-to-all-start = ((bf16[4,64,1280]{2,1,0:T(8,128)(2,1)}), bf16[4,64,1280]{2,1,0:T(8,128)(2,1)S(1)}, u32[]{:S(2)}, u32[]{:S(2)}) async-start(bf16[4,64,1280]{2,1,0:T(8,128)(2,1)} %payload.1), calls=%async_computation | async-start | bytes 1310720 | tf_op jit(solution)/shard_map/adapters/all_to_all | solution.py:328
  10.5 26.1 %copy-start.10 = (s32[4]{0:T(128)S(1)}, s32[4]{0:T(128)}, u32[]{:S(2)}) copy-start(s32[4]{0:T(128)} %param.14) | copy-start | bytes 52
  10.5 26.1 %copy-start.11 = (s32[3,1]{0,1:T(1,128)S(1)}, s32[3,1]{0,1:T(1,128)}, u32[]{:S(2)}) copy-start(s32[3,1]{0,1:T(1,128)} %param.13) | copy-start | bytes 40
  10.5 30.4 %copy-start = (bf16[384,2048]{1,0:T(8,128)(2,1)S(1)}, bf16[384,2048]{1,0:T(8,128)(2,1)}, u32[]{:S(2)}) copy-start(bf16[384,2048]{1,0:T(8,128)(2,1)} %x_ref.3) | copy-start | bytes 4718596
  10.5 23.4 %collective-permute-start.3 = (bf16[256,1024]{1,0:T(8,128)(2,1)}, bf16[256,1024]{1,0:T(8,128)(2,1)}, u32[]{:S(2)}, u32[]{:S(2)}) collective-permute-start(bf16[256,1024]{1,0:T(8,128)(2,1)} %constant_dynamic-slice_fusion), channel_id=1, source_target_pairs={{0,4},{4,0},{8,12},{12,8},{1,5},{5,1},{9,13},{13,9},{2,6},{6,2},{1... | collective-permute-start | bytes 1572872 | tf_op jit(solution)/shard_map/line_1_0/ppermute | solution.py:356
  12.6 21.3 %collective-permute-start.5 = (bf16[256,1024]{1,0:T(8,128)(2,1)}, bf16[256,1024]{1,0:T(8,128)(2,1)}, u32[]{:S(2)}, u32[]{:S(2)}) collective-permute-start(bf16[256,1024]{1,0:T(8,128)(2,1)} %constant_dynamic-slice_fusion), channel_id=1, source_target_pairs={{4,8},{8,4},{5,9},{9,5},{6,10},{10,6},{7,11},{11,7},{20,24},{24,20... | collective-permute-start | bytes 1572872 | tf_op jit(solution)/shard_map/line_1_1/ppermute | solution.py:356
  28.9 12.1 %collective-permute-start = (bf16[4,64,1024]{2,1,0:T(8,128)(2,1)}, bf16[4,64,1024]{2,1,0:T(8,128)(2,1)S(1)}, u32[]{:S(2)}, u32[]{:S(2)}) collective-permute-start(bf16[4,64,1024]{2,1,0:T(8,128)(2,1)} %slice.8), channel_id=1, source_target_pairs={{0,16},{16,0},{1,17},{17,1},{2,18},{18,2},{3,19},{19,3},{4,20},{20... | collective-permute-start | bytes 1572872 | tf_op jit(solution)/shard_map/swap_a/ppermute | solution.py:336
  33.9 17.7 %collective-permute-start.7 = (bf16[256,1024]{1,0:T(8,128)(2,1)}, bf16[256,1024]{1,0:T(8,128)(2,1)}, u32[]{:S(2)}, u32[]{:S(2)}) collective-permute-start(bf16[256,1024]{1,0:T(8,128)(2,1)} %collective-permute-done.5.refs_1_), channel_id=1, source_target_pairs={{4,0},{8,12},{5,1},{9,13},{6,2},{10,14},{7,3},{11,15},{20,16},{24,... | collective-permute-start | bytes 1572872 | tf_op jit(solution)/shard_map/line_2_0/ppermute | solution.py:356
  35.2 16.4 %collective-permute-start.9 = (bf16[256,1024]{1,0:T(8,128)(2,1)}, bf16[256,1024]{1,0:T(8,128)(2,1)}, u32[]{:S(2)}, u32[]{:S(2)}) collective-permute-start(bf16[256,1024]{1,0:T(8,128)(2,1)} %collective-permute-done.3.refs_0_), channel_id=1, source_target_pairs={{4,8},{8,4},{5,9},{9,5},{6,10},{10,6},{7,11},{11,7},{20,24},{24,20... | collective-permute-start | bytes 1572872 | tf_op jit(solution)/shard_map/line_2_1/ppermute | solution.py:356
  42.2 1.4 %collective-permute-start.1 = (bf16[384,128]{1,0:T(8,128)(2,1)S(1)}, bf16[384,128]{1,0:T(8,128)(2,1)S(1)}, u32[]{:S(2)}, u32[]{:S(2)}) collective-permute-start(bf16[384,128]{1,0:T(8,128)(2,1)S(1)} %project.1), channel_id=1, source_target_pairs={{0,1},{1,0},{2,3},{3,2},{4,5},{5,4},{6,7},{7,6},{8,9},{9,8},{10,11... | collective-permute-start | bytes 294920 | tf_op jit(solution)/shard_map/ranks/psum_pipe/ppermute | solution.py:298
  51.6 21.6 %collective-permute-start.11 = (bf16[256,1024]{1,0:T(8,128)(2,1)}, bf16[256,1024]{1,0:T(8,128)(2,1)}, u32[]{:S(2)}, u32[]{:S(2)}) collective-permute-start(bf16[256,1024]{1,0:T(8,128)(2,1)} %collective-permute-done.9.refs_3_), channel_id=1, source_target_pairs={{4,0},{8,12},{5,1},{9,13},{6,2},{10,14},{7,3},{11,15},{20,16},{24,... | collective-permute-start | bytes 1572872 | tf_op jit(solution)/shard_map/ranks/line_3_0/ppermute | solution.py:356
  53.1 4.8 %collective-permute-start.2 = (bf16[384,128]{1,0:T(8,128)(2,1)}, bf16[384,128]{1,0:T(8,128)(2,1)S(1)}, u32[]{:S(2)}, u32[]{:S(2)}) collective-permute-start(bf16[384,128]{1,0:T(8,128)(2,1)} %add_convert_fusion.here_ref), channel_id=1, source_target_pairs={{0,2},{2,0},{1,3},{3,1},{4,6},{6,4},{5,7},{7,5},{8,10},{10,8},{9,1... | collective-permute-start | bytes 294920 | tf_op jit(solution)/shard_map/ranks/psum_tensor/ppermute | solution.py:298
  54.7 26.3 %collective-permute-start.4 = (bf16[256,1024]{1,0:T(8,128)(2,1)}, bf16[256,1024]{1,0:T(8,128)(2,1)}, u32[]{:S(2)}, u32[]{:S(2)}) collective-permute-start(bf16[256,1024]{1,0:T(8,128)(2,1)} %collective-permute-done.3.refs_0_), channel_id=1, source_target_pairs={{4,20},{0,16},{12,28},{8,24},{20,4},{16,0},{28,12},{24,8},{5,21},{... | collective-permute-start | bytes 1572872 | tf_op jit(solution)/shard_map/swap_w_0/ppermute | solution.py:364
  56.2 24.8 %collective-permute-start.6 = (bf16[256,1024]{1,0:T(8,128)(2,1)}, bf16[256,1024]{1,0:T(8,128)(2,1)}, u32[]{:S(2)}, u32[]{:S(2)}) collective-permute-start(bf16[256,1024]{1,0:T(8,128)(2,1)} %collective-permute-done.5.refs_1_), channel_id=1, source_target_pairs={{8,24},{4,20},{24,8},{20,4},{9,25},{5,21},{25,9},{21,5},{10,26},{6... | collective-permute-start | bytes 1572872 | tf_op jit(solution)/shard_map/swap_w_1/ppermute | solution.py:364
  58.0 0.9 copy-start.2
  60.2 1.0 %copy-start.1 = (bf16[4,64,2304]{2,1,0:T(8,128)(2,1)}, bf16[4,64,2304]{2,1,0:T(8,128)(2,1)S(1)}, u32[]{:S(2)}) copy-start(bf16[4,64,2304]{2,1,0:T(8,128)(2,1)S(1)} %get-tuple-element.22) | copy-start | bytes 3538948
  61.2 0.6 copy-start.7
  61.9 13.8 %copy-start.8 = (bf16[384,64]{1,0:T(8,128)(2,1)S(1)}, bf16[384,64]{1,0:T(8,128)(2,1)}, u32[]{:S(2)}) copy-start(bf16[384,64]{1,0:T(8,128)(2,1)} %copy-done.7) | copy-start | bytes 147460
  61.9 36.0 %all-to-all-start.1 = ((bf16[4,64,2304]{2,1,0:T(8,128)(2,1)}), bf16[4,64,2304]{2,1,0:T(8,128)(2,1)S(1)}, u32[]{:S(2)}, u32[]{:S(2)}) async-start(bf16[4,64,2304]{2,1,0:T(8,128)(2,1)} %copy-done.1), calls=%async_computation.1 | async-start | bytes 2359296 | tf_op jit(solution)/shard_map/ranks/all_to_all | solution.py:379
  69.1 11.9 %collective-permute-start.10 = (bf16[256,1024]{1,0:T(8,128)(2,1)}, bf16[256,1024]{1,0:T(8,128)(2,1)S(1)}, u32[]{:S(2)}, u32[]{:S(2)}) collective-permute-start(bf16[256,1024]{1,0:T(8,128)(2,1)} %collective-permute-done.9.refs_3_), channel_id=1, source_target_pairs={{8,24},{4,20},{24,8},{20,4},{9,25},{5,21},{25,9},{21,5},{10,26},{6... | collective-permute-start | bytes 1572872 | tf_op jit(solution)/shard_map/swap_w_3/ppermute | solution.py:364
  69.8 17.0 %collective-permute-start.8 = (bf16[256,1024]{1,0:T(8,128)(2,1)}, bf16[256,1024]{1,0:T(8,128)(2,1)S(1)}, u32[]{:S(2)}, u32[]{:S(2)}) collective-permute-start(bf16[256,1024]{1,0:T(8,128)(2,1)} %collective-permute-done.7.refs_2_), channel_id=1, source_target_pairs={{0,16},{12,28},{16,0},{28,12},{1,17},{13,29},{17,1},{29,13},{2,18}... | collective-permute-start | bytes 1572872 | tf_op jit(solution)/shard_map/swap_w_2/ppermute | solution.py:364
  73.3 20.7 %collective-permute-start.12 = (bf16[256,1024]{1,0:T(8,128)(2,1)}, bf16[256,1024]{1,0:T(8,128)(2,1)S(1)}, u32[]{:S(2)}, u32[]{:S(2)}) collective-permute-start(bf16[256,1024]{1,0:T(8,128)(2,1)} %collective-permute-done.11.refs_4_), channel_id=1, source_target_pairs={{0,16},{12,28},{16,0},{28,12},{1,17},{13,29},{17,1},{29,13},{2,18}... | collective-permute-start | bytes 1572872 | tf_op jit(solution)/shard_map/swap_w_4/ppermute | solution.py:364
  75.7 1.2 %copy-start.5 = (bf16[256,2048]{1,0:T(8,128)(2,1)S(1)}, bf16[256,2048]{1,0:T(8,128)(2,1)}, u32[]{:S(2)}) copy-start(bf16[256,2048]{1,0:T(8,128)(2,1)} %own_ref.3) | copy-start | bytes 3145732

commit v6 on v5

--- a/solution.py
+++ b/solution.py
@@ -352,11 +352,16 @@
             if not pairs:
                 continue
             owner = jnp.where(me % 2 != parity, me - k, me + k)
-            with jax.named_scope(f"line_{k}_{parity}"):
-                new[parity] = lax.ppermute(last[1 - parity], "seq", pairs)
-            arrived.append(new[parity])
-            pairs_of.append(pairs)
-            begins.append(jnp.where((owner >= 0) & (owner < n), owner * depth, -1))
+            cuts = 2 if k == n - 1 else 1
+            for c in range(cuts):
+                span = slice(c * depth // cuts, (c + 1) * depth // cuts)
+                with jax.named_scope(f"line_{k}_{parity}_{c}"):
+                    new[parity] = lax.ppermute(last[1 - parity][span], "seq", pairs)
+                arrived.append(new[parity])
+                pairs_of.append(pairs)
+                begins.append(
+                    jnp.where((owner >= 0) & (owner < n), owner * depth + span.start, -1)
+                )
         return new
 
     def exchange(j, *before):
@@ -371,16 +376,18 @@
     with jax.named_scope("ranks"):
         part = project(group, slab_index, slots, layer_input, weighted, received, down_other)
         here = pair_sum(part)
-        advance(n - 1, last, here)
         there = rest_of(here, "tensor").astype(BF16)
+        swapped = [None] * (len(arrived) + 2)
+        swapped[0] = exchange(0, down_other)
         table, low_b = adapter_grads(
             slab_index, slots, layer_input, weighted, here, there, tenants, slab
         )
+        advance(n - 1, last, table, swapped[0])
+        swapped = swapped[: len(arrived)]
         got = lax.all_to_all(table, "seq", split_axis=0, concat_axis=0, tiled=True)
-    swapped = []
     for j in range(len(arrived)):
-        before = [down_other] if j < 2 else [table] if j < 4 else []
-        swapped.append(exchange(j, *before))
+        if swapped[j] is None:
+            swapped[j] = exchange(j, *([table] if j in (1, 2, 3) else []))
 
     common = (slots, begins, weighted, low_b)
     first = product(group, *common, received, value_weight, arrived)

time: 99.5 us -> 94.2 us (0.947)
  waiting for transfers between devices: 42.2 us -> 32 us
  starting transfers between devices: 33.8 us -> 37.1 us
  local copies, waits for them, and re-layouts: 7.4 us -> 10.2 us
    ppermute x5 -> x6, waiting for transfers between devices: 13 us -> 0.64 us  [exchange(): lax.ppermute(after(arrived[j], before), ('groups', 'seq'), swap_pairs(pai...]
    ppermute x5 -> x6, starting transfers between devices: 9.51 us -> 14.5 us  [exchange(): lax.ppermute(after(arrived[j], before), ('groups', 'seq'), swap_pairs(pai...]
    ppermute x2, waiting for transfers between devices: 1.56 us -> 4.57 us  [rest_of(): rest = rest + lax.ppermute(value, axis, pairs).astype(F32)]
    all_to_all x1, starting transfers between devices: 7.26 us -> 4.99 us  [per_device(): got = lax.all_to_all(table, 'seq', split_axis=0, concat_axis=0, tiled=True)]
    unnamed x24 -> x34, local copies, waits for them, and re-layouts: 5.52 us -> 7.5 us
    ppermute x5 -> x6, waiting for transfers between devices: 9.61 us -> 7.69 us  [advance(): new[parity] = lax.ppermute(last[1 - parity][span], 'seq', pairs)]
    ppermute x1, waiting for transfers between devices: 4.01 us -> 5.06 us  [per_device(): down_other = swap('groups')(received[:, :, :half])]
    ppermute x5 -> x6, starting transfers between devices: 7.5 us -> 8.04 us  [advance(): new[parity] = lax.ppermute(last[1 - parity][span], 'seq', pairs)]
  transfers between devices with their start and end apart: 15 -> 17, of which waited for: 8 -> 7; matrix products, arithmetic and copies ran while one was open for 4% -> 4% of each run, Pallas kernels for 11% -> 10%
where the time goes in v6:
time: 94.2 us; the launch traced here: 93.4 us
  starting transfers between devices  37.1 us (39%)
  waiting for transfers between devices  32 us (34%)
  Pallas kernels  11.6 us (12%)
  local copies, waits for them, and re-layouts  10.2 us (11%)
  other arithmetic  1.62 us (2%)
  between operations  0.98 us (1%)
    ppermute x6, starting transfers between devices, exchange(): lax.ppermute(after(arrived[j], before), ('groups', 'seq'), swap_pairs(pai...  14.5 us
    all_to_all x1, waiting for transfers between devices, per_device(): lax.all_to_all(payload(group, adapter_down, adapter_up, n), 'seq', split_...  14 us
    ppermute x6, starting transfers between devices, advance(): new[parity] = lax.ppermute(last[1 - parity][span], 'seq', pairs)  8.04 us
    ppermute x6, waiting for transfers between devices, advance(): new[parity] = lax.ppermute(last[1 - parity][span], 'seq', pairs)  7.69 us
    unnamed x34, local copies, waits for them, and re-layouts  7.5 us
    pallas_call x2, Pallas kernels, product(): pl.pallas_call(functools.partial(product_kernel, blocks, tiles), out_shap...  7.17 us
    all_to_all x1, starting transfers between devices, per_device(): lax.all_to_all(payload(group, adapter_down, adapter_up, n), 'seq', split_...  6.45 us
    ppermute x1, waiting for transfers between devices, per_device(): down_other = swap('groups')(received[:, :, :half])  5.06 us
  transfers between devices with their start and end apart: 17, of which 7 were waited for; matrix products, arithmetic and copies ran while one was open for 4% of the time, Pallas kernels for 10%

profile of v6, /device:TPU:0, one launch (start us, length us, event | category | flops | bytes accessed | tf_op | source)
XLA Modules:
  0.0 93.4 jit_solution(14471804642648440349)
XLA Ops:
  0.6 0.0 copy-start.4
  0.6 0.9 %copy-done.4 = bf16[1,64,2048]{2,1,0:T(8,128)(2,1)S(1)} copy-done((bf16[1,64,2048]{2,1,0:T(8,128)(2,1)S(1)}, bf16[1,64,2048]{2,1,0:T(8,128)(2,1)}, u32[]{:S(2)}) %copy-start.4) | copy-done | bytes 262168
  1.6 0.8 copy-done.7
  2.3 0.9 payload.1
  3.2 6.4 %all-to-all-start = ((bf16[4,64,1280]{2,1,0:T(8,128)(2,1)}), bf16[4,64,1280]{2,1,0:T(8,128)(2,1)S(1)}, u32[]{:S(2)}, u32[]{:S(2)}) async-start(bf16[4,64,1280]{2,1,0:T(8,128)(2,1)} %payload.1), calls=%async_computation | async-start | bytes 1310720 | tf_op jit(solution)/shard_map/adapters/all_to_all | solution.py:328
  9.7 0.0 copy-done.5
  9.7 0.8 constant_dynamic-slice_fusion
  10.5 2.0 %collective-permute-start.3 = (bf16[256,1024]{1,0:T(8,128)(2,1)}, bf16[256,1024]{1,0:T(8,128)(2,1)}, u32[]{:S(2)}, u32[]{:S(2)}) collective-permute-start(bf16[256,1024]{1,0:T(8,128)(2,1)} %constant_dynamic-slice_fusion), channel_id=1, source_target_pairs={{0,4},{4,0},{8,12},{12,8},{1,5},{5,1},{9,13},{13,9},{2,6},{6,2},{1... | collective-permute-start | bytes 1572872 | tf_op jit(solution)/shard_map/line_1_0_0/ppermute | solution.py:359
  12.6 1.5 %collective-permute-start.5 = (bf16[256,1024]{1,0:T(8,128)(2,1)}, bf16[256,1024]{1,0:T(8,128)(2,1)}, u32[]{:S(2)}, u32[]{:S(2)}) collective-permute-start(bf16[256,1024]{1,0:T(8,128)(2,1)} %constant_dynamic-slice_fusion), channel_id=1, source_target_pairs={{4,8},{8,4},{5,9},{9,5},{6,10},{10,6},{7,11},{11,7},{20,24},{24,20... | collective-permute-start | bytes 1572872 | tf_op jit(solution)/shard_map/line_1_1_0/ppermute | solution.py:359
  14.0 14.0 %all-to-all-done.mine_ref.up_ref.down_ref = bf16[4,64,1280]{2,1,0:T(8,128)(2,1)S(1)} async-done(((bf16[4,64,1280]{2,1,0:T(8,128)(2,1)}), bf16[4,64,1280]{2,1,0:T(8,128)(2,1)S(1)}, u32[]{:S(2)}, u32[]{:S(2)}) %all-to-all-start) | async-done | bytes 655392 | tf_op jit(solution)/shard_map/adapters/all_to_all | solution.py:328
  28.0 0.9 slice.16
  28.9 1.5 %collective-permute-start = (bf16[4,64,1024]{2,1,0:T(8,128)(2,1)}, bf16[4,64,1024]{2,1,0:T(8,128)(2,1)S(1)}, u32[]{:S(2)}, u32[]{:S(2)}) collective-permute-start(bf16[4,64,1024]{2,1,0:T(8,128)(2,1)} %slice.16), channel_id=1, source_target_pairs={{0,16},{16,0},{1,17},{17,1},{2,18},{18,2},{3,19},{19,3},{4,20},{20... | collective-permute-start | bytes 1572872 | tf_op jit(solution)/shard_map/swap_a/ppermute | solution.py:336
  30.4 0.0 copy-done.15
  30.4 0.0 copy-done.16
  30.4 0.2 select_reduce_fusion
  30.6 1.3 %broadcast_multiply_fusion.w_ref.weighted_ref = bf16[384,1024]{1,0:T(8,128)(2,1)S(1)} fusion(bf16[384,1024]{1,0:T(8,128)(2,1)} %param.9, bf16[384]{0:T(512)(128)(2,1)S(1)} %subtract_convert_fusion), kind=kLoop, calls=%fused_computation | loop fusion | flops 393216 | bytes 1573632 | tf_op jit(solution)/shard_map/mul | solution.py:339
  31.9 2.0 %collective-permute-done.3.refs_0_ = bf16[256,1024]{1,0:T(8,128)(2,1)} collective-permute-done((bf16[256,1024]{1,0:T(8,128)(2,1)}, bf16[256,1024]{1,0:T(8,128)(2,1)}, u32[]{:S(2)}, u32[]{:S(2)}) %collective-permute-start.3) | collective-permute-done | bytes 524320 | tf_op jit(solution)/shard_map/line_1_0_0/ppermute | solution.py:359
  33.9 0.0 collective-permute-done.5.refs_1_
  33.9 1.3 %collective-permute-start.7 = (bf16[256,1024]{1,0:T(8,128)(2,1)}, bf16[256,1024]{1,0:T(8,128)(2,1)S(1)}, u32[]{:S(2)}, u32[]{:S(2)}) collective-permute-start(bf16[256,1024]{1,0:T(8,128)(2,1)} %collective-permute-done.5.refs_1_), channel_id=1, source_target_pairs={{4,0},{8,12},{5,1},{9,13},{6,2},{10,14},{7,3},{11,15},{20,16},{24,... | collective-permute-start | bytes 1572872 | tf_op jit(solution)/shard_map/line_2_0_0/ppermute | solution.py:359
  35.2 0.7 collective-permute-start.9
  35.9 5.1 %collective-permute-done.other_ref.down_ref = bf16[4,64,1024]{2,1,0:T(8,128)(2,1)S(1)} collective-permute-done((bf16[4,64,1024]{2,1,0:T(8,128)(2,1)}, bf16[4,64,1024]{2,1,0:T(8,128)(2,1)S(1)}, u32[]{:S(2)}, u32[]{:S(2)}) %collective-permute-start) | collective-permute-done | bytes 524320 | tf_op jit(solution)/shard_map/swap_a/ppermute | solution.py:336
  41.0 1.5 %collective-permute-start.4 = (bf16[256,1024]{1,0:T(8,128)(2,1)}, bf16[256,1024]{1,0:T(8,128)(2,1)S(1)}, u32[]{:S(2)}, u32[]{:S(2)}) collective-permute-start(bf16[256,1024]{1,0:T(8,128)(2,1)} %collective-permute-done.3.refs_0_), channel_id=1, source_target_pairs={{4,20},{0,16},{12,28},{8,24},{20,4},{16,0},{28,12},{24,8},{5,21},{... | collective-permute-start | bytes 1572872 | tf_op jit(solution)/shard_map/ranks/swap_w_0/ppermute | solution.py:369
  42.5 0.1 pad_add_fusion.1.scalars
  42.6 1.3 %project.1 = bf16[384,128]{1,0:T(8,128)(2,1)S(1)} custom-call(s32[5]{0:T(128)S(1)} %pad_add_fusion.1.scalars, bf16[384,2048]{1,0:T(8,128)(2,1)S(1)} %copy-done, bf16[384,1024]{1,0:T(8,128)(2,1)S(1)} %broadcast_multiply_fusion.w_ref.weighted_ref, bf16[4,64,1280]{2,1,0:T(8,128)(2,1)S(1)} %all-to-all-done.mine_ref.up_ref.down_ref, ...), custom_call_target="tpu_custom_call" | custom-call | flops 113246208 | bytes 2949120 | tf_op jit(solution)/shard_map/ranks/project/pallas_call | solution.py:172
  43.8 0.1 collective-permute-start.1
  43.9 1.3 %collective-permute-done.1 = bf16[384,128]{1,0:T(8,128)(2,1)S(1)} collective-permute-done((bf16[384,128]{1,0:T(8,128)(2,1)S(1)}, bf16[384,128]{1,0:T(8,128)(2,1)S(1)}, u32[]{:S(2)}, u32[]{:S(2)}) %collective-permute-start.1) | collective-permute-done | bytes 98336 | tf_op jit(solution)/shard_map/ranks/psum_pipe/ppermute | solution.py:298
  45.2 1.6 %collective-permute-start.2 = (bf16[384,128]{1,0:T(8,128)(2,1)S(1)}, bf16[384,128]{1,0:T(8,128)(2,1)S(1)}, u32[]{:S(2)}, u32[]{:S(2)}) collective-permute-start(bf16[384,128]{1,0:T(8,128)(2,1)S(1)} %add_convert_fusion.here_ref), channel_id=1, source_target_pairs={{0,2},{2,0},{1,3},{3,1},{4,6},{6,4},{5,7},{7,5},{8,10},{10,8},{9,1... | collective-permute-start | bytes 294920 | tf_op jit(solution)/shard_map/ranks/psum_tensor/ppermute | solution.py:298
  46.8 0.1 pad_add_fusion.scalars
  46.9 3.3 %collective-permute-done.2.there_ref = bf16[384,128]{1,0:T(8,128)(2,1)S(1)} collective-permute-done((bf16[384,128]{1,0:T(8,128)(2,1)S(1)}, bf16[384,128]{1,0:T(8,128)(2,1)S(1)}, u32[]{:S(2)}, u32[]{:S(2)}) %collective-permute-start.2) | collective-permute-done | bytes 98336 | tf_op jit(solution)/shard_map/ranks/psum_tensor/ppermute | solution.py:298
  50.2 1.3 %adapter_grads.1 = (bf16[4,64,2304]{2,1,0:T(8,128)(2,1)S(1)}, bf16[384,64]{1,0:T(8,128)(2,1)S(1)}) custom-call(s32[4]{0:T(128)S(1)} %pad_add_fusion.scalars, bf16[384,2048]{1,0:T(8,128)(2,1)S(1)} %copy-done, bf16[384,1024]{1,0:T(8,128)(2,1)S(1)} %broadcast_multiply_fusion.w_ref.weighted_ref, bf16[384,128]{1,0:T(8,128)(2,1)S(1)} %add_convert_fusion.here_ref, ...), custom_call_target="tpu_custom_call" | custom-call | flops 113246208 | bytes 2949120 | tf_op jit(solution)/shard_map/ranks/adapter_grads/pallas_call | solution.py:172
  51.5 0.0 copy-start.1
  51.5 1.0 %copy-done.1 = bf16[4,64,2304]{2,1,0:T(8,128)(2,1)} copy-done((bf16[4,64,2304]{2,1,0:T(8,128)(2,1)}, bf16[4,64,2304]{2,1,0:T(8,128)(2,1)S(1)}, u32[]{:S(2)}) %copy-start.1) | copy-done | bytes 1179672
  52.5 0.6 copy-done.12
  53.1 0.0 collective-permute-done.7.refs_2_
  53.1 0.0 collective-permute-done.9.refs_3_
  53.2 0.0 collective-permute-done.4.refs_0_
  53.2 0.0 copy-start.8
  53.2 0.8 copy-done.2
  54.0 0.8 fusion
  54.8 0.0 copy-done.8
  54.8 1.3 %collective-permute-start.13 = (bf16[128,1024]{1,0:T(8,128)(2,1)}, bf16[128,1024]{1,0:T(8,128)(2,1)S(1)}, u32[]{:S(2)}, u32[]{:S(2)}) collective-permute-start(bf16[128,1024]{1,0:T(8,128)(2,1)} %get-tuple-element.29), channel_id=1, source_target_pairs={{4,0},{8,12},{5,1},{9,13},{6,2},{10,14},{7,3},{11,15},{20,16},{24,... | collective-permute-start | bytes 786440 | tf_op jit(solution)/shard_map/ranks/line_3_0_1/ppermute | solution.py:359
  56.1 1.3 %collective-permute-start.11 = (bf16[128,1024]{1,0:T(8,128)(2,1)}, bf16[128,1024]{1,0:T(8,128)(2,1)}, u32[]{:S(2)}, u32[]{:S(2)}) collective-permute-start(bf16[128,1024]{1,0:T(8,128)(2,1)} %get-tuple-element.30), channel_id=1, source_target_pairs={{4,0},{8,12},{5,1},{9,13},{6,2},{10,14},{7,3},{11,15},{20,16},{24,... | collective-permute-start | bytes 786440 | tf_op jit(solution)/shard_map/ranks/line_3_0_0/ppermute | solution.py:359
  57.5 0.1 stack.64.scalars
  57.6 0.1 stack.59.scalars
  57.7 5.0 %all-to-all-start.1 = ((bf16[4,64,2304]{2,1,0:T(8,128)(2,1)}), bf16[4,64,2304]{2,1,0:T(8,128)(2,1)S(1)}, u32[]{:S(2)}, u32[]{:S(2)}) async-start(bf16[4,64,2304]{2,1,0:T(8,128)(2,1)} %copy-done.1), calls=%async_computation.1 | async-start | bytes 2359296 | tf_op jit(solution)/shard_map/ranks/all_to_all | solution.py:387
  62.6 0.7 collective-permute-start.6
  63.3 3.0 %collective-permute-start.8 = (bf16[256,1024]{1,0:T(8,128)(2,1)}, bf16[256,1024]{1,0:T(8,128)(2,1)S(1)}, u32[]{:S(2)}, u32[]{:S(2)}) collective-permute-start(bf16[256,1024]{1,0:T(8,128)(2,1)} %copy-done.10), channel_id=1, source_target_pairs={{0,16},{12,28},{16,0},{28,12},{1,17},{13,29},{17,1},{29,13},{2,18}... | collective-permute-start | bytes 1572872 | tf_op jit(solution)/shard_map/swap_w_2/ppermute | solution.py:369
  66.3 0.7 collective-permute-start.10
  67.0 0.0 collective-permute-done.13.refs_5_
  67.1 5.9 %collective-permute-start.14 = (bf16[128,1024]{1,0:T(8,128)(2,1)S(1)}, bf16[128,1024]{1,0:T(8,128)(2,1)S(1)}, u32[]{:S(2)}, u32[]{:S(2)}) collective-permute-start(bf16[128,1024]{1,0:T(8,128)(2,1)S(1)} %collective-permute-done.13.refs_5_), channel_id=1, source_target_pairs={{0,16},{12,28},{16,0},{28,12},{1,17},{13,29},{17,1},{29,13},{2,18}... | collective-permute-start | bytes 786440 | tf_op jit(solution)/shard_map/swap_w_5/ppermute | solution.py:369
  72.9 5.6 %collective-permute-done.11.refs_4_ = bf16[128,1024]{1,0:T(8,128)(2,1)} collective-permute-done((bf16[128,1024]{1,0:T(8,128)(2,1)}, bf16[128,1024]{1,0:T(8,128)(2,1)}, u32[]{:S(2)}, u32[]{:S(2)}) %collective-permute-start.11) | collective-permute-done | bytes 262176 | tf_op jit(solution)/shard_map/ranks/line_3_0_0/ppermute | solution.py:359
  78.6 2.7 %collective-permute-start.12 = (bf16[128,1024]{1,0:T(8,128)(2,1)}, bf16[128,1024]{1,0:T(8,128)(2,1)S(1)}, u32[]{:S(2)}, u32[]{:S(2)}) collective-permute-start(bf16[128,1024]{1,0:T(8,128)(2,1)} %collective-permute-done.11.refs_4_), channel_id=1, source_target_pairs={{0,16},{12,28},{16,0},{28,12},{1,17},{13,29},{17,1},{29,13},{2,18}... | collective-permute-start | bytes 786440 | tf_op jit(solution)/shard_map/swap_w_4/ppermute | solution.py:369
  81.3 1.0 %copy-done.3 = bf16[256,1024]{1,0:T(8,128)(2,1)S(1)} copy-done((bf16[256,1024]{1,0:T(8,128)(2,1)S(1)}, bf16[256,1024]{1,0:T(8,128)(2,1)}, u32[]{:S(2)}) %copy-start.3) | copy-done | bytes 524312
  82.4 1.2 %copy-done.6 = bf16[256,2048]{1,0:T(8,128)(2,1)S(1)} copy-done((bf16[256,2048]{1,0:T(8,128)(2,1)S(1)}, bf16[256,2048]{1,0:T(8,128)(2,1)}, u32[]{:S(2)}) %copy-start.6) | copy-done | bytes 1048600
  83.6 1.0 %copy-done.11 = bf16[256,1024]{1,0:T(8,128)(2,1)S(1)} copy-done((bf16[256,1024]{1,0:T(8,128)(2,1)S(1)}, bf16[256,1024]{1,0:T(8,128)(2,1)}, u32[]{:S(2)}) %copy-start.11) | copy-done | bytes 524312
  84.6 4.0 %product.2.refs_6_ = bf16[384,2048]{1,0:T(8,128)(2,1)} custom-call(s32[11]{0:T(128)S(1)} %stack.64.scalars, bf16[384,1024]{1,0:T(8,128)(2,1)S(1)} %broadcast_multiply_fusion.w_ref.weighted_ref, bf16[384,64]{1,0:T(8,128)(2,1)S(1)} %copy-done.13, bf16[4,64,1280]{2,1,0:T(8,128)(2,1)S(1)} %all-to-all-done.mine_ref.up_ref.down_ref, ...), custom_call_target="tpu_custom_call" | custom-call | flops 9663676416 | bytes 2883584 | tf_op jit(solution)/shard_map/product/pallas_call | solution.py:144
  88.6 0.0 collective-permute-done.6.refs_1_
  88.6 0.0 collective-permute-done.8.refs_2_
  88.6 0.0 collective-permute-done.10.refs_3_
  88.6 0.0 collective-permute-done.14.refs_5_
  88.6 0.6 collective-permute-done.12.refs_4_
  89.3 3.2 %product.3 = bf16[384,2048]{1,0:T(8,128)(2,1)} custom-call(s32[11]{0:T(128)S(1)} %stack.59.scalars, bf16[384,1024]{1,0:T(8,128)(2,1)S(1)} %broadcast_multiply_fusion.w_ref.weighted_ref, bf16[384,64]{1,0:T(8,128)(2,1)S(1)} %copy-done.13, bf16[4,64,1024]{2,1,0:T(8,128)(2,1)S(1)} %collective-permute-done.other_ref.down_ref, ...), custom_call_target="tpu_custom_call", output_to_operand_aliasing={{}: (11, {})} | custom-call | flops 9663676416 | bytes 2883584 | tf_op jit(solution)/shard_map/product/pallas_call | solution.py:144
  92.5 0.0 all-to-all-done.1.got_ref
  92.5 0.9 owner_sums.1
  (21 shorter events, 0.1 us)
Async XLA Ops:
  0.6 1.0 %copy-start.4 = (bf16[1,64,2048]{2,1,0:T(8,128)(2,1)S(1)}, bf16[1,64,2048]{2,1,0:T(8,128)(2,1)}, u32[]{:S(2)}) copy-start(bf16[1,64,2048]{2,1,0:T(8,128)(2,1)} %down_ref.1) | copy-start | bytes 786436
  1.6 0.8 copy-start.7
  2.3 7.3 %copy-start.5 = (bf16[256,2048]{1,0:T(8,128)(2,1)S(1)}, bf16[256,2048]{1,0:T(8,128)(2,1)}, u32[]{:S(2)}) copy-start(bf16[256,2048]{1,0:T(8,128)(2,1)} %own_ref.3) | copy-start | bytes 3145732
  3.2 27.2 %copy-start.15 = (s32[4]{0:T(128)S(1)}, s32[4]{0:T(128)}, u32[]{:S(2)}) copy-start(s32[4]{0:T(128)} %param.14) | copy-start | bytes 52
  3.2 27.2 %copy-start.16 = (s32[3,1]{0,1:T(1,128)S(1)}, s32[3,1]{0,1:T(1,128)}, u32[]{:S(2)}) copy-start(s32[3,1]{0,1:T(1,128)} %param.13) | copy-start | bytes 40
  3.2 27.4 %copy-start.14 = (s32[384]{0:T(512)S(1)}, s32[384]{0:T(512)}, u32[]{:S(2)}) copy-start(s32[384]{0:T(512)} %param.15) | copy-start | bytes 4612
  3.2 24.8 %all-to-all-start = ((bf16[4,64,1280]{2,1,0:T(8,128)(2,1)}), bf16[4,64,1280]{2,1,0:T(8,128)(2,1)S(1)}, u32[]{:S(2)}, u32[]{:S(2)}) async-start(bf16[4,64,1280]{2,1,0:T(8,128)(2,1)} %payload.1), calls=%async_computation | async-start | bytes 1310720 | tf_op jit(solution)/shard_map/adapters/all_to_all | solution.py:328
  10.5 32.0 %copy-start = (bf16[384,2048]{1,0:T(8,128)(2,1)S(1)}, bf16[384,2048]{1,0:T(8,128)(2,1)}, u32[]{:S(2)}) copy-start(bf16[384,2048]{1,0:T(8,128)(2,1)} %x_ref.3) | copy-start | bytes 4718596
  10.5 23.4 %collective-permute-start.3 = (bf16[256,1024]{1,0:T(8,128)(2,1)}, bf16[256,1024]{1,0:T(8,128)(2,1)}, u32[]{:S(2)}, u32[]{:S(2)}) collective-permute-start(bf16[256,1024]{1,0:T(8,128)(2,1)} %constant_dynamic-slice_fusion), channel_id=1, source_target_pairs={{0,4},{4,0},{8,12},{12,8},{1,5},{5,1},{9,13},{13,9},{2,6},{6,2},{1... | collective-permute-start | bytes 1572872 | tf_op jit(solution)/shard_map/line_1_0_0/ppermute | solution.py:359
  12.6 21.4 %collective-permute-start.5 = (bf16[256,1024]{1,0:T(8,128)(2,1)}, bf16[256,1024]{1,0:T(8,128)(2,1)}, u32[]{:S(2)}, u32[]{:S(2)}) collective-permute-start(bf16[256,1024]{1,0:T(8,128)(2,1)} %constant_dynamic-slice_fusion), channel_id=1, source_target_pairs={{4,8},{8,4},{5,9},{9,5},{6,10},{10,6},{7,11},{11,7},{20,24},{24,20... | collective-permute-start | bytes 1572872 | tf_op jit(solution)/shard_map/line_1_1_0/ppermute | solution.py:359
  28.9 12.1 %collective-permute-start = (bf16[4,64,1024]{2,1,0:T(8,128)(2,1)}, bf16[4,64,1024]{2,1,0:T(8,128)(2,1)S(1)}, u32[]{:S(2)}, u32[]{:S(2)}) collective-permute-start(bf16[4,64,1024]{2,1,0:T(8,128)(2,1)} %slice.16), channel_id=1, source_target_pairs={{0,16},{16,0},{1,17},{17,1},{2,18},{18,2},{3,19},{19,3},{4,20},{20... | collective-permute-start | bytes 1572872 | tf_op jit(solution)/shard_map/swap_a/ppermute | solution.py:336
  33.9 19.2 %collective-permute-start.7 = (bf16[256,1024]{1,0:T(8,128)(2,1)}, bf16[256,1024]{1,0:T(8,128)(2,1)S(1)}, u32[]{:S(2)}, u32[]{:S(2)}) collective-permute-start(bf16[256,1024]{1,0:T(8,128)(2,1)} %collective-permute-done.5.refs_1_), channel_id=1, source_target_pairs={{4,0},{8,12},{5,1},{9,13},{6,2},{10,14},{7,3},{11,15},{20,16},{24,... | collective-permute-start | bytes 1572872 | tf_op jit(solution)/shard_map/line_2_0_0/ppermute | solution.py:359
  35.2 17.9 %collective-permute-start.9 = (bf16[256,1024]{1,0:T(8,128)(2,1)}, bf16[256,1024]{1,0:T(8,128)(2,1)S(1)}, u32[]{:S(2)}, u32[]{:S(2)}) collective-permute-start(bf16[256,1024]{1,0:T(8,128)(2,1)} %collective-permute-done.3.refs_0_), channel_id=1, source_target_pairs={{4,8},{8,4},{5,9},{9,5},{6,10},{10,6},{7,11},{11,7},{20,24},{24,20... | collective-permute-start | bytes 1572872 | tf_op jit(solution)/shard_map/line_2_1_0/ppermute | solution.py:359
  41.0 12.2 %collective-permute-start.4 = (bf16[256,1024]{1,0:T(8,128)(2,1)}, bf16[256,1024]{1,0:T(8,128)(2,1)S(1)}, u32[]{:S(2)}, u32[]{:S(2)}) collective-permute-start(bf16[256,1024]{1,0:T(8,128)(2,1)} %collective-permute-done.3.refs_0_), channel_id=1, source_target_pairs={{4,20},{0,16},{12,28},{8,24},{20,4},{16,0},{28,12},{24,8},{5,21},{... | collective-permute-start | bytes 1572872 | tf_op jit(solution)/shard_map/ranks/swap_w_0/ppermute | solution.py:369
  43.8 1.4 %collective-permute-start.1 = (bf16[384,128]{1,0:T(8,128)(2,1)S(1)}, bf16[384,128]{1,0:T(8,128)(2,1)S(1)}, u32[]{:S(2)}, u32[]{:S(2)}) collective-permute-start(bf16[384,128]{1,0:T(8,128)(2,1)S(1)} %project.1), channel_id=1, source_target_pairs={{0,1},{1,0},{2,3},{3,2},{4,5},{5,4},{6,7},{7,6},{8,9},{9,8},{10,11... | collective-permute-start | bytes 294920 | tf_op jit(solution)/shard_map/ranks/psum_pipe/ppermute | solution.py:298
  45.2 4.9 %collective-permute-start.2 = (bf16[384,128]{1,0:T(8,128)(2,1)S(1)}, bf16[384,128]{1,0:T(8,128)(2,1)S(1)}, u32[]{:S(2)}, u32[]{:S(2)}) collective-permute-start(bf16[384,128]{1,0:T(8,128)(2,1)S(1)} %add_convert_fusion.here_ref), channel_id=1, source_target_pairs={{0,2},{2,0},{1,3},{3,1},{4,6},{6,4},{5,7},{7,5},{8,10},{10,8},{9,1... | collective-permute-start | bytes 294920 | tf_op jit(solution)/shard_map/ranks/psum_tensor/ppermute | solution.py:298
  51.5 1.0 %copy-start.1 = (bf16[4,64,2304]{2,1,0:T(8,128)(2,1)}, bf16[4,64,2304]{2,1,0:T(8,128)(2,1)S(1)}, u32[]{:S(2)}) copy-start(bf16[4,64,2304]{2,1,0:T(8,128)(2,1)S(1)} %get-tuple-element.20) | copy-start | bytes 3538948
  52.5 0.6 copy-start.12
  53.1 1.7 %copy-start.10 = (bf16[256,1024]{1,0:T(8,128)(2,1)}, bf16[256,1024]{1,0:T(8,128)(2,1)S(1)}, u32[]{:S(2)}) copy-start(bf16[256,1024]{1,0:T(8,128)(2,1)S(1)} %collective-permute-done.7.refs_2_) | copy-start | bytes 1572868
  53.2 0.8 copy-start.2
  53.2 1.6 %copy-start.8 = (bf16[256,1024]{1,0:T(8,128)(2,1)}, bf16[256,1024]{1,0:T(8,128)(2,1)S(1)}, u32[]{:S(2)}) copy-start(bf16[256,1024]{1,0:T(8,128)(2,1)S(1)} %collective-permute-done.4.refs_0_) | copy-start | bytes 1572868
  54.0 27.3 %copy-start.13 = (bf16[384,64]{1,0:T(8,128)(2,1)S(1)}, bf16[384,64]{1,0:T(8,128)(2,1)}, u32[]{:S(2)}) copy-start(bf16[384,64]{1,0:T(8,128)(2,1)} %copy-done.12) | copy-start | bytes 147460
  54.8 12.2 %collective-permute-start.13 = (bf16[128,1024]{1,0:T(8,128)(2,1)}, bf16[128,1024]{1,0:T(8,128)(2,1)S(1)}, u32[]{:S(2)}, u32[]{:S(2)}) collective-permute-start(bf16[128,1024]{1,0:T(8,128)(2,1)} %get-tuple-element.29), channel_id=1, source_target_pairs={{4,0},{8,12},{5,1},{9,13},{6,2},{10,14},{7,3},{11,15},{20,16},{24,... | collective-permute-start | bytes 786440 | tf_op jit(solution)/shard_map/ranks/line_3_0_1/ppermute | solution.py:359
  56.1 22.5 %collective-permute-start.11 = (bf16[128,1024]{1,0:T(8,128)(2,1)}, bf16[128,1024]{1,0:T(8,128)(2,1)}, u32[]{:S(2)}, u32[]{:S(2)}) collective-permute-start(bf16[128,1024]{1,0:T(8,128)(2,1)} %get-tuple-element.30), channel_id=1, source_target_pairs={{4,0},{8,12},{5,1},{9,13},{6,2},{10,14},{7,3},{11,15},{20,16},{24,... | collective-permute-start | bytes 786440 | tf_op jit(solution)/shard_map/ranks/line_3_0_0/ppermute | solution.py:359
  57.7 34.9 %all-to-all-start.1 = ((bf16[4,64,2304]{2,1,0:T(8,128)(2,1)}), bf16[4,64,2304]{2,1,0:T(8,128)(2,1)S(1)}, u32[]{:S(2)}, u32[]{:S(2)}) async-start(bf16[4,64,2304]{2,1,0:T(8,128)(2,1)} %copy-done.1), calls=%async_computation.1 | async-start | bytes 2359296 | tf_op jit(solution)/shard_map/ranks/all_to_all | solution.py:387
  62.6 26.0 %collective-permute-start.6 = (bf16[256,1024]{1,0:T(8,128)(2,1)}, bf16[256,1024]{1,0:T(8,128)(2,1)S(1)}, u32[]{:S(2)}, u32[]{:S(2)}) collective-permute-start(bf16[256,1024]{1,0:T(8,128)(2,1)} %collective-permute-done.5.refs_1_), channel_id=1, source_target_pairs={{8,24},{4,20},{24,8},{20,4},{9,25},{5,21},{25,9},{21,5},{10,26},{6... | collective-permute-start | bytes 1572872 | tf_op jit(solution)/shard_map/swap_w_1/ppermute | solution.py:369
  63.3 25.3 %collective-permute-start.8 = (bf16[256,1024]{1,0:T(8,128)(2,1)}, bf16[256,1024]{1,0:T(8,128)(2,1)S(1)}, u32[]{:S(2)}, u32[]{:S(2)}) collective-permute-start(bf16[256,1024]{1,0:T(8,128)(2,1)} %copy-done.10), channel_id=1, source_target_pairs={{0,16},{12,28},{16,0},{28,12},{1,17},{13,29},{17,1},{29,13},{2,18}... | collective-permute-start | bytes 1572872 | tf_op jit(solution)/shard_map/swap_w_2/ppermute | solution.py:369
  66.3 22.3 %collective-permute-start.10 = (bf16[256,1024]{1,0:T(8,128)(2,1)}, bf16[256,1024]{1,0:T(8,128)(2,1)S(1)}, u32[]{:S(2)}, u32[]{:S(2)}) collective-permute-start(bf16[256,1024]{1,0:T(8,128)(2,1)} %copy-done.2), channel_id=1, source_target_pairs={{8,24},{4,20},{24,8},{20,4},{9,25},{5,21},{25,9},{21,5},{10,26},{6... | collective-permute-start | bytes 1572872 | tf_op jit(solution)/shard_map/swap_w_3/ppermute | solution.py:369
  67.1 21.6 %collective-permute-start.14 = (bf16[128,1024]{1,0:T(8,128)(2,1)S(1)}, bf16[128,1024]{1,0:T(8,128)(2,1)S(1)}, u32[]{:S(2)}, u32[]{:S(2)}) collective-permute-start(bf16[128,1024]{1,0:T(8,128)(2,1)S(1)} %collective-permute-done.13.refs_5_), channel_id=1, source_target_pairs={{0,16},{12,28},{16,0},{28,12},{1,17},{13,29},{17,1},{29,13},{2,18}... | collective-permute-start | bytes 786440 | tf_op jit(solution)/shard_map/swap_w_5/ppermute | solution.py:369
  78.6 10.7 %collective-permute-start.12 = (bf16[128,1024]{1,0:T(8,128)(2,1)}, bf16[128,1024]{1,0:T(8,128)(2,1)S(1)}, u32[]{:S(2)}, u32[]{:S(2)}) collective-permute-start(bf16[128,1024]{1,0:T(8,128)(2,1)} %collective-permute-done.11.refs_4_), channel_id=1, source_target_pairs={{0,16},{12,28},{16,0},{28,12},{1,17},{13,29},{17,1},{29,13},{2,18}... | collective-permute-start | bytes 786440 | tf_op jit(solution)/shard_map/swap_w_4/ppermute | solution.py:369
  81.3 1.0 %copy-start.3 = (bf16[256,1024]{1,0:T(8,128)(2,1)S(1)}, bf16[256,1024]{1,0:T(8,128)(2,1)}, u32[]{:S(2)}) copy-start(bf16[256,1024]{1,0:T(8,128)(2,1)} %copy-done.2) | copy-start | bytes 1572868
  82.4 1.2 %copy-start.6 = (bf16[256,2048]{1,0:T(8,128)(2,1)S(1)}, bf16[256,2048]{1,0:T(8,128)(2,1)}, u32[]{:S(2)}) copy-start(bf16[256,2048]{1,0:T(8,128)(2,1)} %own_ref.3) | copy-start | bytes 3145732
  83.6 1.0 %copy-start.11 = (bf16[256,1024]{1,0:T(8,128)(2,1)S(1)}, bf16[256,1024]{1,0:T(8,128)(2,1)}, u32[]{:S(2)}) copy-start(bf16[256,1024]{1,0:T(8,128)(2,1)} %copy-done.10) | copy-start | bytes 1572868
  84.6 4.6 %copy-start.9 = (bf16[256,1024]{1,0:T(8,128)(2,1)S(1)}, bf16[256,1024]{1,0:T(8,128)(2,1)}, u32[]{:S(2)}) copy-start(bf16[256,1024]{1,0:T(8,128)(2,1)} %copy-done.8) | copy-start | bytes 1572868

commit v7 on v6

--- a/solution.py
+++ b/solution.py
@@ -25,22 +25,22 @@
         out_ref[span, :, part:] = up_ref[...]
 
 
-def project_kernel(blocks, scalars, x_ref, w_ref, mine_ref, other_ref, up_ref, out_ref):
+def project_kernel(blocks, part, scalars, x_ref, w_ref, mine_ref, other_ref, out_ref):
     rows = x_ref.shape[0] // blocks
-    rank, part = mine_ref.shape[1:]
+    rank, cut = mine_ref.shape[1], mine_ref.shape[2] - part
+
+    def over(a, b):
+        return lax.dot_general(a, b, ROWS_BY_ROWS, preferred_element_type=F32)
 
     def run(first, second):
         for b in range(blocks):
             s = scalars[b]
             span = slice(b * rows, (b + 1) * rows)
-            hidden = lax.dot_general(
-                x_ref[span, :part], first[s], ROWS_BY_ROWS, preferred_element_type=F32
-            ) + lax.dot_general(
-                x_ref[span, part:], second[s], ROWS_BY_ROWS, preferred_element_type=F32
-            )
-            low = lax.dot_general(
-                w_ref[span, :], up_ref[s], ROWS_BY_ROWS, preferred_element_type=F32
-            )
+            hidden = over(x_ref[span, :part], first[s, :, :part])
+            hidden += over(x_ref[span, part:], second[s, :, :part])
+            low = over(w_ref[span, :cut], first[s, :, part:])
+            if cut < w_ref.shape[1]:
+                low += over(w_ref[span, cut:], second[s, :, part:])
             out_ref[span, :rank] = hidden.astype(BF16)
             out_ref[span, rank:] = low.astype(BF16)
 
@@ -165,7 +165,7 @@
     )(jnp.stack([*slots, half, *begins]), *operands)
 
 
-def call(kernel, name, out_shape, scalars, operands, specs=None, scratch=(), flops=0, moved=0):
+def call(kernel, name, out_shape, scalars, operands, specs=None, scratch=(), flops=0, moved=0, limit=VMEM_LIMIT):
     whole = lambda shape: pl.BlockSpec(shape, lambda i, s: (0,) * len(shape))
     specs = specs or [whole(o.shape) for o in operands]
     single = isinstance(out_shape, jax.ShapeDtypeStruct)
@@ -179,7 +179,7 @@
             out_specs=whole(out_shape.shape) if single else [whole(o.shape) for o in out_shape],
             scratch_shapes=list(scratch),
         ),
-        compiler_params=pltpu.CompilerParams(vmem_limit_bytes=VMEM_LIMIT),
+        compiler_params=pltpu.CompilerParams(vmem_limit_bytes=limit),
         cost_estimate=pl.CostEstimate(flops=flops, bytes_accessed=moved, transcendentals=0),
         name=name,
     )(scalars, *operands)
@@ -192,36 +192,36 @@
 def payload(group, down, up, n):
     owned, rank, width = down.shape
     slab, part = up.shape[2], width // 2
+    cut = slab // 2 if slab % 256 == 0 else slab
     specs = [
         pl.BlockSpec((owned, rank, part), lambda i, s: (0, 0, s[0])),
-        pl.BlockSpec((owned, rank, slab), lambda i, s: (0, 0, 0)),
+        pl.BlockSpec((owned, rank, cut), lambda i, s: (0, 0, s[0] if cut < slab else 0)),
     ]
-    shape = bf16(n * owned, rank, part + slab)
-    return call(payload_kernel, "payload", shape, group[None], [down, up], specs)
-
-
-def project(group, slab_index, slots, x, weighted, received, other):
+    shape = bf16(n * owned, rank, part + cut)
+    return call(
+        payload_kernel, "payload", shape, group[None], [down, up], specs, limit=62 << 20
+    )
+
+
+def project(group, slab_index, slots, x, weighted, mine, other, slab):
     rows, width = x.shape
-    tenants, rank, part = other.shape
-    slab = received.shape[2] - part
+    rank = mine.shape[1]
     blocks = slots.shape[0]
-    whole = lambda i, s: (0, 0, 0)
     specs = [
         pl.BlockSpec((rows, width), lambda i, s: (0, 0)),
         pl.BlockSpec((rows, slab), lambda i, s: (0, s[blocks + 1])),
-        pl.BlockSpec((tenants, rank, part), whole),
-        pl.BlockSpec((tenants, rank, part), whole),
-        pl.BlockSpec((tenants, rank, slab), lambda i, s: (0, 0, part // slab)),
+        pl.BlockSpec(mine.shape, lambda i, s: (0, 0, 0)),
+        pl.BlockSpec(mine.shape, lambda i, s: (0, 0, 0)),
     ]
     return call(
-        functools.partial(project_kernel, blocks),
+        functools.partial(project_kernel, blocks, width // 2),
         "project",
         bf16(rows, 2 * rank),
         jnp.stack([*slots, group, slab_index]),
-        [x, weighted, received, other, received],
+        [x, weighted, mine, other],
         specs,
         flops=2 * rows * rank * (width + slab),
-        moved=2 * (rows + tenants * rank) * (width + slab),
+        moved=2 * (rows * (width + slab) + 2 * mine.size),
     )
 
 
@@ -333,7 +333,7 @@
             tiled=True,
         )
     with jax.named_scope("swap_a"):
-        down_other = swap("groups")(received[:, :, :half])
+        down_other = swap("groups")(received)
 
     row_sign = (1 - 2 * forget_flag).astype(BF16)
     weighted = out_grad * row_sign[:, None]
@@ -374,7 +374,9 @@
     for k in range(2, n - 1):
         last = advance(k, last, received)
     with jax.named_scope("ranks"):
-        part = project(group, slab_index, slots, layer_input, weighted, received, down_other)
+        part = project(
+            group, slab_index, slots, layer_input, weighted, received, down_other, slab
+        )
         here = pair_sum(part)
         there = rest_of(here, "tensor").astype(BF16)
         swapped = [None] * (len(arrived) + 2)

time: 94.2 us -> 92.2 us (0.979)
  local copies, waits for them, and re-layouts: 10.2 us -> 7.62 us
    unnamed x34 -> x30, local copies, waits for them, and re-layouts: 7.5 us -> 5.79 us
    ppermute x6, waiting for transfers between devices: 7.69 us -> 9.22 us  [advance(): new[parity] = lax.ppermute(last[1 - parity][span], 'seq', pairs)]
    all_to_all x1, waiting for transfers between devices: 14 us -> 12.6 us  [per_device(): lax.all_to_all(payload(group, adapter_down, adapter_up, n), 'seq', split_...]
    pallas_call x3, Pallas kernels: 3.46 us -> 4.41 us  [call(): pl.pallas_call(kernel, out_shape=out_shape, grid_spec=pltpu.PrefetchScala...]
  transfers between devices with their start and end apart: 17 -> 17, of which waited for: 7 -> 7; matrix products, arithmetic and copies ran while one was open for 4% -> 3% of each run, Pallas kernels for 10% -> 11%
where the time goes in v7:
time: 92.2 us; the launch traced here: 91.5 us
  starting transfers between devices  36.4 us (39%)
  waiting for transfers between devices  32.4 us (35%)
  Pallas kernels  12.5 us (14%)
  local copies, waits for them, and re-layouts  7.62 us (8%)
  other arithmetic  1.62 us (2%)
  between operations  1 us (1%)
    ppermute x6, starting transfers between devices, exchange(): lax.ppermute(after(arrived[j], before), ('groups', 'seq'), swap_pairs(pai...  13.9 us
    all_to_all x1, waiting for transfers between devices, per_device(): lax.all_to_all(payload(group, adapter_down, adapter_up, n), 'seq', split_...  12.6 us
    ppermute x6, waiting for transfers between devices, advance(): new[parity] = lax.ppermute(last[1 - parity][span], 'seq', pairs)  9.22 us
    ppermute x6, starting transfers between devices, advance(): new[parity] = lax.ppermute(last[1 - parity][span], 'seq', pairs)  8.04 us
    pallas_call x2, Pallas kernels, product(): pl.pallas_call(functools.partial(product_kernel, blocks, tiles), out_shap...  7.2 us
    all_to_all x1, starting transfers between devices, per_device(): lax.all_to_all(payload(group, adapter_down, adapter_up, n), 'seq', split_...  6.32 us
    unnamed x30, local copies, waits for them, and re-layouts  5.79 us
    ppermute x1, waiting for transfers between devices, per_device(): down_other = swap('groups')(received)  5.05 us
  transfers between devices with their start and end apart: 17, of which 7 were waited for; matrix products, arithmetic and copies ran while one was open for 3% of the time, Pallas kernels for 11%

profile of v7, /device:TPU:0, one launch (start us, length us, event | category | flops | bytes accessed | tf_op | source)
XLA Modules:
  0.0 91.5 jit_solution(5298848546759962117)
XLA Ops:
  0.6 0.0 copy-start.4
  0.6 0.0 copy-start.13
  0.7 0.0 copy-start.14
  0.7 0.0 copy-start.12
  0.7 1.8 %payload.1 = bf16[4,64,1152]{2,1,0:T(8,128)(2,1)} custom-call(s32[1]{0:T(128)} %bitcast.10.scalars, bf16[1,64,2048]{2,1,0:T(8,128)(2,1)} %down_ref.1, bf16[1,64,256]{2,1,0:T(8,128)(2,1)} %up_ref.1), custom_call_target="tpu_custom_call" | custom-call | tf_op jit(solution)/shard_map/adapters/payload/pallas_call | solution.py:172
  2.5 6.3 %all-to-all-start = ((bf16[4,64,1152]{2,1,0:T(8,128)(2,1)}), bf16[4,64,1152]{2,1,0:T(8,128)(2,1)S(1)}, u32[]{:S(2)}, u32[]{:S(2)}) async-start(bf16[4,64,1152]{2,1,0:T(8,128)(2,1)} %payload.1), calls=%async_computation | async-start | bytes 1179648 | tf_op jit(solution)/shard_map/adapters/all_to_all | solution.py:328
  8.8 0.0 copy-done.4
  8.8 0.8 constant_dynamic-slice_fusion
  9.7 2.0 %collective-permute-start.3 = (bf16[256,1024]{1,0:T(8,128)(2,1)}, bf16[256,1024]{1,0:T(8,128)(2,1)}, u32[]{:S(2)}, u32[]{:S(2)}) collective-permute-start(bf16[256,1024]{1,0:T(8,128)(2,1)} %constant_dynamic-slice_fusion), channel_id=1, source_target_pairs={{0,4},{4,0},{8,12},{12,8},{1,5},{5,1},{9,13},{13,9},{2,6},{6,2},{1... | collective-permute-start | bytes 1572872 | tf_op jit(solution)/shard_map/line_1_0_0/ppermute | solution.py:359
  11.7 1.5 %collective-permute-start.5 = (bf16[256,1024]{1,0:T(8,128)(2,1)}, bf16[256,1024]{1,0:T(8,128)(2,1)}, u32[]{:S(2)}, u32[]{:S(2)}) collective-permute-start(bf16[256,1024]{1,0:T(8,128)(2,1)} %constant_dynamic-slice_fusion), channel_id=1, source_target_pairs={{4,8},{8,4},{5,9},{9,5},{6,10},{10,6},{7,11},{11,7},{20,24},{24,20... | collective-permute-start | bytes 1572872 | tf_op jit(solution)/shard_map/line_1_1_0/ppermute | solution.py:359
  13.2 12.6 %all-to-all-done.mine_ref.down_ref = bf16[4,64,1152]{2,1,0:T(8,128)(2,1)S(1)} async-done(((bf16[4,64,1152]{2,1,0:T(8,128)(2,1)}), bf16[4,64,1152]{2,1,0:T(8,128)(2,1)S(1)}, u32[]{:S(2)}, u32[]{:S(2)}) %all-to-all-start) | async-done | bytes 589856 | tf_op jit(solution)/shard_map/adapters/all_to_all | solution.py:328
  25.8 1.5 %collective-permute-start = (bf16[4,64,1152]{2,1,0:T(8,128)(2,1)S(1)}, bf16[4,64,1152]{2,1,0:T(8,128)(2,1)S(1)}, u32[]{:S(2)}, u32[]{:S(2)}) collective-permute-start(bf16[4,64,1152]{2,1,0:T(8,128)(2,1)S(1)} %all-to-all-done.mine_ref.down_ref), channel_id=1, source_target_pairs={{0,16},{16,0},{1,17},{17,1},{2,18},{18,2},{3,19},{19,3},{4,20},{20... | collective-permute-start | bytes 1769480 | tf_op jit(solution)/shard_map/swap_a/ppermute | solution.py:336
  27.3 0.0 copy-done.13
  27.3 0.2 select_reduce_fusion
  27.5 1.3 %broadcast_multiply_fusion.w_ref.weighted_ref = bf16[384,1024]{1,0:T(8,128)(2,1)S(1)} fusion(bf16[384,1024]{1,0:T(8,128)(2,1)} %param.9, bf16[384]{0:T(512)(128)(2,1)S(1)} %subtract_convert_fusion), kind=kLoop, calls=%fused_computation | loop fusion | flops 393216 | bytes 1573632 | tf_op jit(solution)/shard_map/mul | solution.py:339
  28.8 3.2 %collective-permute-done.3.refs_0_ = bf16[256,1024]{1,0:T(8,128)(2,1)} collective-permute-done((bf16[256,1024]{1,0:T(8,128)(2,1)}, bf16[256,1024]{1,0:T(8,128)(2,1)}, u32[]{:S(2)}, u32[]{:S(2)}) %collective-permute-start.3) | collective-permute-done | bytes 524320 | tf_op jit(solution)/shard_map/line_1_0_0/ppermute | solution.py:359
  32.0 0.0 collective-permute-done.5.refs_1_
  32.0 1.3 %collective-permute-start.7 = (bf16[256,1024]{1,0:T(8,128)(2,1)}, bf16[256,1024]{1,0:T(8,128)(2,1)S(1)}, u32[]{:S(2)}, u32[]{:S(2)}) collective-permute-start(bf16[256,1024]{1,0:T(8,128)(2,1)} %collective-permute-done.5.refs_1_), channel_id=1, source_target_pairs={{4,0},{8,12},{5,1},{9,13},{6,2},{10,14},{7,3},{11,15},{20,16},{24,... | collective-permute-start | bytes 1572872 | tf_op jit(solution)/shard_map/line_2_0_0/ppermute | solution.py:359
  33.3 0.7 collective-permute-start.9
  34.0 5.1 %collective-permute-done.other_ref.down_ref = bf16[4,64,1152]{2,1,0:T(8,128)(2,1)S(1)} collective-permute-done((bf16[4,64,1152]{2,1,0:T(8,128)(2,1)S(1)}, bf16[4,64,1152]{2,1,0:T(8,128)(2,1)S(1)}, u32[]{:S(2)}, u32[]{:S(2)}) %collective-permute-start) | collective-permute-done | bytes 589856 | tf_op jit(solution)/shard_map/swap_a/ppermute | solution.py:336
  39.1 1.5 %collective-permute-start.4 = (bf16[256,1024]{1,0:T(8,128)(2,1)}, bf16[256,1024]{1,0:T(8,128)(2,1)S(1)}, u32[]{:S(2)}, u32[]{:S(2)}) collective-permute-start(bf16[256,1024]{1,0:T(8,128)(2,1)} %collective-permute-done.3.refs_0_), channel_id=1, source_target_pairs={{4,20},{0,16},{12,28},{8,24},{20,4},{16,0},{28,12},{24,8},{5,21},{... | collective-permute-start | bytes 1572872 | tf_op jit(solution)/shard_map/ranks/swap_w_0/ppermute | solution.py:369
  40.6 0.1 pad_add_fusion.1.scalars
  40.7 0.0 copy-done
  40.7 1.2 %project.1 = bf16[384,128]{1,0:T(8,128)(2,1)S(1)} custom-call(s32[5]{0:T(128)S(1)} %pad_add_fusion.1.scalars, bf16[384,2048]{1,0:T(8,128)(2,1)S(1)} %copy-done, bf16[384,1024]{1,0:T(8,128)(2,1)S(1)} %broadcast_multiply_fusion.w_ref.weighted_ref, bf16[4,64,1152]{2,1,0:T(8,128)(2,1)S(1)} %all-to-all-done.mine_ref.down_ref, ...), custom_call_target="tpu_custom_call" | custom-call | flops 113246208 | bytes 2949120 | tf_op jit(solution)/shard_map/ranks/project/pallas_call | solution.py:172
  41.9 0.1 collective-permute-start.1
  42.0 1.3 %collective-permute-done.1 = bf16[384,128]{1,0:T(8,128)(2,1)S(1)} collective-permute-done((bf16[384,128]{1,0:T(8,128)(2,1)S(1)}, bf16[384,128]{1,0:T(8,128)(2,1)S(1)}, u32[]{:S(2)}, u32[]{:S(2)}) %collective-permute-start.1) | collective-permute-done | bytes 98336 | tf_op jit(solution)/shard_map/ranks/psum_pipe/ppermute | solution.py:298
  43.3 1.6 %collective-permute-start.2 = (bf16[384,128]{1,0:T(8,128)(2,1)S(1)}, bf16[384,128]{1,0:T(8,128)(2,1)S(1)}, u32[]{:S(2)}, u32[]{:S(2)}) collective-permute-start(bf16[384,128]{1,0:T(8,128)(2,1)S(1)} %add_convert_fusion.here_ref), channel_id=1, source_target_pairs={{0,2},{2,0},{1,3},{3,1},{4,6},{6,4},{5,7},{7,5},{8,10},{10,8},{9,1... | collective-permute-start | bytes 294920 | tf_op jit(solution)/shard_map/ranks/psum_tensor/ppermute | solution.py:298
  44.9 0.1 pad_add_fusion.scalars
  45.0 3.3 %collective-permute-done.2.there_ref = bf16[384,128]{1,0:T(8,128)(2,1)S(1)} collective-permute-done((bf16[384,128]{1,0:T(8,128)(2,1)S(1)}, bf16[384,128]{1,0:T(8,128)(2,1)S(1)}, u32[]{:S(2)}, u32[]{:S(2)}) %collective-permute-start.2) | collective-permute-done | bytes 98336 | tf_op jit(solution)/shard_map/ranks/psum_tensor/ppermute | solution.py:298
  48.2 1.3 %adapter_grads.1 = (bf16[4,64,2304]{2,1,0:T(8,128)(2,1)S(1)}, bf16[384,64]{1,0:T(8,128)(2,1)S(1)}) custom-call(s32[4]{0:T(128)S(1)} %pad_add_fusion.scalars, bf16[384,2048]{1,0:T(8,128)(2,1)S(1)} %copy-done, bf16[384,1024]{1,0:T(8,128)(2,1)S(1)} %broadcast_multiply_fusion.w_ref.weighted_ref, bf16[384,128]{1,0:T(8,128)(2,1)S(1)} %add_convert_fusion.here_ref, ...), custom_call_target="tpu_custom_call" | custom-call | flops 113246208 | bytes 2949120 | tf_op jit(solution)/shard_map/ranks/adapter_grads/pallas_call | solution.py:172
  49.6 1.0 %copy-done.1 = bf16[4,64,2304]{2,1,0:T(8,128)(2,1)} copy-done((bf16[4,64,2304]{2,1,0:T(8,128)(2,1)}, bf16[4,64,2304]{2,1,0:T(8,128)(2,1)S(1)}, u32[]{:S(2)}) %copy-start.1) | copy-done | bytes 1179672
  50.6 0.6 copy-done.10
  51.2 0.0 collective-permute-done.7.refs_2_
  51.2 0.0 collective-permute-done.9.refs_3_
  51.2 0.0 collective-permute-done.4.refs_0_
  51.3 0.0 copy-start.6
  51.3 0.8 copy-done.2
  52.1 0.8 fusion
  52.9 1.3 %collective-permute-start.13 = (bf16[128,1024]{1,0:T(8,128)(2,1)}, bf16[128,1024]{1,0:T(8,128)(2,1)S(1)}, u32[]{:S(2)}, u32[]{:S(2)}) collective-permute-start(bf16[128,1024]{1,0:T(8,128)(2,1)} %get-tuple-element.29), channel_id=1, source_target_pairs={{4,0},{8,12},{5,1},{9,13},{6,2},{10,14},{7,3},{11,15},{20,16},{24,... | collective-permute-start | bytes 786440 | tf_op jit(solution)/shard_map/ranks/line_3_0_1/ppermute | solution.py:359
  54.2 1.3 %collective-permute-start.11 = (bf16[128,1024]{1,0:T(8,128)(2,1)}, bf16[128,1024]{1,0:T(8,128)(2,1)}, u32[]{:S(2)}, u32[]{:S(2)}) collective-permute-start(bf16[128,1024]{1,0:T(8,128)(2,1)} %get-tuple-element.30), channel_id=1, source_target_pairs={{4,0},{8,12},{5,1},{9,13},{6,2},{10,14},{7,3},{11,15},{20,16},{24,... | collective-permute-start | bytes 786440 | tf_op jit(solution)/shard_map/ranks/line_3_0_0/ppermute | solution.py:359
  55.5 0.1 stack.64.scalars
  55.6 0.1 stack.59.scalars
  55.7 5.0 %all-to-all-start.1 = ((bf16[4,64,2304]{2,1,0:T(8,128)(2,1)}), bf16[4,64,2304]{2,1,0:T(8,128)(2,1)S(1)}, u32[]{:S(2)}, u32[]{:S(2)}) async-start(bf16[4,64,2304]{2,1,0:T(8,128)(2,1)} %copy-done.1), calls=%async_computation.1 | async-start | bytes 2359296 | tf_op jit(solution)/shard_map/ranks/all_to_all | solution.py:389
  60.7 0.7 collective-permute-start.6
  61.4 2.7 %collective-permute-start.8 = (bf16[256,1024]{1,0:T(8,128)(2,1)}, bf16[256,1024]{1,0:T(8,128)(2,1)S(1)}, u32[]{:S(2)}, u32[]{:S(2)}) collective-permute-start(bf16[256,1024]{1,0:T(8,128)(2,1)} %copy-done.8), channel_id=1, source_target_pairs={{0,16},{12,28},{16,0},{28,12},{1,17},{13,29},{17,1},{29,13},{2,18}... | collective-permute-start | bytes 1572872 | tf_op jit(solution)/shard_map/swap_w_2/ppermute | solution.py:369
  64.1 0.7 collective-permute-start.10
  64.8 0.0 collective-permute-done.13.refs_5_
  64.8 5.9 %collective-permute-start.14 = (bf16[128,1024]{1,0:T(8,128)(2,1)S(1)}, bf16[128,1024]{1,0:T(8,128)(2,1)S(1)}, u32[]{:S(2)}, u32[]{:S(2)}) collective-permute-start(bf16[128,1024]{1,0:T(8,128)(2,1)S(1)} %collective-permute-done.13.refs_5_), channel_id=1, source_target_pairs={{0,16},{12,28},{16,0},{28,12},{1,17},{13,29},{17,1},{29,13},{2,18}... | collective-permute-start | bytes 786440 | tf_op jit(solution)/shard_map/swap_w_5/ppermute | solution.py:369
  70.7 6.0 %collective-permute-done.11.refs_4_ = bf16[128,1024]{1,0:T(8,128)(2,1)} collective-permute-done((bf16[128,1024]{1,0:T(8,128)(2,1)}, bf16[128,1024]{1,0:T(8,128)(2,1)}, u32[]{:S(2)}, u32[]{:S(2)}) %collective-permute-start.11) | collective-permute-done | bytes 262176 | tf_op jit(solution)/shard_map/ranks/line_3_0_0/ppermute | solution.py:359
  76.7 2.4 %collective-permute-start.12 = (bf16[128,1024]{1,0:T(8,128)(2,1)}, bf16[128,1024]{1,0:T(8,128)(2,1)S(1)}, u32[]{:S(2)}, u32[]{:S(2)}) collective-permute-start(bf16[128,1024]{1,0:T(8,128)(2,1)} %collective-permute-done.11.refs_4_), channel_id=1, source_target_pairs={{0,16},{12,28},{16,0},{28,12},{1,17},{13,29},{17,1},{29,13},{2,18}... | collective-permute-start | bytes 786440 | tf_op jit(solution)/shard_map/swap_w_4/ppermute | solution.py:369
  79.1 0.0 copy-done.11
  79.1 0.0 copy-start.3
  79.1 1.0 %copy-done.3 = bf16[256,1024]{1,0:T(8,128)(2,1)S(1)} copy-done((bf16[256,1024]{1,0:T(8,128)(2,1)S(1)}, bf16[256,1024]{1,0:T(8,128)(2,1)}, u32[]{:S(2)}) %copy-start.3) | copy-done | bytes 524312
  80.1 1.2 %copy-done.5 = bf16[256,2048]{1,0:T(8,128)(2,1)S(1)} copy-done((bf16[256,2048]{1,0:T(8,128)(2,1)S(1)}, bf16[256,2048]{1,0:T(8,128)(2,1)}, u32[]{:S(2)}) %copy-start.5) | copy-done | bytes 1048600
  81.4 1.0 %copy-done.9 = bf16[256,1024]{1,0:T(8,128)(2,1)S(1)} copy-done((bf16[256,1024]{1,0:T(8,128)(2,1)S(1)}, bf16[256,1024]{1,0:T(8,128)(2,1)}, u32[]{:S(2)}) %copy-start.9) | copy-done | bytes 524312
  82.4 4.0 %product.2.refs_6_ = bf16[384,2048]{1,0:T(8,128)(2,1)} custom-call(s32[11]{0:T(128)S(1)} %stack.64.scalars, bf16[384,1024]{1,0:T(8,128)(2,1)S(1)} %broadcast_multiply_fusion.w_ref.weighted_ref, bf16[384,64]{1,0:T(8,128)(2,1)S(1)} %copy-done.11, bf16[4,64,1152]{2,1,0:T(8,128)(2,1)S(1)} %all-to-all-done.mine_ref.down_ref, bf16[256,2048]{1,0:T(8,128)(2,1)S(1)} %copy-done.5, ...), custom_call_target="tpu_custom_call" | custom-call | flops 9663676416 | bytes 2883584 | tf_op jit(solution)/shard_map/product/pallas_call | solution.py:144
  86.4 0.0 collective-permute-done.6.refs_1_
  86.4 0.0 collective-permute-done.8.refs_2_
  86.4 0.0 collective-permute-done.10.refs_3_
  86.4 0.0 collective-permute-done.14.refs_5_
  86.4 0.9 %collective-permute-done.12.refs_4_ = bf16[128,1024]{1,0:T(8,128)(2,1)S(1)} collective-permute-done((bf16[128,1024]{1,0:T(8,128)(2,1)}, bf16[128,1024]{1,0:T(8,128)(2,1)S(1)}, u32[]{:S(2)}, u32[]{:S(2)}) %collective-permute-start.12) | collective-permute-done | bytes 262176 | tf_op jit(solution)/shard_map/swap_w_4/ppermute | solution.py:369
  87.3 3.2 %product.3 = bf16[384,2048]{1,0:T(8,128)(2,1)} custom-call(s32[11]{0:T(128)S(1)} %stack.59.scalars, bf16[384,1024]{1,0:T(8,128)(2,1)S(1)} %broadcast_multiply_fusion.w_ref.weighted_ref, bf16[384,64]{1,0:T(8,128)(2,1)S(1)} %copy-done.11, bf16[4,64,1152]{2,1,0:T(8,128)(2,1)S(1)} %collective-permute-done.other_ref.down_ref, ...), custom_call_target="tpu_custom_call", output_to_operand_aliasing={{}: (11, {})} | custom-call | flops 9663676416 | bytes 2883584 | tf_op jit(solution)/shard_map/product/pallas_call | solution.py:144
  90.6 0.0 all-to-all-done.1.got_ref
  90.6 0.9 %owner_sums.1 = (f32[1,64,2048]{2,1,0:T(8,128)}, f32[1,64,256]{2,1,0:T(8,128)}) custom-call(bf16[4,64,2304]{2,1,0:T(8,128)(2,1)S(1)} %all-to-all-done.1.got_ref), custom_call_target="tpu_custom_call" | custom-call | flops 589824 | bytes 1179648 | tf_op jit(solution)/shard_map/owner_sums/pallas_call | solution.py:255
  (16 shorter events, 0.1 us)
Async XLA Ops:
  0.6 8.2 %copy-start.4 = (bf16[256,2048]{1,0:T(8,128)(2,1)S(1)}, bf16[256,2048]{1,0:T(8,128)(2,1)}, u32[]{:S(2)}) copy-start(bf16[256,2048]{1,0:T(8,128)(2,1)} %own_ref.3) | copy-start | bytes 3145732
  0.6 26.7 %copy-start.13 = (s32[4]{0:T(128)S(1)}, s32[4]{0:T(128)}, u32[]{:S(2)}) copy-start(s32[4]{0:T(128)} %param.14) | copy-start | bytes 52
  0.7 26.7 %copy-start.14 = (s32[3,1]{0,1:T(1,128)S(1)}, s32[3,1]{0,1:T(1,128)}, u32[]{:S(2)}) copy-start(s32[3,1]{0,1:T(1,128)} %param.13) | copy-start | bytes 40
  0.7 26.8 %copy-start.12 = (s32[384]{0:T(512)S(1)}, s32[384]{0:T(512)}, u32[]{:S(2)}) copy-start(s32[384]{0:T(512)} %param.15) | copy-start | bytes 4612
  2.5 23.3 %all-to-all-start = ((bf16[4,64,1152]{2,1,0:T(8,128)(2,1)}), bf16[4,64,1152]{2,1,0:T(8,128)(2,1)S(1)}, u32[]{:S(2)}, u32[]{:S(2)}) async-start(bf16[4,64,1152]{2,1,0:T(8,128)(2,1)} %payload.1), calls=%async_computation | async-start | bytes 1179648 | tf_op jit(solution)/shard_map/adapters/all_to_all | solution.py:328
  8.8 31.8 %copy-start = (bf16[384,2048]{1,0:T(8,128)(2,1)S(1)}, bf16[384,2048]{1,0:T(8,128)(2,1)}, u32[]{:S(2)}) copy-start(bf16[384,2048]{1,0:T(8,128)(2,1)} %x_ref.3) | copy-start | bytes 4718596
  9.7 22.3 %collective-permute-start.3 = (bf16[256,1024]{1,0:T(8,128)(2,1)}, bf16[256,1024]{1,0:T(8,128)(2,1)}, u32[]{:S(2)}, u32[]{:S(2)}) collective-permute-start(bf16[256,1024]{1,0:T(8,128)(2,1)} %constant_dynamic-slice_fusion), channel_id=1, source_target_pairs={{0,4},{4,0},{8,12},{12,8},{1,5},{5,1},{9,13},{13,9},{2,6},{6,2},{1... | collective-permute-start | bytes 1572872 | tf_op jit(solution)/shard_map/line_1_0_0/ppermute | solution.py:359
  11.7 20.3 %collective-permute-start.5 = (bf16[256,1024]{1,0:T(8,128)(2,1)}, bf16[256,1024]{1,0:T(8,128)(2,1)}, u32[]{:S(2)}, u32[]{:S(2)}) collective-permute-start(bf16[256,1024]{1,0:T(8,128)(2,1)} %constant_dynamic-slice_fusion), channel_id=1, source_target_pairs={{4,8},{8,4},{5,9},{9,5},{6,10},{10,6},{7,11},{11,7},{20,24},{24,20... | collective-permute-start | bytes 1572872 | tf_op jit(solution)/shard_map/line_1_1_0/ppermute | solution.py:359
  25.8 13.3 %collective-permute-start = (bf16[4,64,1152]{2,1,0:T(8,128)(2,1)S(1)}, bf16[4,64,1152]{2,1,0:T(8,128)(2,1)S(1)}, u32[]{:S(2)}, u32[]{:S(2)}) collective-permute-start(bf16[4,64,1152]{2,1,0:T(8,128)(2,1)S(1)} %all-to-all-done.mine_ref.down_ref), channel_id=1, source_target_pairs={{0,16},{16,0},{1,17},{17,1},{2,18},{18,2},{3,19},{19,3},{4,20},{20... | collective-permute-start | bytes 1769480 | tf_op jit(solution)/shard_map/swap_a/ppermute | solution.py:336
  32.0 19.2 %collective-permute-start.7 = (bf16[256,1024]{1,0:T(8,128)(2,1)}, bf16[256,1024]{1,0:T(8,128)(2,1)S(1)}, u32[]{:S(2)}, u32[]{:S(2)}) collective-permute-start(bf16[256,1024]{1,0:T(8,128)(2,1)} %collective-permute-done.5.refs_1_), channel_id=1, source_target_pairs={{4,0},{8,12},{5,1},{9,13},{6,2},{10,14},{7,3},{11,15},{20,16},{24,... | collective-permute-start | bytes 1572872 | tf_op jit(solution)/shard_map/line_2_0_0/ppermute | solution.py:359
  33.3 17.9 %collective-permute-start.9 = (bf16[256,1024]{1,0:T(8,128)(2,1)}, bf16[256,1024]{1,0:T(8,128)(2,1)S(1)}, u32[]{:S(2)}, u32[]{:S(2)}) collective-permute-start(bf16[256,1024]{1,0:T(8,128)(2,1)} %collective-permute-done.3.refs_0_), channel_id=1, source_target_pairs={{4,8},{8,4},{5,9},{9,5},{6,10},{10,6},{7,11},{11,7},{20,24},{24,20... | collective-permute-start | bytes 1572872 | tf_op jit(solution)/shard_map/line_2_1_0/ppermute | solution.py:359
  39.1 12.2 %collective-permute-start.4 = (bf16[256,1024]{1,0:T(8,128)(2,1)}, bf16[256,1024]{1,0:T(8,128)(2,1)S(1)}, u32[]{:S(2)}, u32[]{:S(2)}) collective-permute-start(bf16[256,1024]{1,0:T(8,128)(2,1)} %collective-permute-done.3.refs_0_), channel_id=1, source_target_pairs={{4,20},{0,16},{12,28},{8,24},{20,4},{16,0},{28,12},{24,8},{5,21},{... | collective-permute-start | bytes 1572872 | tf_op jit(solution)/shard_map/ranks/swap_w_0/ppermute | solution.py:369
  41.9 1.4 %collective-permute-start.1 = (bf16[384,128]{1,0:T(8,128)(2,1)S(1)}, bf16[384,128]{1,0:T(8,128)(2,1)S(1)}, u32[]{:S(2)}, u32[]{:S(2)}) collective-permute-start(bf16[384,128]{1,0:T(8,128)(2,1)S(1)} %project.1), channel_id=1, source_target_pairs={{0,1},{1,0},{2,3},{3,2},{4,5},{5,4},{6,7},{7,6},{8,9},{9,8},{10,11... | collective-permute-start | bytes 294920 | tf_op jit(solution)/shard_map/ranks/psum_pipe/ppermute | solution.py:298
  43.3 4.9 %collective-permute-start.2 = (bf16[384,128]{1,0:T(8,128)(2,1)S(1)}, bf16[384,128]{1,0:T(8,128)(2,1)S(1)}, u32[]{:S(2)}, u32[]{:S(2)}) collective-permute-start(bf16[384,128]{1,0:T(8,128)(2,1)S(1)} %add_convert_fusion.here_ref), channel_id=1, source_target_pairs={{0,2},{2,0},{1,3},{3,1},{4,6},{6,4},{5,7},{7,5},{8,10},{10,8},{9,1... | collective-permute-start | bytes 294920 | tf_op jit(solution)/shard_map/ranks/psum_tensor/ppermute | solution.py:298
  49.6 1.0 %copy-start.1 = (bf16[4,64,2304]{2,1,0:T(8,128)(2,1)}, bf16[4,64,2304]{2,1,0:T(8,128)(2,1)S(1)}, u32[]{:S(2)}) copy-start(bf16[4,64,2304]{2,1,0:T(8,128)(2,1)S(1)} %get-tuple-element.20) | copy-start | bytes 3538948
  50.6 0.6 copy-start.10
  51.2 1.7 %copy-start.8 = (bf16[256,1024]{1,0:T(8,128)(2,1)}, bf16[256,1024]{1,0:T(8,128)(2,1)S(1)}, u32[]{:S(2)}) copy-start(bf16[256,1024]{1,0:T(8,128)(2,1)S(1)} %collective-permute-done.7.refs_2_) | copy-start | bytes 1572868
  51.2 0.8 copy-start.2
  51.3 1.6 %copy-start.6 = (bf16[256,1024]{1,0:T(8,128)(2,1)}, bf16[256,1024]{1,0:T(8,128)(2,1)S(1)}, u32[]{:S(2)}) copy-start(bf16[256,1024]{1,0:T(8,128)(2,1)S(1)} %collective-permute-done.4.refs_0_) | copy-start | bytes 1572868
  52.1 27.0 %copy-start.11 = (bf16[384,64]{1,0:T(8,128)(2,1)S(1)}, bf16[384,64]{1,0:T(8,128)(2,1)}, u32[]{:S(2)}) copy-start(bf16[384,64]{1,0:T(8,128)(2,1)} %copy-done.10) | copy-start | bytes 147460
  52.9 11.9 %collective-permute-start.13 = (bf16[128,1024]{1,0:T(8,128)(2,1)}, bf16[128,1024]{1,0:T(8,128)(2,1)S(1)}, u32[]{:S(2)}, u32[]{:S(2)}) collective-permute-start(bf16[128,1024]{1,0:T(8,128)(2,1)} %get-tuple-element.29), channel_id=1, source_target_pairs={{4,0},{8,12},{5,1},{9,13},{6,2},{10,14},{7,3},{11,15},{20,16},{24,... | collective-permute-start | bytes 786440 | tf_op jit(solution)/shard_map/ranks/line_3_0_1/ppermute | solution.py:359
  54.2 22.5 %collective-permute-start.11 = (bf16[128,1024]{1,0:T(8,128)(2,1)}, bf16[128,1024]{1,0:T(8,128)(2,1)}, u32[]{:S(2)}, u32[]{:S(2)}) collective-permute-start(bf16[128,1024]{1,0:T(8,128)(2,1)} %get-tuple-element.30), channel_id=1, source_target_pairs={{4,0},{8,12},{5,1},{9,13},{6,2},{10,14},{7,3},{11,15},{20,16},{24,... | collective-permute-start | bytes 786440 | tf_op jit(solution)/shard_map/ranks/line_3_0_0/ppermute | solution.py:359
  55.7 34.9 %all-to-all-start.1 = ((bf16[4,64,2304]{2,1,0:T(8,128)(2,1)}), bf16[4,64,2304]{2,1,0:T(8,128)(2,1)S(1)}, u32[]{:S(2)}, u32[]{:S(2)}) async-start(bf16[4,64,2304]{2,1,0:T(8,128)(2,1)} %copy-done.1), calls=%async_computation.1 | async-start | bytes 2359296 | tf_op jit(solution)/shard_map/ranks/all_to_all | solution.py:389
  60.7 25.7 %collective-permute-start.6 = (bf16[256,1024]{1,0:T(8,128)(2,1)}, bf16[256,1024]{1,0:T(8,128)(2,1)S(1)}, u32[]{:S(2)}, u32[]{:S(2)}) collective-permute-start(bf16[256,1024]{1,0:T(8,128)(2,1)} %collective-permute-done.5.refs_1_), channel_id=1, source_target_pairs={{8,24},{4,20},{24,8},{20,4},{9,25},{5,21},{25,9},{21,5},{10,26},{6... | collective-permute-start | bytes 1572872 | tf_op jit(solution)/shard_map/swap_w_1/ppermute | solution.py:369
  61.4 25.0 %collective-permute-start.8 = (bf16[256,1024]{1,0:T(8,128)(2,1)}, bf16[256,1024]{1,0:T(8,128)(2,1)S(1)}, u32[]{:S(2)}, u32[]{:S(2)}) collective-permute-start(bf16[256,1024]{1,0:T(8,128)(2,1)} %copy-done.8), channel_id=1, source_target_pairs={{0,16},{12,28},{16,0},{28,12},{1,17},{13,29},{17,1},{29,13},{2,18}... | collective-permute-start | bytes 1572872 | tf_op jit(solution)/shard_map/swap_w_2/ppermute | solution.py:369
  64.1 22.3 %collective-permute-start.10 = (bf16[256,1024]{1,0:T(8,128)(2,1)}, bf16[256,1024]{1,0:T(8,128)(2,1)S(1)}, u32[]{:S(2)}, u32[]{:S(2)}) collective-permute-start(bf16[256,1024]{1,0:T(8,128)(2,1)} %copy-done.2), channel_id=1, source_target_pairs={{8,24},{4,20},{24,8},{20,4},{9,25},{5,21},{25,9},{21,5},{10,26},{6... | collective-permute-start | bytes 1572872 | tf_op jit(solution)/shard_map/swap_w_3/ppermute | solution.py:369
  64.8 21.6 %collective-permute-start.14 = (bf16[128,1024]{1,0:T(8,128)(2,1)S(1)}, bf16[128,1024]{1,0:T(8,128)(2,1)S(1)}, u32[]{:S(2)}, u32[]{:S(2)}) collective-permute-start(bf16[128,1024]{1,0:T(8,128)(2,1)S(1)} %collective-permute-done.13.refs_5_), channel_id=1, source_target_pairs={{0,16},{12,28},{16,0},{28,12},{1,17},{13,29},{17,1},{29,13},{2,18}... | collective-permute-start | bytes 786440 | tf_op jit(solution)/shard_map/swap_w_5/ppermute | solution.py:369
  76.7 10.7 %collective-permute-start.12 = (bf16[128,1024]{1,0:T(8,128)(2,1)}, bf16[128,1024]{1,0:T(8,128)(2,1)S(1)}, u32[]{:S(2)}, u32[]{:S(2)}) collective-permute-start(bf16[128,1024]{1,0:T(8,128)(2,1)} %collective-permute-done.11.refs_4_), channel_id=1, source_target_pairs={{0,16},{12,28},{16,0},{28,12},{1,17},{13,29},{17,1},{29,13},{2,18}... | collective-permute-start | bytes 786440 | tf_op jit(solution)/shard_map/swap_w_4/ppermute | solution.py:369
  79.1 1.0 %copy-start.3 = (bf16[256,1024]{1,0:T(8,128)(2,1)S(1)}, bf16[256,1024]{1,0:T(8,128)(2,1)}, u32[]{:S(2)}) copy-start(bf16[256,1024]{1,0:T(8,128)(2,1)} %copy-done.2) | copy-start | bytes 1572868
  80.1 1.2 %copy-start.5 = (bf16[256,2048]{1,0:T(8,128)(2,1)S(1)}, bf16[256,2048]{1,0:T(8,128)(2,1)}, u32[]{:S(2)}) copy-start(bf16[256,2048]{1,0:T(8,128)(2,1)} %own_ref.3) | copy-start | bytes 3145732
  81.3 1.0 %copy-start.9 = (bf16[256,1024]{1,0:T(8,128)(2,1)S(1)}, bf16[256,1024]{1,0:T(8,128)(2,1)}, u32[]{:S(2)}) copy-start(bf16[256,1024]{1,0:T(8,128)(2,1)} %copy-done.8) | copy-start | bytes 1572868
  82.4 4.9 %copy-start.7 = (bf16[256,1024]{1,0:T(8,128)(2,1)S(1)}, bf16[256,1024]{1,0:T(8,128)(2,1)}, u32[]{:S(2)}) copy-start(bf16[256,1024]{1,0:T(8,128)(2,1)} %copy-done.6) | copy-start | bytes 1572868

commit v8 on v7

--- a/solution.py
+++ b/solution.py
@@ -389,7 +389,7 @@
         got = lax.all_to_all(table, "seq", split_axis=0, concat_axis=0, tiled=True)
     for j in range(len(arrived)):
         if swapped[j] is None:
-            swapped[j] = exchange(j, *([table] if j in (1, 2, 3) else []))
+            swapped[j] = exchange(j, *([table] if j in (2, 3) else [swapped[0]] if j == 1 else []))
 
     common = (slots, begins, weighted, low_b)
     first = product(group, *common, received, value_weight, arrived)

time: 92.2 us -> 91.5 us (level)
  no operation moved by 1% of the time
where the time goes in v8:
time: 91.5 us; the launch traced here: 90.8 us
  starting transfers between devices  36.4 us (40%)
  waiting for transfers between devices  31.7 us (35%)
  Pallas kernels  12.5 us (14%)
  local copies, waits for them, and re-layouts  7.62 us (8%)
  other arithmetic  1.62 us (2%)
  between operations  0.99 us (1%)
    ppermute x6, starting transfers between devices, exchange(): lax.ppermute(after(arrived[j], before), ('groups', 'seq'), swap_pairs(pai...  13.9 us
    all_to_all x1, waiting for transfers between devices, per_device(): lax.all_to_all(payload(group, adapter_down, adapter_up, n), 'seq', split_...  12.6 us
    ppermute x6, waiting for transfers between devices, advance(): new[parity] = lax.ppermute(last[1 - parity][span], 'seq', pairs)  9.22 us
    ppermute x6, starting transfers between devices, advance(): new[parity] = lax.ppermute(last[1 - parity][span], 'seq', pairs)  8.03 us
    pallas_call x2, Pallas kernels, product(): pl.pallas_call(functools.partial(product_kernel, blocks, tiles), out_shap...  7.2 us
    all_to_all x1, starting transfers between devices, per_device(): lax.all_to_all(payload(group, adapter_down, adapter_up, n), 'seq', split_...  6.32 us
    unnamed x30, local copies, waits for them, and re-layouts  5.79 us
    ppermute x1, waiting for transfers between devices, per_device(): down_other = swap('groups')(received)  5.05 us
  transfers between devices with their start and end apart: 17, of which 7 were waited for; matrix products, arithmetic and copies ran while one was open for 3% of the time, Pallas kernels for 11%

profile of v8, /device:TPU:0, one launch (start us, length us, event | category | flops | bytes accessed | tf_op | source)
XLA Modules:
  0.0 90.8 jit_solution(17091281180152838554)
XLA Ops:
  0.6 0.0 copy-start.4
  0.6 0.0 copy-start.13
  0.7 0.0 copy-start.14
  0.7 0.0 copy-start.12
  0.7 1.8 %payload.1 = bf16[4,64,1152]{2,1,0:T(8,128)(2,1)} custom-call(s32[1]{0:T(128)} %bitcast.10.scalars, bf16[1,64,2048]{2,1,0:T(8,128)(2,1)} %down_ref.1, bf16[1,64,256]{2,1,0:T(8,128)(2,1)} %up_ref.1), custom_call_target="tpu_custom_call" | custom-call | tf_op jit(solution)/shard_map/adapters/payload/pallas_call | solution.py:172
  2.5 6.3 %all-to-all-start = ((bf16[4,64,1152]{2,1,0:T(8,128)(2,1)}), bf16[4,64,1152]{2,1,0:T(8,128)(2,1)S(1)}, u32[]{:S(2)}, u32[]{:S(2)}) async-start(bf16[4,64,1152]{2,1,0:T(8,128)(2,1)} %payload.1), calls=%async_computation | async-start | bytes 1179648 | tf_op jit(solution)/shard_map/adapters/all_to_all | solution.py:328
  8.8 0.0 copy-done.4
  8.8 0.8 constant_dynamic-slice_fusion
  9.7 2.0 %collective-permute-start.3 = (bf16[256,1024]{1,0:T(8,128)(2,1)}, bf16[256,1024]{1,0:T(8,128)(2,1)}, u32[]{:S(2)}, u32[]{:S(2)}) collective-permute-start(bf16[256,1024]{1,0:T(8,128)(2,1)} %constant_dynamic-slice_fusion), channel_id=1, source_target_pairs={{0,4},{4,0},{8,12},{12,8},{1,5},{5,1},{9,13},{13,9},{2,6},{6,2},{1... | collective-permute-start | bytes 1572872 | tf_op jit(solution)/shard_map/line_1_0_0/ppermute | solution.py:359
  11.7 1.5 %collective-permute-start.5 = (bf16[256,1024]{1,0:T(8,128)(2,1)}, bf16[256,1024]{1,0:T(8,128)(2,1)}, u32[]{:S(2)}, u32[]{:S(2)}) collective-permute-start(bf16[256,1024]{1,0:T(8,128)(2,1)} %constant_dynamic-slice_fusion), channel_id=1, source_target_pairs={{4,8},{8,4},{5,9},{9,5},{6,10},{10,6},{7,11},{11,7},{20,24},{24,20... | collective-permute-start | bytes 1572872 | tf_op jit(solution)/shard_map/line_1_1_0/ppermute | solution.py:359
  13.2 12.6 %all-to-all-done.mine_ref.down_ref = bf16[4,64,1152]{2,1,0:T(8,128)(2,1)S(1)} async-done(((bf16[4,64,1152]{2,1,0:T(8,128)(2,1)}), bf16[4,64,1152]{2,1,0:T(8,128)(2,1)S(1)}, u32[]{:S(2)}, u32[]{:S(2)}) %all-to-all-start) | async-done | bytes 589856 | tf_op jit(solution)/shard_map/adapters/all_to_all | solution.py:328
  25.8 1.5 %collective-permute-start = (bf16[4,64,1152]{2,1,0:T(8,128)(2,1)S(1)}, bf16[4,64,1152]{2,1,0:T(8,128)(2,1)S(1)}, u32[]{:S(2)}, u32[]{:S(2)}) collective-permute-start(bf16[4,64,1152]{2,1,0:T(8,128)(2,1)S(1)} %all-to-all-done.mine_ref.down_ref), channel_id=1, source_target_pairs={{0,16},{16,0},{1,17},{17,1},{2,18},{18,2},{3,19},{19,3},{4,20},{20... | collective-permute-start | bytes 1769480 | tf_op jit(solution)/shard_map/swap_a/ppermute | solution.py:336
  27.3 0.0 copy-done.13
  27.3 0.2 select_reduce_fusion
  27.5 1.3 %broadcast_multiply_fusion.w_ref.weighted_ref = bf16[384,1024]{1,0:T(8,128)(2,1)S(1)} fusion(bf16[384,1024]{1,0:T(8,128)(2,1)} %param.9, bf16[384]{0:T(512)(128)(2,1)S(1)} %subtract_convert_fusion), kind=kLoop, calls=%fused_computation | loop fusion | flops 393216 | bytes 1573632 | tf_op jit(solution)/shard_map/mul | solution.py:339
  28.8 3.2 %collective-permute-done.3.refs_0_ = bf16[256,1024]{1,0:T(8,128)(2,1)} collective-permute-done((bf16[256,1024]{1,0:T(8,128)(2,1)}, bf16[256,1024]{1,0:T(8,128)(2,1)}, u32[]{:S(2)}, u32[]{:S(2)}) %collective-permute-start.3) | collective-permute-done | bytes 524320 | tf_op jit(solution)/shard_map/line_1_0_0/ppermute | solution.py:359
  32.0 0.0 collective-permute-done.5.refs_1_
  32.0 1.3 %collective-permute-start.7 = (bf16[256,1024]{1,0:T(8,128)(2,1)}, bf16[256,1024]{1,0:T(8,128)(2,1)S(1)}, u32[]{:S(2)}, u32[]{:S(2)}) collective-permute-start(bf16[256,1024]{1,0:T(8,128)(2,1)} %collective-permute-done.5.refs_1_), channel_id=1, source_target_pairs={{4,0},{8,12},{5,1},{9,13},{6,2},{10,14},{7,3},{11,15},{20,16},{24,... | collective-permute-start | bytes 1572872 | tf_op jit(solution)/shard_map/line_2_0_0/ppermute | solution.py:359
  33.3 0.7 collective-permute-start.9
  34.0 5.1 %collective-permute-done.other_ref.down_ref = bf16[4,64,1152]{2,1,0:T(8,128)(2,1)S(1)} collective-permute-done((bf16[4,64,1152]{2,1,0:T(8,128)(2,1)S(1)}, bf16[4,64,1152]{2,1,0:T(8,128)(2,1)S(1)}, u32[]{:S(2)}, u32[]{:S(2)}) %collective-permute-start) | collective-permute-done | bytes 589856 | tf_op jit(solution)/shard_map/swap_a/ppermute | solution.py:336
  39.1 1.5 %collective-permute-start.4 = (bf16[256,1024]{1,0:T(8,128)(2,1)}, bf16[256,1024]{1,0:T(8,128)(2,1)S(1)}, u32[]{:S(2)}, u32[]{:S(2)}) collective-permute-start(bf16[256,1024]{1,0:T(8,128)(2,1)} %collective-permute-done.3.refs_0_), channel_id=1, source_target_pairs={{4,20},{0,16},{12,28},{8,24},{20,4},{16,0},{28,12},{24,8},{5,21},{... | collective-permute-start | bytes 1572872 | tf_op jit(solution)/shard_map/ranks/swap_w_0/ppermute | solution.py:369
  40.6 0.1 pad_add_fusion.1.scalars
  40.7 1.2 %project.1 = bf16[384,128]{1,0:T(8,128)(2,1)S(1)} custom-call(s32[5]{0:T(128)S(1)} %pad_add_fusion.1.scalars, bf16[384,2048]{1,0:T(8,128)(2,1)S(1)} %copy-done, bf16[384,1024]{1,0:T(8,128)(2,1)S(1)} %broadcast_multiply_fusion.w_ref.weighted_ref, bf16[4,64,1152]{2,1,0:T(8,128)(2,1)S(1)} %all-to-all-done.mine_ref.down_ref, ...), custom_call_target="tpu_custom_call" | custom-call | flops 113246208 | bytes 2949120 | tf_op jit(solution)/shard_map/ranks/project/pallas_call | solution.py:172
  41.9 0.1 collective-permute-start.1
  42.0 1.3 %collective-permute-done.1 = bf16[384,128]{1,0:T(8,128)(2,1)S(1)} collective-permute-done((bf16[384,128]{1,0:T(8,128)(2,1)S(1)}, bf16[384,128]{1,0:T(8,128)(2,1)S(1)}, u32[]{:S(2)}, u32[]{:S(2)}) %collective-permute-start.1) | collective-permute-done | bytes 98336 | tf_op jit(solution)/shard_map/ranks/psum_pipe/ppermute | solution.py:298
  43.3 1.6 %collective-permute-start.2 = (bf16[384,128]{1,0:T(8,128)(2,1)S(1)}, bf16[384,128]{1,0:T(8,128)(2,1)S(1)}, u32[]{:S(2)}, u32[]{:S(2)}) collective-permute-start(bf16[384,128]{1,0:T(8,128)(2,1)S(1)} %add_convert_fusion.here_ref), channel_id=1, source_target_pairs={{0,2},{2,0},{1,3},{3,1},{4,6},{6,4},{5,7},{7,5},{8,10},{10,8},{9,1... | collective-permute-start | bytes 294920 | tf_op jit(solution)/shard_map/ranks/psum_tensor/ppermute | solution.py:298
  44.9 0.1 pad_add_fusion.scalars
  45.0 3.3 %collective-permute-done.2.there_ref = bf16[384,128]{1,0:T(8,128)(2,1)S(1)} collective-permute-done((bf16[384,128]{1,0:T(8,128)(2,1)S(1)}, bf16[384,128]{1,0:T(8,128)(2,1)S(1)}, u32[]{:S(2)}, u32[]{:S(2)}) %collective-permute-start.2) | collective-permute-done | bytes 98336 | tf_op jit(solution)/shard_map/ranks/psum_tensor/ppermute | solution.py:298
  48.2 1.3 %adapter_grads.1 = (bf16[4,64,2304]{2,1,0:T(8,128)(2,1)S(1)}, bf16[384,64]{1,0:T(8,128)(2,1)S(1)}) custom-call(s32[4]{0:T(128)S(1)} %pad_add_fusion.scalars, bf16[384,2048]{1,0:T(8,128)(2,1)S(1)} %copy-done, bf16[384,1024]{1,0:T(8,128)(2,1)S(1)} %broadcast_multiply_fusion.w_ref.weighted_ref, bf16[384,128]{1,0:T(8,128)(2,1)S(1)} %add_convert_fusion.here_ref, ...), custom_call_target="tpu_custom_call" | custom-call | flops 113246208 | bytes 2949120 | tf_op jit(solution)/shard_map/ranks/adapter_grads/pallas_call | solution.py:172
  49.6 0.0 copy-start.1
  49.6 1.0 %copy-done.1 = bf16[4,64,2304]{2,1,0:T(8,128)(2,1)} copy-done((bf16[4,64,2304]{2,1,0:T(8,128)(2,1)}, bf16[4,64,2304]{2,1,0:T(8,128)(2,1)S(1)}, u32[]{:S(2)}) %copy-start.1) | copy-done | bytes 1179672
  50.6 0.6 copy-done.10
  51.2 0.0 collective-permute-done.7.refs_2_
  51.2 0.0 collective-permute-done.9.refs_3_
  51.2 0.0 copy-start.2
  51.2 0.0 collective-permute-done.4.refs_0_
  51.3 0.0 copy-start.6
  51.3 0.8 copy-done.2
  52.1 0.8 fusion
  52.9 0.0 copy-done.6
  52.9 1.3 %collective-permute-start.13 = (bf16[128,1024]{1,0:T(8,128)(2,1)}, bf16[128,1024]{1,0:T(8,128)(2,1)S(1)}, u32[]{:S(2)}, u32[]{:S(2)}) collective-permute-start(bf16[128,1024]{1,0:T(8,128)(2,1)} %get-tuple-element.29), channel_id=1, source_target_pairs={{4,0},{8,12},{5,1},{9,13},{6,2},{10,14},{7,3},{11,15},{20,16},{24,... | collective-permute-start | bytes 786440 | tf_op jit(solution)/shard_map/ranks/line_3_0_1/ppermute | solution.py:359
  54.2 1.3 %collective-permute-start.11 = (bf16[128,1024]{1,0:T(8,128)(2,1)}, bf16[128,1024]{1,0:T(8,128)(2,1)}, u32[]{:S(2)}, u32[]{:S(2)}) collective-permute-start(bf16[128,1024]{1,0:T(8,128)(2,1)} %get-tuple-element.30), channel_id=1, source_target_pairs={{4,0},{8,12},{5,1},{9,13},{6,2},{10,14},{7,3},{11,15},{20,16},{24,... | collective-permute-start | bytes 786440 | tf_op jit(solution)/shard_map/ranks/line_3_0_0/ppermute | solution.py:359
  55.5 0.1 stack.64.scalars
  55.6 0.1 stack.59.scalars
  55.7 5.0 %all-to-all-start.1 = ((bf16[4,64,2304]{2,1,0:T(8,128)(2,1)}), bf16[4,64,2304]{2,1,0:T(8,128)(2,1)S(1)}, u32[]{:S(2)}, u32[]{:S(2)}) async-start(bf16[4,64,2304]{2,1,0:T(8,128)(2,1)} %copy-done.1), calls=%async_computation.1 | async-start | bytes 2359296 | tf_op jit(solution)/shard_map/ranks/all_to_all | solution.py:389
  60.7 2.7 %collective-permute-start.8 = (bf16[256,1024]{1,0:T(8,128)(2,1)}, bf16[256,1024]{1,0:T(8,128)(2,1)S(1)}, u32[]{:S(2)}, u32[]{:S(2)}) collective-permute-start(bf16[256,1024]{1,0:T(8,128)(2,1)} %copy-done.8), channel_id=1, source_target_pairs={{0,16},{12,28},{16,0},{28,12},{1,17},{13,29},{17,1},{29,13},{2,18}... | collective-permute-start | bytes 1572872 | tf_op jit(solution)/shard_map/swap_w_2/ppermute | solution.py:369
  63.4 0.7 collective-permute-start.10
  64.1 0.7 collective-permute-start.6
  64.8 0.0 collective-permute-done.13.refs_5_
  64.8 5.9 %collective-permute-start.14 = (bf16[128,1024]{1,0:T(8,128)(2,1)S(1)}, bf16[128,1024]{1,0:T(8,128)(2,1)S(1)}, u32[]{:S(2)}, u32[]{:S(2)}) collective-permute-start(bf16[128,1024]{1,0:T(8,128)(2,1)S(1)} %collective-permute-done.13.refs_5_), channel_id=1, source_target_pairs={{0,16},{12,28},{16,0},{28,12},{1,17},{13,29},{17,1},{29,13},{2,18}... | collective-permute-start | bytes 786440 | tf_op jit(solution)/shard_map/swap_w_5/ppermute | solution.py:369
  70.7 6.0 %collective-permute-done.11.refs_4_ = bf16[128,1024]{1,0:T(8,128)(2,1)} collective-permute-done((bf16[128,1024]{1,0:T(8,128)(2,1)}, bf16[128,1024]{1,0:T(8,128)(2,1)}, u32[]{:S(2)}, u32[]{:S(2)}) %collective-permute-start.11) | collective-permute-done | bytes 262176 | tf_op jit(solution)/shard_map/ranks/line_3_0_0/ppermute | solution.py:359
  76.7 2.4 %collective-permute-start.12 = (bf16[128,1024]{1,0:T(8,128)(2,1)}, bf16[128,1024]{1,0:T(8,128)(2,1)S(1)}, u32[]{:S(2)}, u32[]{:S(2)}) collective-permute-start(bf16[128,1024]{1,0:T(8,128)(2,1)} %collective-permute-done.11.refs_4_), channel_id=1, source_target_pairs={{0,16},{12,28},{16,0},{28,12},{1,17},{13,29},{17,1},{29,13},{2,18}... | collective-permute-start | bytes 786440 | tf_op jit(solution)/shard_map/swap_w_4/ppermute | solution.py:369
  79.1 1.0 %copy-done.3 = bf16[256,1024]{1,0:T(8,128)(2,1)S(1)} copy-done((bf16[256,1024]{1,0:T(8,128)(2,1)S(1)}, bf16[256,1024]{1,0:T(8,128)(2,1)}, u32[]{:S(2)}) %copy-start.3) | copy-done | bytes 524312
  80.1 1.2 %copy-done.5 = bf16[256,2048]{1,0:T(8,128)(2,1)S(1)} copy-done((bf16[256,2048]{1,0:T(8,128)(2,1)S(1)}, bf16[256,2048]{1,0:T(8,128)(2,1)}, u32[]{:S(2)}) %copy-start.5) | copy-done | bytes 1048600
  81.4 1.0 %copy-done.9 = bf16[256,1024]{1,0:T(8,128)(2,1)S(1)} copy-done((bf16[256,1024]{1,0:T(8,128)(2,1)S(1)}, bf16[256,1024]{1,0:T(8,128)(2,1)}, u32[]{:S(2)}) %copy-start.9) | copy-done | bytes 524312
  82.4 4.0 %product.2.refs_6_ = bf16[384,2048]{1,0:T(8,128)(2,1)} custom-call(s32[11]{0:T(128)S(1)} %stack.64.scalars, bf16[384,1024]{1,0:T(8,128)(2,1)S(1)} %broadcast_multiply_fusion.w_ref.weighted_ref, bf16[384,64]{1,0:T(8,128)(2,1)S(1)} %copy-done.11, bf16[4,64,1152]{2,1,0:T(8,128)(2,1)S(1)} %all-to-all-done.mine_ref.down_ref, bf16[256,2048]{1,0:T(8,128)(2,1)S(1)} %copy-done.5, ...), custom_call_target="tpu_custom_call" | custom-call | flops 9663676416 | bytes 2883584 | tf_op jit(solution)/shard_map/product/pallas_call | solution.py:144
  86.4 0.0 collective-permute-done.8.refs_2_
  86.4 0.0 collective-permute-done.10.refs_3_
  86.4 0.0 collective-permute-done.14.refs_5_
  86.4 0.2 collective-permute-done.12.refs_4_
  86.6 0.0 collective-permute-done.6.refs_1_
  86.6 3.2 %product.3 = bf16[384,2048]{1,0:T(8,128)(2,1)} custom-call(s32[11]{0:T(128)S(1)} %stack.59.scalars, bf16[384,1024]{1,0:T(8,128)(2,1)S(1)} %broadcast_multiply_fusion.w_ref.weighted_ref, bf16[384,64]{1,0:T(8,128)(2,1)S(1)} %copy-done.11, bf16[4,64,1152]{2,1,0:T(8,128)(2,1)S(1)} %collective-permute-done.other_ref.down_ref, ...), custom_call_target="tpu_custom_call", output_to_operand_aliasing={{}: (11, {})} | custom-call | flops 9663676416 | bytes 2883584 | tf_op jit(solution)/shard_map/product/pallas_call | solution.py:144
  89.9 0.0 all-to-all-done.1.got_ref
  89.9 0.9 %owner_sums.1 = (f32[1,64,2048]{2,1,0:T(8,128)}, f32[1,64,256]{2,1,0:T(8,128)}) custom-call(bf16[4,64,2304]{2,1,0:T(8,128)(2,1)S(1)} %all-to-all-done.1.got_ref), custom_call_target="tpu_custom_call" | custom-call | flops 589824 | bytes 1179648 | tf_op jit(solution)/shard_map/owner_sums/pallas_call | solution.py:255
  (16 shorter events, 0.1 us)
Async XLA Ops:
  0.6 8.2 %copy-start.4 = (bf16[256,2048]{1,0:T(8,128)(2,1)S(1)}, bf16[256,2048]{1,0:T(8,128)(2,1)}, u32[]{:S(2)}) copy-start(bf16[256,2048]{1,0:T(8,128)(2,1)} %own_ref.3) | copy-start | bytes 3145732
  0.6 26.7 %copy-start.13 = (s32[4]{0:T(128)S(1)}, s32[4]{0:T(128)}, u32[]{:S(2)}) copy-start(s32[4]{0:T(128)} %param.14) | copy-start | bytes 52
  0.7 26.7 %copy-start.14 = (s32[3,1]{0,1:T(1,128)S(1)}, s32[3,1]{0,1:T(1,128)}, u32[]{:S(2)}) copy-start(s32[3,1]{0,1:T(1,128)} %param.13) | copy-start | bytes 40
  0.7 26.8 %copy-start.12 = (s32[384]{0:T(512)S(1)}, s32[384]{0:T(512)}, u32[]{:S(2)}) copy-start(s32[384]{0:T(512)} %param.15) | copy-start | bytes 4612
  2.5 23.3 %all-to-all-start = ((bf16[4,64,1152]{2,1,0:T(8,128)(2,1)}), bf16[4,64,1152]{2,1,0:T(8,128)(2,1)S(1)}, u32[]{:S(2)}, u32[]{:S(2)}) async-start(bf16[4,64,1152]{2,1,0:T(8,128)(2,1)} %payload.1), calls=%async_computation | async-start | bytes 1179648 | tf_op jit(solution)/shard_map/adapters/all_to_all | solution.py:328
  8.8 31.8 %copy-start = (bf16[384,2048]{1,0:T(8,128)(2,1)S(1)}, bf16[384,2048]{1,0:T(8,128)(2,1)}, u32[]{:S(2)}) copy-start(bf16[384,2048]{1,0:T(8,128)(2,1)} %x_ref.3) | copy-start | bytes 4718596
  9.7 22.3 %collective-permute-start.3 = (bf16[256,1024]{1,0:T(8,128)(2,1)}, bf16[256,1024]{1,0:T(8,128)(2,1)}, u32[]{:S(2)}, u32[]{:S(2)}) collective-permute-start(bf16[256,1024]{1,0:T(8,128)(2,1)} %constant_dynamic-slice_fusion), channel_id=1, source_target_pairs={{0,4},{4,0},{8,12},{12,8},{1,5},{5,1},{9,13},{13,9},{2,6},{6,2},{1... | collective-permute-start | bytes 1572872 | tf_op jit(solution)/shard_map/line_1_0_0/ppermute | solution.py:359
  11.7 20.3 %collective-permute-start.5 = (bf16[256,1024]{1,0:T(8,128)(2,1)}, bf16[256,1024]{1,0:T(8,128)(2,1)}, u32[]{:S(2)}, u32[]{:S(2)}) collective-permute-start(bf16[256,1024]{1,0:T(8,128)(2,1)} %constant_dynamic-slice_fusion), channel_id=1, source_target_pairs={{4,8},{8,4},{5,9},{9,5},{6,10},{10,6},{7,11},{11,7},{20,24},{24,20... | collective-permute-start | bytes 1572872 | tf_op jit(solution)/shard_map/line_1_1_0/ppermute | solution.py:359
  25.8 13.3 %collective-permute-start = (bf16[4,64,1152]{2,1,0:T(8,128)(2,1)S(1)}, bf16[4,64,1152]{2,1,0:T(8,128)(2,1)S(1)}, u32[]{:S(2)}, u32[]{:S(2)}) collective-permute-start(bf16[4,64,1152]{2,1,0:T(8,128)(2,1)S(1)} %all-to-all-done.mine_ref.down_ref), channel_id=1, source_target_pairs={{0,16},{16,0},{1,17},{17,1},{2,18},{18,2},{3,19},{19,3},{4,20},{20... | collective-permute-start | bytes 1769480 | tf_op jit(solution)/shard_map/swap_a/ppermute | solution.py:336
  32.0 19.2 %collective-permute-start.7 = (bf16[256,1024]{1,0:T(8,128)(2,1)}, bf16[256,1024]{1,0:T(8,128)(2,1)S(1)}, u32[]{:S(2)}, u32[]{:S(2)}) collective-permute-start(bf16[256,1024]{1,0:T(8,128)(2,1)} %collective-permute-done.5.refs_1_), channel_id=1, source_target_pairs={{4,0},{8,12},{5,1},{9,13},{6,2},{10,14},{7,3},{11,15},{20,16},{24,... | collective-permute-start | bytes 1572872 | tf_op jit(solution)/shard_map/line_2_0_0/ppermute | solution.py:359
  33.3 17.9 %collective-permute-start.9 = (bf16[256,1024]{1,0:T(8,128)(2,1)}, bf16[256,1024]{1,0:T(8,128)(2,1)S(1)}, u32[]{:S(2)}, u32[]{:S(2)}) collective-permute-start(bf16[256,1024]{1,0:T(8,128)(2,1)} %collective-permute-done.3.refs_0_), channel_id=1, source_target_pairs={{4,8},{8,4},{5,9},{9,5},{6,10},{10,6},{7,11},{11,7},{20,24},{24,20... | collective-permute-start | bytes 1572872 | tf_op jit(solution)/shard_map/line_2_1_0/ppermute | solution.py:359
  39.1 12.2 %collective-permute-start.4 = (bf16[256,1024]{1,0:T(8,128)(2,1)}, bf16[256,1024]{1,0:T(8,128)(2,1)S(1)}, u32[]{:S(2)}, u32[]{:S(2)}) collective-permute-start(bf16[256,1024]{1,0:T(8,128)(2,1)} %collective-permute-done.3.refs_0_), channel_id=1, source_target_pairs={{4,20},{0,16},{12,28},{8,24},{20,4},{16,0},{28,12},{24,8},{5,21},{... | collective-permute-start | bytes 1572872 | tf_op jit(solution)/shard_map/ranks/swap_w_0/ppermute | solution.py:369
  41.9 1.4 %collective-permute-start.1 = (bf16[384,128]{1,0:T(8,128)(2,1)S(1)}, bf16[384,128]{1,0:T(8,128)(2,1)S(1)}, u32[]{:S(2)}, u32[]{:S(2)}) collective-permute-start(bf16[384,128]{1,0:T(8,128)(2,1)S(1)} %project.1), channel_id=1, source_target_pairs={{0,1},{1,0},{2,3},{3,2},{4,5},{5,4},{6,7},{7,6},{8,9},{9,8},{10,11... | collective-permute-start | bytes 294920 | tf_op jit(solution)/shard_map/ranks/psum_pipe/ppermute | solution.py:298
  43.3 4.9 %collective-permute-start.2 = (bf16[384,128]{1,0:T(8,128)(2,1)S(1)}, bf16[384,128]{1,0:T(8,128)(2,1)S(1)}, u32[]{:S(2)}, u32[]{:S(2)}) collective-permute-start(bf16[384,128]{1,0:T(8,128)(2,1)S(1)} %add_convert_fusion.here_ref), channel_id=1, source_target_pairs={{0,2},{2,0},{1,3},{3,1},{4,6},{6,4},{5,7},{7,5},{8,10},{10,8},{9,1... | collective-permute-start | bytes 294920 | tf_op jit(solution)/shard_map/ranks/psum_tensor/ppermute | solution.py:298
  49.6 1.0 %copy-start.1 = (bf16[4,64,2304]{2,1,0:T(8,128)(2,1)}, bf16[4,64,2304]{2,1,0:T(8,128)(2,1)S(1)}, u32[]{:S(2)}) copy-start(bf16[4,64,2304]{2,1,0:T(8,128)(2,1)S(1)} %get-tuple-element.22) | copy-start | bytes 3538948
  50.6 0.6 copy-start.10
  51.2 1.7 %copy-start.8 = (bf16[256,1024]{1,0:T(8,128)(2,1)}, bf16[256,1024]{1,0:T(8,128)(2,1)S(1)}, u32[]{:S(2)}) copy-start(bf16[256,1024]{1,0:T(8,128)(2,1)S(1)} %collective-permute-done.7.refs_2_) | copy-start | bytes 1572868
  51.2 0.8 copy-start.2
  51.3 1.6 %copy-start.6 = (bf16[256,1024]{1,0:T(8,128)(2,1)}, bf16[256,1024]{1,0:T(8,128)(2,1)S(1)}, u32[]{:S(2)}) copy-start(bf16[256,1024]{1,0:T(8,128)(2,1)S(1)} %collective-permute-done.4.refs_0_) | copy-start | bytes 1572868
  52.1 27.0 %copy-start.11 = (bf16[384,64]{1,0:T(8,128)(2,1)S(1)}, bf16[384,64]{1,0:T(8,128)(2,1)}, u32[]{:S(2)}) copy-start(bf16[384,64]{1,0:T(8,128)(2,1)} %copy-done.10) | copy-start | bytes 147460
  52.9 11.9 %collective-permute-start.13 = (bf16[128,1024]{1,0:T(8,128)(2,1)}, bf16[128,1024]{1,0:T(8,128)(2,1)S(1)}, u32[]{:S(2)}, u32[]{:S(2)}) collective-permute-start(bf16[128,1024]{1,0:T(8,128)(2,1)} %get-tuple-element.29), channel_id=1, source_target_pairs={{4,0},{8,12},{5,1},{9,13},{6,2},{10,14},{7,3},{11,15},{20,16},{24,... | collective-permute-start | bytes 786440 | tf_op jit(solution)/shard_map/ranks/line_3_0_1/ppermute | solution.py:359
  54.2 22.5 %collective-permute-start.11 = (bf16[128,1024]{1,0:T(8,128)(2,1)}, bf16[128,1024]{1,0:T(8,128)(2,1)}, u32[]{:S(2)}, u32[]{:S(2)}) collective-permute-start(bf16[128,1024]{1,0:T(8,128)(2,1)} %get-tuple-element.30), channel_id=1, source_target_pairs={{4,0},{8,12},{5,1},{9,13},{6,2},{10,14},{7,3},{11,15},{20,16},{24,... | collective-permute-start | bytes 786440 | tf_op jit(solution)/shard_map/ranks/line_3_0_0/ppermute | solution.py:359
  55.7 34.2 %all-to-all-start.1 = ((bf16[4,64,2304]{2,1,0:T(8,128)(2,1)}), bf16[4,64,2304]{2,1,0:T(8,128)(2,1)S(1)}, u32[]{:S(2)}, u32[]{:S(2)}) async-start(bf16[4,64,2304]{2,1,0:T(8,128)(2,1)} %copy-done.1), calls=%async_computation.1 | async-start | bytes 2359296 | tf_op jit(solution)/shard_map/ranks/all_to_all | solution.py:389
  60.7 25.7 %collective-permute-start.8 = (bf16[256,1024]{1,0:T(8,128)(2,1)}, bf16[256,1024]{1,0:T(8,128)(2,1)S(1)}, u32[]{:S(2)}, u32[]{:S(2)}) collective-permute-start(bf16[256,1024]{1,0:T(8,128)(2,1)} %copy-done.8), channel_id=1, source_target_pairs={{0,16},{12,28},{16,0},{28,12},{1,17},{13,29},{17,1},{29,13},{2,18}... | collective-permute-start | bytes 1572872 | tf_op jit(solution)/shard_map/swap_w_2/ppermute | solution.py:369
  63.4 23.0 %collective-permute-start.10 = (bf16[256,1024]{1,0:T(8,128)(2,1)}, bf16[256,1024]{1,0:T(8,128)(2,1)S(1)}, u32[]{:S(2)}, u32[]{:S(2)}) collective-permute-start(bf16[256,1024]{1,0:T(8,128)(2,1)} %copy-done.2), channel_id=1, source_target_pairs={{8,24},{4,20},{24,8},{20,4},{9,25},{5,21},{25,9},{21,5},{10,26},{6... | collective-permute-start | bytes 1572872 | tf_op jit(solution)/shard_map/swap_w_3/ppermute | solution.py:369
  64.1 22.5 %collective-permute-start.6 = (bf16[256,1024]{1,0:T(8,128)(2,1)}, bf16[256,1024]{1,0:T(8,128)(2,1)S(1)}, u32[]{:S(2)}, u32[]{:S(2)}) collective-permute-start(bf16[256,1024]{1,0:T(8,128)(2,1)} %collective-permute-done.5.refs_1_), channel_id=1, source_target_pairs={{8,24},{4,20},{24,8},{20,4},{9,25},{5,21},{25,9},{21,5},{10,26},{6... | collective-permute-start | bytes 1572872 | tf_op jit(solution)/shard_map/swap_w_1/ppermute | solution.py:369
  64.8 21.6 %collective-permute-start.14 = (bf16[128,1024]{1,0:T(8,128)(2,1)S(1)}, bf16[128,1024]{1,0:T(8,128)(2,1)S(1)}, u32[]{:S(2)}, u32[]{:S(2)}) collective-permute-start(bf16[128,1024]{1,0:T(8,128)(2,1)S(1)} %collective-permute-done.13.refs_5_), channel_id=1, source_target_pairs={{0,16},{12,28},{16,0},{28,12},{1,17},{13,29},{17,1},{29,13},{2,18}... | collective-permute-start | bytes 786440 | tf_op jit(solution)/shard_map/swap_w_5/ppermute | solution.py:369
  76.7 10.0 %collective-permute-start.12 = (bf16[128,1024]{1,0:T(8,128)(2,1)}, bf16[128,1024]{1,0:T(8,128)(2,1)S(1)}, u32[]{:S(2)}, u32[]{:S(2)}) collective-permute-start(bf16[128,1024]{1,0:T(8,128)(2,1)} %collective-permute-done.11.refs_4_), channel_id=1, source_target_pairs={{0,16},{12,28},{16,0},{28,12},{1,17},{13,29},{17,1},{29,13},{2,18}... | collective-permute-start | bytes 786440 | tf_op jit(solution)/shard_map/swap_w_4/ppermute | solution.py:369
  79.1 1.0 %copy-start.3 = (bf16[256,1024]{1,0:T(8,128)(2,1)S(1)}, bf16[256,1024]{1,0:T(8,128)(2,1)}, u32[]{:S(2)}) copy-start(bf16[256,1024]{1,0:T(8,128)(2,1)} %copy-done.2) | copy-start | bytes 1572868
  80.1 1.2 %copy-start.5 = (bf16[256,2048]{1,0:T(8,128)(2,1)S(1)}, bf16[256,2048]{1,0:T(8,128)(2,1)}, u32[]{:S(2)}) copy-start(bf16[256,2048]{1,0:T(8,128)(2,1)} %own_ref.3) | copy-start | bytes 3145732
  81.3 1.0 %copy-start.9 = (bf16[256,1024]{1,0:T(8,128)(2,1)S(1)}, bf16[256,1024]{1,0:T(8,128)(2,1)}, u32[]{:S(2)}) copy-start(bf16[256,1024]{1,0:T(8,128)(2,1)} %copy-done.8) | copy-start | bytes 1572868
  82.4 4.2 %copy-start.7 = (bf16[256,1024]{1,0:T(8,128)(2,1)S(1)}, bf16[256,1024]{1,0:T(8,128)(2,1)}, u32[]{:S(2)}) copy-start(bf16[256,1024]{1,0:T(8,128)(2,1)} %copy-done.6) | copy-start | bytes 1572868
